TPU v7x, 256 devices: a whole 4x4x8 slice. The times are simulated.
256 devices in a mesh: section: 8 (over y, core), tensor: 32 (over z, x).
Axes of the slice: x: 4, y: 4, z: 8, core: 2. Of those that a mesh axis runs over, the one named last changes fastest.
Arguments:
- saved_inputs: bfloat16 [8, 4, 256, 1024], P('section', None, 'tensor'), may hold values from -6 to 6
- slot_index: int32 [8, 3], P('section'), may hold values from 0 to 3
- example_lengths: int32 [8, 3, 2], P('section'), may hold values from 1 to 192, 256 in all within a row
- first_grads: bfloat16 [8, 256, 1024], P('section', 'tensor'), may hold values from -6 to 6
- loss_grads: bfloat16 [2, 256, 1024], P(None, 'tensor'), may hold values from -6 to 6
- w_in: bfloat16 [8, 1024, 32768], P('section', None, 'tensor'), may hold values from -0.1875 to 0.1875
- w_out: bfloat16 [8, 32768, 1024], P('section', 'tensor'), may hold values from -0.03125 to 0.03125
Outputs:
- grad_in: bfloat16 [8, 1024, 32768], P('section', None, 'tensor')
- grad_out: bfloat16 [8, 32768, 1024], P('section', 'tensor')
- input_grads: bfloat16 [8, 3, 256, 1024], P('section', None, 'tensor')
Inputs may be any that keep to these rules, and one draw needn't show every extreme that they name: `example_lengths`: the 2 lengths of one microbatch sum to 256.
All inputs are finite; a program needn't handle non-finite values.
Results may differ from a plain program's by a relative error of at most 0.0095.
Values may be sent and summed in bfloat16 or wider, within the bound.
No kernel may reach another device: no remote copies, remote signals or barrier semaphores. Data moves between devices by JAX's collectives and lax.ppermute only.
A program may use at most 128 MiB of HBM per device.

v0:
```python
import jax
import jax.numpy as jnp
from jax import lax
from jax.sharding import PartitionSpec as P

D = 1024
FF = 32768


GAMMA = 0.01


def joined_along(blocks, dim):
    blocks = jnp.moveaxis(blocks, 0, dim)
    shape = blocks.shape
    return blocks.reshape(*shape[:dim], shape[dim] * shape[dim + 1], *shape[dim + 2 :])


def from_everyone(shard, axis):
    copies = jnp.broadcast_to(shard, (lax.axis_size(axis), *shard.shape))
    return lax.all_to_all(copies, axis, split_axis=0, concat_axis=0, tiled=True)


def gathered_copies(shard, axis, dim):
    return joined_along(from_everyone(shard, axis), dim)


def split_up(shard, dim, count):
    before, after = (shard.shape[:dim], shard.shape[dim + 1 :])
    return jnp.moveaxis(shard.reshape(*before, count, -1, *after), dim, 0)


def summed_on_arrival(shard, axis, dim):
    blocks = split_up(shard, dim, lax.axis_size(axis))
    arrived = lax.all_to_all(blocks, axis, split_axis=0, concat_axis=0, tiled=True)
    return arrived.sum(axis=0)


def over_copies(shard, axis):
    everything = from_everyone(shard, axis)
    return jnp.sum(everything, axis=0)


def shifted(value, axis, steps):
    count = lax.axis_size(axis)
    first, last = (max(0, -steps), min(count, count - steps))
    return lax.ppermute(value, axis, [(source, source + steps) for source in range(first, last)])


def membership(lengths, tokens):
    ends = jnp.cumsum(lengths)
    position = jnp.arange(tokens, dtype=jnp.int32)
    example_id = jnp.sum((position[:, None] >= ends[None, :-1]).astype(jnp.int32), axis=1)
    labels = jnp.arange(lengths.shape[0], dtype=jnp.int32)
    return (example_id[:, None] == labels[None, :]).astype(jnp.float32)


def per_device(saved_inputs, slot_index, example_lengths, first_grads, loss_grads, w_in, w_out):
    section_count = lax.axis_size("section")
    is_last = lax.axis_index("section") == section_count - 1
    first = w_in[0]
    second = w_out[0]
    slot_count = loss_grads.shape[0] + 1
    picked = [
        lax.dynamic_index_in_dim(saved_inputs[0], slot_index[0, slot], 0, keepdims=False)
        for slot in range(slot_count)
    ]
    every_input = gathered_copies(jnp.stack(picked), "tensor", 1)
    acc_first = jnp.zeros(first.shape, jnp.float32)
    acc_second = jnp.zeros(second.shape, jnp.float32)
    incoming = first_grads[0]
    results = []
    for slot in range(slot_count):
        inputs = every_input[slot]
        grads = gathered_copies(incoming, "tensor", 0)
        z = jnp.dot(inputs, first, preferred_element_type=jnp.float32)
        relu = jnp.maximum(z, 0.0)
        hidden = (relu * relu).astype(jnp.bfloat16)
        back = jnp.einsum("td,fd->tf", grads, second, preferred_element_type=jnp.float32)
        dz = (2.0 * relu * back).astype(jnp.bfloat16)
        shares = summed_on_arrival(
            jnp.einsum("tf,df->td", dz, first, preferred_element_type=jnp.float32), "tensor", 0
        )
        member = membership(example_lengths[0, slot], inputs.shape[0])
        gram_x = jnp.einsum("td,ud->tu", inputs, inputs, preferred_element_type=jnp.float32)
        gram_z = jnp.einsum("tf,uf->tu", dz, dz, preferred_element_type=jnp.float32)
        gram_h = jnp.einsum("tf,uf->tu", hidden, hidden, preferred_element_type=jnp.float32)
        gram_y = jnp.einsum("td,ud->tu", grads, grads, preferred_element_type=jnp.float32)
        paired = gram_x * gram_z + gram_h * gram_y
        local_squares = jnp.sum(
            member * jnp.dot(paired, member, precision=lax.Precision.HIGHEST), axis=0
        )
        squares = over_copies(local_squares, "tensor")
        factor = 1.0 / (jnp.sqrt(squares / (D * FF)) + GAMMA)
        token_factor = jnp.sum(member * factor[None, :], axis=1)
        dzc = (dz.astype(jnp.float32) * token_factor[:, None]).astype(jnp.bfloat16)
        dyc = (grads.astype(jnp.float32) * token_factor[:, None]).astype(jnp.bfloat16)
        acc_first = acc_first + jnp.einsum(
            "td,tf->df", inputs, dzc, preferred_element_type=jnp.float32
        )
        acc_second = acc_second + jnp.einsum(
            "tf,td->fd", hidden, dyc, preferred_element_type=jnp.float32
        )
        passing = (incoming.astype(jnp.float32) + shares).astype(jnp.bfloat16)
        results.append(passing)
        if slot + 1 < slot_count:
            arrived = shifted(passing, "section", -1)
            incoming = jnp.where(is_last, loss_grads[slot], arrived)
    grad_in = acc_first.astype(jnp.bfloat16)[None]
    grad_out = acc_second.astype(jnp.bfloat16)[None]
    input_grads = jnp.stack(results)[None]
    return (grad_in, grad_out, input_grads)


def solution(mesh):
    return jax.shard_map(
        per_device,
        mesh=mesh,
        in_specs=(
            P("section", None, "tensor", None),
            P("section", None),
            P("section", None, None),
            P("section", "tensor", None),
            P(None, "tensor", None),
            P("section", None, "tensor"),
            P("section", "tensor", None),
        ),
        out_specs=(
            P("section", None, "tensor"),
            P("section", "tensor", None),
            P("section", None, "tensor", None),
        ),
        check_vma=False,
    )
```

profile of v0, /device:TPU:8, one launch (start us, length us, event | category | flops | bytes accessed | tf_op | source)
XLA Modules:
  0.0 294.6 jit_solution(17744155631959182082)
XLA Ops:
  0.6 1.4 fusion.86
  8.9 51.5 %all_to_all.53 = bf16[32,3,8,1024]{3,2,1,0:T(8,128)(2,1)} all-to-all(bf16[32,3,8,1024]{3,2,1,0:T(8,128)(2,1)S(1)} %broadcast_in_dim.20), channel_id=1, replica_groups=mesh['section'=8,'tensor'=32] {'tensor'}, dimensions={0} | all-to-all | bytes 3145728 | tf_op jit(solution)/shard_map/all_to_all | solution.py:21
  61.3 4.7 %all-to-all-start.1 = ((bf16[32,8,1024]{2,1,0:T(8,128)(2,1)}), bf16[32,8,1024]{2,1,0:T(8,128)(2,1)}, u32[]{:S(2)}, u32[]{:S(2)}) async-start(bf16[32,8,1024]{2,1,0:T(8,128)(2,1)} %broadcast_in_dim.21), calls=%async_computation.1 | async-start | bytes 1048576 | tf_op jit(solution)/shard_map/all_to_all | solution.py:21
  66.0 1.8 fusion.20
  67.7 15.1 %all-to-all-done.1 = bf16[32,8,1024]{2,1,0:T(8,128)(2,1)} async-done(((bf16[32,8,1024]{2,1,0:T(8,128)(2,1)}), bf16[32,8,1024]{2,1,0:T(8,128)(2,1)}, u32[]{:S(2)}, u32[]{:S(2)}) %all-to-all-start.1) | async-done | bytes 524320 | tf_op jit(solution)/shard_map/all_to_all | solution.py:21
  82.8 2.5 fusion.44
  86.1 1.7 fusion.4
  87.9 4.8 %all-to-all-start.3 = ((f32[32,8,1024]{2,1,0:T(8,128)}), f32[32,8,1024]{2,1,0:T(8,128)}, u32[]{:S(2)}, u32[]{:S(2)}) async-start(f32[32,8,1024]{2,1,0:T(8,128)} %fusion.4), calls=%async_computation.3 | async-start | bytes 2097152 | tf_op jit(solution)/shard_map/all_to_all | solution.py:35
  94.7 24.9 %all-to-all-done.3 = f32[32,8,1024]{2,1,0:T(8,128)} async-done(((f32[32,8,1024]{2,1,0:T(8,128)}), f32[32,8,1024]{2,1,0:T(8,128)}, u32[]{:S(2)}, u32[]{:S(2)}) %all-to-all-start.3) | async-done | bytes 1048608 | tf_op jit(solution)/shard_map/all_to_all | solution.py:35
  119.7 1.3 reduce_sum.125
  121.0 1.9 collective-permute-start
  125.2 5.7 %all-to-all-start.4 = ((bf16[32,8,1024]{2,1,0:T(8,128)(2,1)}), bf16[32,8,1024]{2,1,0:T(8,128)(2,1)}, u32[]{:S(2)}, u32[]{:S(2)}) async-start(bf16[32,8,1024]{2,1,0:T(8,128)(2,1)} %broadcast_in_dim.23), calls=%async_computation.4 | async-start | bytes 1048576 | tf_op jit(solution)/shard_map/all_to_all | solution.py:21
  130.9 1.7 fusion.75
  132.6 1.5 convolution_multiply_fusion.4
  134.9 1.8 fusion.23
  136.7 12.4 %all-to-all-done.4 = bf16[32,8,1024]{2,1,0:T(8,128)(2,1)} async-done(((bf16[32,8,1024]{2,1,0:T(8,128)(2,1)}), bf16[32,8,1024]{2,1,0:T(8,128)(2,1)}, u32[]{:S(2)}, u32[]{:S(2)}) %all-to-all-start.4) | async-done | bytes 524320 | tf_op jit(solution)/shard_map/all_to_all | solution.py:21
  149.7 5.1 %all-to-all-start.2 = ((f32[32,1,2]{2,1,0:T(1,128)}), f32[32,1,2]{2,1,0:T(1,128)S(1)}, u32[]{:S(2)}, u32[]{:S(2)}) async-start(f32[32,1,2]{2,1,0:T(1,128)} %broadcast_in_dim.22), calls=%async_computation.2 | async-start | bytes 32768 | tf_op jit(solution)/shard_map/all_to_all | solution.py:21
  154.8 2.5 fusion.41
  158.1 1.7 fusion.2
  159.8 4.6 %all-to-all-done.2 = f32[32,1,2]{2,1,0:T(1,128)S(1)} async-done(((f32[32,1,2]{2,1,0:T(1,128)}), f32[32,1,2]{2,1,0:T(1,128)S(1)}, u32[]{:S(2)}, u32[]{:S(2)}) %all-to-all-start.2) | async-done | bytes 288 | tf_op jit(solution)/shard_map/all_to_all | solution.py:21
  164.5 5.3 %all-to-all-start.6 = ((f32[32,8,1024]{2,1,0:T(8,128)}), f32[32,8,1024]{2,1,0:T(8,128)}, u32[]{:S(2)}, u32[]{:S(2)}) async-start(f32[32,8,1024]{2,1,0:T(8,128)} %fusion.2), calls=%async_computation.6 | async-start | bytes 2097152 | tf_op jit(solution)/shard_map/all_to_all | solution.py:35
  169.8 2.4 fusion.77
  172.1 2.3 fusion.76
  175.4 1.7 fusion.26
  178.3 1.7 convolution_multiply_fusion.3
  179.9 2.4 fusion.48
  182.3 15.5 %all-to-all-done.6 = f32[32,8,1024]{2,1,0:T(8,128)} async-done(((f32[32,8,1024]{2,1,0:T(8,128)}), f32[32,8,1024]{2,1,0:T(8,128)}, u32[]{:S(2)}, u32[]{:S(2)}) %all-to-all-start.6) | async-done | bytes 1048608 | tf_op jit(solution)/shard_map/all_to_all | solution.py:35
  197.8 1.3 reduce_sum.129
  199.2 1.9 collective-permute-start.1
  201.1 1.3 fusion.51
  203.0 5.5 %all-to-all-start.5 = ((f32[32,1,2]{2,1,0:T(1,128)}), f32[32,1,2]{2,1,0:T(1,128)S(1)}, u32[]{:S(2)}, u32[]{:S(2)}) async-start(f32[32,1,2]{2,1,0:T(1,128)} %broadcast_in_dim.24), calls=%async_computation.5 | async-start | bytes 32768 | tf_op jit(solution)/shard_map/all_to_all | solution.py:21
  208.5 9.6 %all-to-all-done.5 = f32[32,1,2]{2,1,0:T(1,128)S(1)} async-done(((f32[32,1,2]{2,1,0:T(1,128)}), f32[32,1,2]{2,1,0:T(1,128)S(1)}, u32[]{:S(2)}, u32[]{:S(2)}) %all-to-all-start.5) | async-done | bytes 288 | tf_op jit(solution)/shard_map/all_to_all | solution.py:21
  219.0 4.8 %all-to-all-start.7 = ((bf16[32,8,1024]{2,1,0:T(8,128)(2,1)}), bf16[32,8,1024]{2,1,0:T(8,128)(2,1)}, u32[]{:S(2)}, u32[]{:S(2)}) async-start(bf16[32,8,1024]{2,1,0:T(8,128)(2,1)} %broadcast_in_dim.25), calls=%async_computation.7 | async-start | bytes 1048576 | tf_op jit(solution)/shard_map/all_to_all | solution.py:21
  223.9 4.0 %fusion.53 = f32[1024,1024]{1,0:T(8,128)} fusion(bf16[256,1024]{1,0:T(8,128)(2,1)} %copy-done.8, f32[256]{0:T(256)} %select_reduce_fusion.2, bf16[3,32,8,1024]{3,2,0,1:T(8,128)(2,1)} %bitcast.143), kind=kOutput, calls=%fused_computation.55 | convolution fusion | flops 537657344 | bytes 5243904 | tf_op jit(solution)/shard_map/td,tf->df/dot_general | solution.py:98
  227.9 3.8 %fusion.55 = f32[1024,1024]{1,0:T(8,128)} fusion(bf16[32,8,1024]{2,1,0:T(8,128)(2,1)} %all-to-all-done.1, f32[256]{0:T(256)S(1)} %copy-done.15, f32[256,1024]{1,0:T(8,128)S(1)} %copy-done.4), kind=kOutput, calls=%fused_computation.57 | convolution fusion | flops 538181632 | bytes 5768192 | tf_op jit(solution)/shard_map/tf,td->fd/dot_general | solution.py:101
  231.9 9.0 %all-to-all-done.7 = bf16[32,8,1024]{2,1,0:T(8,128)(2,1)} async-done(((bf16[32,8,1024]{2,1,0:T(8,128)(2,1)}), bf16[32,8,1024]{2,1,0:T(8,128)(2,1)}, u32[]{:S(2)}, u32[]{:S(2)}) %all-to-all-start.7) | async-done | bytes 524320 | tf_op jit(solution)/shard_map/all_to_all | solution.py:21
  240.9 2.5 fusion.38
  244.6 1.5 fusion.49
  247.1 4.7 %all-to-all-start.8 = ((f32[32,1,2]{2,1,0:T(1,128)}), f32[32,1,2]{2,1,0:T(1,128)S(1)}, u32[]{:S(2)}, u32[]{:S(2)}) async-start(f32[32,1,2]{2,1,0:T(1,128)} %broadcast_in_dim.26), calls=%async_computation.8 | async-start | bytes 32768 | tf_op jit(solution)/shard_map/all_to_all | solution.py:21
  251.8 2.8 fusion
  254.6 6.9 %all-to-all-done.8 = f32[32,1,2]{2,1,0:T(1,128)S(1)} async-done(((f32[32,1,2]{2,1,0:T(1,128)}), f32[32,1,2]{2,1,0:T(1,128)S(1)}, u32[]{:S(2)}, u32[]{:S(2)}) %all-to-all-start.8) | async-done | bytes 288 | tf_op jit(solution)/shard_map/all_to_all | solution.py:21
  261.4 4.7 %all-to-all-start.9 = ((f32[32,8,1024]{2,1,0:T(8,128)}), f32[32,8,1024]{2,1,0:T(8,128)}, u32[]{:S(2)}, u32[]{:S(2)}) async-start(f32[32,8,1024]{2,1,0:T(8,128)} %fusion), calls=%async_computation.9 | async-start | bytes 2097152 | tf_op jit(solution)/shard_map/all_to_all | solution.py:35
  266.1 4.1 %fusion.54 = f32[1024,1024]{1,0:T(8,128)} fusion(bf16[256,1024]{1,0:T(8,128)(2,1)} %copy-done.10, f32[256]{0:T(256)S(1)} %select_reduce_fusion.1, bf16[3,32,8,1024]{3,2,0,1:T(8,128)(2,1)} %bitcast.144), kind=kOutput, calls=%fused_computation.56 | convolution fusion | flops 537657344 | bytes 5243904 | tf_op jit(solution)/shard_map/td,tf->df/dot_general | solution.py:98
  270.2 3.8 %fusion.56 = f32[1024,1024]{1,0:T(8,128)} fusion(bf16[32,8,1024]{2,1,0:T(8,128)(2,1)} %all-to-all-done.4, f32[256]{0:T(256)S(1)} %select_reduce_fusion.1, f32[256,1024]{1,0:T(8,128)S(1)} %copy-done.6), kind=kOutput, calls=%fused_computation.58 | convolution fusion | flops 538181632 | bytes 5768192 | tf_op jit(solution)/shard_map/tf,td->fd/dot_general | solution.py:101
  274.2 6.0 %fusion.18 = bf16[1,1024,1024]{2,1,0:T(8,128)(2,1)} fusion(f32[1024,1024]{1,0:T(8,128)} %fusion.53, f32[1024,1024]{1,0:T(8,128)} %fusion.54, bf16[256,1024]{1,0:T(8,128)(2,1)} %copy-done.7, f32[256]{0:T(256)S(1)} %select_reduce_fusion, bf16[3,32,8,1024]{3,2,0,1:T(8,128)(2,1)} %bitcast.145), kind=kOutput, calls=%fused_computation.20 | convolution fusion | flops 540803072 | bytes 11535360 | tf_op jit(solution)/shard_map/td,tf->df/dot_general | solution.py:98
  281.1 3.2 %fusion.19 = bf16[1,1024,1024]{2,1,0:T(8,128)(2,1)} fusion(f32[1024,1024]{1,0:T(8,128)S(1)} %copy-done.1, f32[1024,1024]{1,0:T(8,128)S(1)} %copy-done.2, bf16[32,8,1024]{2,1,0:T(8,128)(2,1)} %all-to-all-done.7, f32[256]{0:T(256)S(1)} %select_reduce_fusion, f32[256,1024]{1,0:T(8,128)S(1)} %fusion.26), kind=kOutput, calls=%fused_computation.21 | convolution fusion | flops 541327360 | bytes 12059648 | tf_op jit(solution)/shard_map/tf,td->fd/dot_general | solution.py:101
  284.3 8.3 %all-to-all-done.9 = f32[32,8,1024]{2,1,0:T(8,128)} async-done(((f32[32,8,1024]{2,1,0:T(8,128)}), f32[32,8,1024]{2,1,0:T(8,128)}, u32[]{:S(2)}, u32[]{:S(2)}) %all-to-all-start.9) | async-done | bytes 1048608 | tf_op jit(solution)/shard_map/all_to_all | solution.py:35
  292.7 1.3 reduce_sum.134
  (77 shorter events, 16.7 us)
Async XLA Ops:
  0.6 65.3 %copy-start = (bf16[1,1024,1024]{2,1,0:T(8,128)(2,1)S(1)}, bf16[1,1024,1024]{2,1,0:T(8,128)(2,1)}, u32[]{:S(2)}) copy-start(bf16[1,1024,1024]{2,1,0:T(8,128)(2,1)} %param.12) | copy-start | bytes 6291460
  8.7 51.8 %copy-start.12 = (bf16[1,8,1024]{2,1,0:T(8,128)(2,1)S(1)}, bf16[1,8,1024]{2,1,0:T(8,128)(2,1)}, u32[]{:S(2)}) copy-start(bf16[1,8,1024]{2,1,0:T(8,128)(2,1)} %param.10) | copy-start | bytes 49156
  61.3 21.6 %all-to-all-start.1 = ((bf16[32,8,1024]{2,1,0:T(8,128)(2,1)}), bf16[32,8,1024]{2,1,0:T(8,128)(2,1)}, u32[]{:S(2)}, u32[]{:S(2)}) async-start(bf16[32,8,1024]{2,1,0:T(8,128)(2,1)} %broadcast_in_dim.21), calls=%async_computation.1 | async-start | bytes 1048576 | tf_op jit(solution)/shard_map/all_to_all | solution.py:21
  67.7 55.2 %copy-start.3 = (f32[256,1024]{1,0:T(8,128)}, f32[256,1024]{1,0:T(8,128)S(1)}, u32[]{:S(2)}) copy-start(f32[256,1024]{1,0:T(8,128)S(1)} %fusion.20) | copy-start | bytes 3145732
  85.3 0.8 copy-start.8
  86.1 6.5 %copy-start.14 = (s32[1,3,2]{1,2,0:T(2,128)S(1)}, s32[1,3,2]{1,2,0:T(2,128)}, u32[]{:S(2)}) copy-start(s32[1,3,2]{1,2,0:T(2,128)} %param.9) | copy-start | bytes 76
  87.9 36.5 %copy-start.13 = (bf16[2,8,1024]{2,1,0:T(8,128)(2,1)S(1)}, bf16[2,8,1024]{2,1,0:T(8,128)(2,1)}, u32[]{:S(2)}) copy-start(bf16[2,8,1024]{2,1,0:T(8,128)(2,1)} %param.11) | copy-start | bytes 98308
  87.9 31.8 %all-to-all-start.3 = ((f32[32,8,1024]{2,1,0:T(8,128)}), f32[32,8,1024]{2,1,0:T(8,128)}, u32[]{:S(2)}, u32[]{:S(2)}) async-start(f32[32,8,1024]{2,1,0:T(8,128)} %fusion.4), calls=%async_computation.3 | async-start | bytes 2097152 | tf_op jit(solution)/shard_map/all_to_all | solution.py:35
  121.0 3.4 %collective-permute-start = (bf16[8,1024]{1,0:T(8,128)(2,1)S(1)}, bf16[8,1024]{1,0:T(8,128)(2,1)S(1)}, u32[]{:S(2)}, u32[]{:S(2)}) collective-permute-start(bf16[8,1024]{1,0:T(8,128)(2,1)S(1)} %add_convert_fusion.4), channel_id=1, source_target_pairs={{32,0},{64,32},{96,64},{128,96},{160,128},{192,160},{224,192},{33,... | collective-permute-start | bytes 49160 | tf_op jit(solution)/shard_map/ppermute | solution.py:47
  123.3 10.9 %copy-start.9 = (bf16[256,1024]{1,0:T(8,128)(2,1)S(1)}, bf16[256,1024]{1,0:T(8,128)(2,1)}, u32[]{:S(2)}) copy-start(bf16[256,1024]{1,0:T(8,128)(2,1)} %copy-done.8) | copy-start | bytes 1572868
  125.2 23.9 %all-to-all-start.4 = ((bf16[32,8,1024]{2,1,0:T(8,128)(2,1)}), bf16[32,8,1024]{2,1,0:T(8,128)(2,1)}, u32[]{:S(2)}, u32[]{:S(2)}) async-start(bf16[32,8,1024]{2,1,0:T(8,128)(2,1)} %broadcast_in_dim.23), calls=%async_computation.4 | async-start | bytes 1048576 | tf_op jit(solution)/shard_map/all_to_all | solution.py:21
  136.7 37.7 %copy-start.5 = (f32[256,1024]{1,0:T(8,128)}, f32[256,1024]{1,0:T(8,128)S(1)}, u32[]{:S(2)}) copy-start(f32[256,1024]{1,0:T(8,128)S(1)} %fusion.23) | copy-start | bytes 3145732
  149.7 14.7 %all-to-all-start.2 = ((f32[32,1,2]{2,1,0:T(1,128)}), f32[32,1,2]{2,1,0:T(1,128)S(1)}, u32[]{:S(2)}, u32[]{:S(2)}) async-start(f32[32,1,2]{2,1,0:T(1,128)} %broadcast_in_dim.22), calls=%async_computation.2 | async-start | bytes 32768 | tf_op jit(solution)/shard_map/all_to_all | solution.py:21
  157.3 0.8 copy-start.10
  164.5 33.4 %all-to-all-start.6 = ((f32[32,8,1024]{2,1,0:T(8,128)}), f32[32,8,1024]{2,1,0:T(8,128)}, u32[]{:S(2)}, u32[]{:S(2)}) async-start(f32[32,8,1024]{2,1,0:T(8,128)} %fusion.2), calls=%async_computation.6 | async-start | bytes 2097152 | tf_op jit(solution)/shard_map/all_to_all | solution.py:35
  199.2 9.4 %collective-permute-start.1 = (bf16[8,1024]{1,0:T(8,128)(2,1)S(1)}, bf16[8,1024]{1,0:T(8,128)(2,1)S(1)}, u32[]{:S(2)}, u32[]{:S(2)}) collective-permute-start(bf16[8,1024]{1,0:T(8,128)(2,1)S(1)} %add_convert_fusion.3), channel_id=1, source_target_pairs={{32,0},{64,32},{96,64},{128,96},{160,128},{192,160},{224,192},{33,... | collective-permute-start | bytes 49160 | tf_op jit(solution)/shard_map/ppermute | solution.py:47
  203.0 15.1 %all-to-all-start.5 = ((f32[32,1,2]{2,1,0:T(1,128)}), f32[32,1,2]{2,1,0:T(1,128)S(1)}, u32[]{:S(2)}, u32[]{:S(2)}) async-start(f32[32,1,2]{2,1,0:T(1,128)} %broadcast_in_dim.24), calls=%async_computation.5 | async-start | bytes 32768 | tf_op jit(solution)/shard_map/all_to_all | solution.py:21
  219.0 21.8 %all-to-all-start.7 = ((bf16[32,8,1024]{2,1,0:T(8,128)(2,1)}), bf16[32,8,1024]{2,1,0:T(8,128)(2,1)}, u32[]{:S(2)}, u32[]{:S(2)}) async-start(bf16[32,8,1024]{2,1,0:T(8,128)(2,1)} %broadcast_in_dim.25), calls=%async_computation.7 | async-start | bytes 1048576 | tf_op jit(solution)/shard_map/all_to_all | solution.py:21
  223.8 4.0 %copy-start.4 = (f32[256,1024]{1,0:T(8,128)S(1)}, f32[256,1024]{1,0:T(8,128)}, u32[]{:S(2)}) copy-start(f32[256,1024]{1,0:T(8,128)} %copy-done.3) | copy-start | bytes 3145732
  223.9 4.0 %copy-start.15 = (f32[256]{0:T(256)S(1)}, f32[256]{0:T(256)}, u32[]{:S(2)}) copy-start(f32[256]{0:T(256)} %select_reduce_fusion.2) | copy-start | bytes 3076
  227.9 3.9 %copy-start.17 = (s32[256]{0:T(256)S(1)}, s32[256]{0:T(256)}, u32[]{:S(2)}) copy-start(s32[256]{0:T(256)} %compare_convert_fusion.1) | copy-start | bytes 3076
  240.9 3.3 %copy-start.11 = (f32[256,256]{1,0:T(8,128)S(1)}, f32[256,256]{1,0:T(8,128)}, u32[]{:S(2)}) copy-start(f32[256,256]{1,0:T(8,128)} %fusion.77) | copy-start | bytes 786436
  243.4 0.8 copy-start.7
  244.2 1.9 copy-start.16
  247.1 14.3 %all-to-all-start.8 = ((f32[32,1,2]{2,1,0:T(1,128)}), f32[32,1,2]{2,1,0:T(1,128)S(1)}, u32[]{:S(2)}, u32[]{:S(2)}) async-start(f32[32,1,2]{2,1,0:T(1,128)} %broadcast_in_dim.26), calls=%async_computation.8 | async-start | bytes 32768 | tf_op jit(solution)/shard_map/all_to_all | solution.py:21
  261.4 31.2 %all-to-all-start.9 = ((f32[32,8,1024]{2,1,0:T(8,128)}), f32[32,8,1024]{2,1,0:T(8,128)}, u32[]{:S(2)}, u32[]{:S(2)}) async-start(f32[32,8,1024]{2,1,0:T(8,128)} %fusion), calls=%async_computation.9 | async-start | bytes 2097152 | tf_op jit(solution)/shard_map/all_to_all | solution.py:35
  266.1 4.1 %copy-start.6 = (f32[256,1024]{1,0:T(8,128)S(1)}, f32[256,1024]{1,0:T(8,128)}, u32[]{:S(2)}) copy-start(f32[256,1024]{1,0:T(8,128)} %copy-done.5) | copy-start | bytes 3145732
  274.2 6.0 %copy-start.1 = (f32[1024,1024]{1,0:T(8,128)S(1)}, f32[1024,1024]{1,0:T(8,128)}, u32[]{:S(2)}) copy-start(f32[1024,1024]{1,0:T(8,128)} %fusion.55) | copy-start | bytes 12582916
  274.2 7.0 %copy-start.2 = (f32[1024,1024]{1,0:T(8,128)S(1)}, f32[1024,1024]{1,0:T(8,128)}, u32[]{:S(2)}) copy-start(f32[1024,1024]{1,0:T(8,128)} %fusion.56) | copy-start | bytes 12582916
where the time goes:
time: 297 us; the launch traced here: 295 us
  waiting for transfers between devices  107 us (36%)
  matrix products  61.9 us (21%)
  blocking collectives  51.5 us (17%)
  starting transfers between devices  49 us (16%)
  local copies, waits for them, and re-layouts  10.4 us (4%)
  other arithmetic  7.41 us (2%)
  between operations  6.89 us (2%)
    all_to_all x6, waiting for transfers between devices, from_everyone(): return lax.all_to_all(copies, axis, split_axis=0, concat_axis=0, tiled=True)  57.6 us
    all_to_all x1, blocking collectives, from_everyone(): return lax.all_to_all(copies, axis, split_axis=0, concat_axis=0, tiled=True)  51.5 us
    all_to_all x3, waiting for transfers between devices, summed_on_arrival(): lax.all_to_all(blocks, axis, split_axis=0, concat_axis=0, tiled=True)  48.8 us
    all_to_all x6, starting transfers between devices, from_everyone(): return lax.all_to_all(copies, axis, split_axis=0, concat_axis=0, tiled=True)  30.4 us
    all_to_all x3, starting transfers between devices, summed_on_arrival(): lax.all_to_all(blocks, axis, split_axis=0, concat_axis=0, tiled=True)  14.8 us
    dot_general x3, matrix products, per_device(): jnp.einsum('td,tf->df', inputs, dzc, preferred_element_type=jnp.float32)  14.1 us
    dot_general x3, matrix products, per_device(): jnp.einsum('tf,td->fd', hidden, dyc, preferred_element_type=jnp.float32)  10.8 us
    dot_general x3, matrix products, per_device(): jnp.einsum('td,fd->tf', grads, second, preferred_element_type=jnp.float32)  7.56 us
  transfers between devices with their start and end apart: 11, of which 10 were waited for; matrix products, arithmetic and copies ran while one was open for 19% of the time, Pallas kernels for 0%

commit v1 on v0

v1 whole, which is shorter than its diff:
```python
import jax
import jax.numpy as jnp
from jax import lax
from jax.experimental import pallas as pl
from jax.experimental.pallas import tpu as pltpu
from jax.sharding import PartitionSpec as P

D = 1024
FF = 32768
GAMMA = 0.01
F32 = jnp.float32
BF16 = jnp.bfloat16
MIB = 1 << 20


def spread(shard):
    count = lax.axis_size("tensor")
    copies = jnp.broadcast_to(shard, (count, *shard.shape))
    arrived = lax.all_to_all(copies, "tensor", split_axis=0, concat_axis=0, tiled=True)
    return arrived.reshape(count * shard.shape[0], *shard.shape[1:])


def back_kernel(grads_ref, slope_ref, out_t_ref, in_t_ref, dz_ref, share_ref):
    hidden, width = in_t_ref.shape
    step = 256
    grads = grads_ref[...]
    for at in range(0, hidden, step):
        cols = slice(at, at + step)
        back = jnp.dot(grads, out_t_ref[:, cols], preferred_element_type=F32)
        dz_ref[:, cols] = (slope_ref[:, cols] * back).astype(BF16)
    dz = dz_ref[...]
    for at in range(0, width, step):
        cols = slice(at, at + step)
        share = jnp.dot(dz, in_t_ref[:, cols], preferred_element_type=F32)
        share_ref[:, cols] = share.astype(BF16)


def back_step(grads, slope, out_t, in_t):
    tokens, width = grads.shape
    hidden = in_t.shape[0]
    whole = pl.BlockSpec(memory_space=pltpu.VMEM)
    return pl.pallas_call(
        back_kernel,
        out_shape=(
            jax.ShapeDtypeStruct((tokens, hidden), BF16),
            jax.ShapeDtypeStruct((tokens, width), BF16),
        ),
        in_specs=[whole] * 4,
        out_specs=(whole, whole),
        compiler_params=pltpu.CompilerParams(vmem_limit_bytes=24 * MIB),
        cost_estimate=pl.CostEstimate(
            flops=4 * tokens * width * hidden, bytes_accessed=8 * MIB, transcendentals=0
        ),
    )(grads, slope, out_t, in_t)


def per_device(saved_inputs, slot_index, example_lengths, first_grads, loss_grads, w_in, w_out):
    sections = lax.axis_size("section")
    is_last = lax.axis_index("section") == sections - 1
    first, second = w_in[0], w_out[0]
    slots = loss_grads.shape[0] + 1
    picked = [
        lax.dynamic_index_in_dim(saved_inputs[0], slot_index[0, slot], 0, keepdims=False)
        for slot in range(slots)
    ]
    incoming = first_grads[0]
    start = spread(jnp.concatenate([picked[0], incoming], axis=1))
    out_t, in_t = second.T, first.T
    later, out_t, in_t = lax.optimization_barrier(
        (jnp.concatenate(picked[1:], axis=1), out_t, in_t)
    )
    later = spread(later)
    inputs = [start[:, :D]] + [later[:, D * i : D * (i + 1)] for i in range(slots - 1)]
    grads = start[:, D:]
    tokens = grads.shape[0]
    position = jnp.arange(tokens, dtype=jnp.int32)

    dzs, hiddens, dys, results, squares = [], [], [], [], []
    for slot in range(slots):
        x = inputs[slot]
        relu = jnp.maximum(jnp.dot(x, first, preferred_element_type=F32), 0.0)
        hidden = (relu * relu).astype(BF16)
        dz, share = back_step(grads, 2.0 * relu, out_t, in_t)
        arrived = lax.all_to_all(
            share.reshape(-1, 8, D), "tensor", split_axis=0, concat_axis=0, tiled=True
        )
        second_example = (position >= example_lengths[0, slot, 0]).astype(F32)
        same = second_example[:, None] == second_example[None, :]
        gram_x = jnp.einsum("td,ud->tu", x, x, preferred_element_type=F32)
        gram_z = jnp.einsum("tf,uf->tu", dz, dz, preferred_element_type=F32)
        gram_h = jnp.einsum("tf,uf->tu", hidden, hidden, preferred_element_type=F32)
        gram_y = jnp.einsum("td,ud->tu", grads, grads, preferred_element_type=F32)
        rows = jnp.sum(jnp.where(same, gram_x * gram_z + gram_h * gram_y, 0.0), axis=1)
        both = jnp.stack([1.0 - second_example, second_example])
        squares.append(jnp.sum(both * rows[None, :], axis=1))
        dzs.append(dz)
        hiddens.append(hidden)
        dys.append(grads)
        passing = (incoming.astype(F32) + jnp.sum(arrived.astype(F32), axis=0)).astype(BF16)
        results.append(passing)
        if slot + 1 < slots:
            shifted = lax.ppermute(
                passing, "section", [(source, source - 1) for source in range(1, sections)]
            )
            incoming = jnp.where(is_last, loss_grads[slot], shifted)
            grads = spread(incoming)

    mine = jnp.concatenate(squares)
    mine = jnp.pad(mine, (0, 128 - mine.shape[0]))[None]
    totals = jnp.sum(spread(mine), axis=0)[: 2 * slots].reshape(slots, 2)
    factor = 1.0 / (jnp.sqrt(totals / (D * FF)) + GAMMA)
    scale = jnp.concatenate(
        [
            jnp.where(position >= example_lengths[0, slot, 0], factor[slot, 1], factor[slot, 0])
            for slot in range(slots)
        ]
    )[:, None]
    dzc = (jnp.concatenate(dzs).astype(F32) * scale).astype(BF16)
    dyc = (jnp.concatenate(dys).astype(F32) * scale).astype(BF16)
    grad_in = jnp.einsum(
        "td,tf->df", jnp.concatenate(inputs), dzc, preferred_element_type=F32
    ).astype(BF16)
    grad_out = jnp.einsum(
        "tf,td->fd", jnp.concatenate(hiddens), dyc, preferred_element_type=F32
    ).astype(BF16)
    return grad_in[None], grad_out[None], jnp.stack(results)[None]


def solution(mesh):
    return jax.shard_map(
        per_device,
        mesh=mesh,
        in_specs=(
            P("section", None, "tensor", None),
            P("section", None),
            P("section", None, None),
            P("section", "tensor", None),
            P(None, "tensor", None),
            P("section", None, "tensor"),
            P("section", "tensor", None),
        ),
        out_specs=(
            P("section", None, "tensor"),
            P("section", "tensor", None),
            P("section", None, "tensor", None),
        ),
        check_vma=False,
    )
```

time: 297 us -> 237 us (0.80)
  matrix products: 61.9 us -> 28.8 us
  blocking collectives: 51.5 us -> 22.2 us
  waiting for transfers between devices: 107 us -> 80.8 us
  local copies, waits for them, and re-layouts: 10.4 us -> 30.8 us
  other arithmetic: 7.41 us -> 16.3 us
  starting transfers between devices: 49 us -> 44.7 us
  Pallas kernels: 0 us -> 3.75 us
    dot_general x30 -> x17, matrix products: 61.9 us -> 28.8 us  [the longest x3 7.95 us: per_device(): relu = jnp.maximum(jnp.dot(x, first, preferred_element_type=F32), 0.0)]
    all_to_all x1, blocking collectives: 51.5 us -> 22.2 us  [per_device(): lax.all_to_all(share.reshape(-1, 8, D), 'tensor', split_axis=0, concat_ax...]
    all_to_all x9 -> x7, waiting for transfers between devices: 106 us -> 79.5 us  [the longest x5 67.1 us: spread(): lax.all_to_all(copies, 'tensor', split_axis=0, concat_axis=0, tiled=True)]
    unnamed x36 -> x72, local copies, waits for them, and re-layouts: 3.39 us -> 19.6 us
    select_n x2 -> x4, other arithmetic: 0.01 us -> 5.57 us  [the longest x2 5.55 us: per_device(): jnp.where(position >= example_lengths[0, slot, 0], factor[slot, 1], facto...]
    all_to_all x9 -> x7, starting transfers between devices: 45.1 us -> 40.8 us  [the longest x5 31.6 us: spread(): lax.all_to_all(copies, 'tensor', split_axis=0, concat_axis=0, tiled=True)]
    slice x1 -> x4, local copies, waits for them, and re-layouts: 0.21 us -> 4.47 us  [the longest x1 2.34 us: per_device(): later[:, D * i:D * (i + 1)]]
    pallas_call x0 -> x3, Pallas kernels: none -> 3.75 us  [back_step(): pl.pallas_call(back_kernel, out_shape=(jax.ShapeDtypeStruct((tokens, hidd...]
  transfers between devices with their start and end apart: 11 -> 9, of which waited for: 10 -> 8; matrix products, arithmetic and copies ran while one was open for 19% -> 21% of each run, Pallas kernels for 0% -> 0%
where the time goes in v1:
time: 237 us; the launch traced here: 234 us
  waiting for transfers between devices  80.8 us (34%)
  starting transfers between devices  44.7 us (19%)
  local copies, waits for them, and re-layouts  30.8 us (13%)
  matrix products  28.8 us (12%)
  blocking collectives  22.2 us (9%)
  other arithmetic  16.3 us (7%)
  between operations  7.02 us (3%)
  Pallas kernels  3.75 us (2%)
    all_to_all x5, waiting for transfers between devices, spread(): lax.all_to_all(copies, 'tensor', split_axis=0, concat_axis=0, tiled=True)  67.1 us
    all_to_all x5, starting transfers between devices, spread(): lax.all_to_all(copies, 'tensor', split_axis=0, concat_axis=0, tiled=True)  31.6 us
    all_to_all x1, blocking collectives, per_device(): lax.all_to_all(share.reshape(-1, 8, D), 'tensor', split_axis=0, concat_ax...  22.2 us
    unnamed x72, local copies, waits for them, and re-layouts  19.6 us
    all_to_all x2, waiting for transfers between devices, per_device(): lax.all_to_all(share.reshape(-1, 8, D), 'tensor', split_axis=0, concat_ax...  12.4 us
    all_to_all x2, starting transfers between devices, per_device(): lax.all_to_all(share.reshape(-1, 8, D), 'tensor', split_axis=0, concat_ax...  9.24 us
    dot_general x3, matrix products, per_device(): relu = jnp.maximum(jnp.dot(x, first, preferred_element_type=F32), 0.0)  7.95 us
    dot_general x3, matrix products, per_device(): gram_x = jnp.einsum('td,ud->tu', x, x, preferred_element_type=F32)  6.25 us
  transfers between devices with their start and end apart: 9, of which 8 were waited for; matrix products, arithmetic and copies ran while one was open for 21% of the time, Pallas kernels for 0%

profile of v1, /device:TPU:8, one launch (start us, length us, event | category | flops | bytes accessed | tf_op | source)
XLA Modules:
  0.0 234.4 jit_solution(14091618748253603575)
XLA Ops:
  0.6 1.4 fusion.75
  9.3 1.1 broadcast_in_dim.61
  10.4 11.3 %all-to-all-start = ((bf16[32,8,2048]{2,1,0:T(8,128)(2,1)}), bf16[32,8,2048]{2,1,0:T(8,128)(2,1)S(1)}, u32[]{:S(2)}, u32[]{:S(2)}) async-start(bf16[32,8,2048]{2,1,0:T(8,128)(2,1)} %broadcast_in_dim.61), calls=%async_computation | async-start | bytes 2097152 | tf_op jit(solution)/shard_map/all_to_all | solution.py:19
  21.7 2.9 %copy.16 = bf16[1,1024,1024]{1,2,0:T(8,128)(2,1)S(1)} copy(bf16[1,1024,1024]{2,1,0:T(8,128)(2,1)} %param.13) | data formatting | bytes 4194304 | tf_op args[6]
  24.6 3.9 %copy.17 = bf16[1,1024,1024]{1,2,0:T(8,128)(2,1)} copy(bf16[1,1024,1024]{2,1,0:T(8,128)(2,1)} %param.12) | data formatting | bytes 4194304 | tf_op args[5]
  28.6 21.3 %all-to-all-done = bf16[32,8,2048]{2,1,0:T(8,128)(2,1)S(1)} async-done(((bf16[32,8,2048]{2,1,0:T(8,128)(2,1)}), bf16[32,8,2048]{2,1,0:T(8,128)(2,1)S(1)}, u32[]{:S(2)}, u32[]{:S(2)}) %all-to-all-start) | async-done | bytes 1048608 | tf_op jit(solution)/shard_map/all_to_all | solution.py:19
  50.7 1.3 copy-done.22
  52.0 1.5 multiply_convert_fusion.6
  54.0 1.2 shard_map.94
  55.3 22.2 %all_to_all.40 = bf16[32,8,1024]{2,1,0:T(8,128)(2,1)S(1)} all-to-all(bf16[32,8,1024]{2,1,0:T(8,128)(2,1)S(1)} %bitcast.100), channel_id=1, replica_groups=mesh['section'=8,'tensor'=32] {'tensor'}, dimensions={0} | all-to-all | bytes 1048576 | tf_op jit(solution)/shard_map/all_to_all | solution.py:84
  77.5 1.1 broadcast_in_dim.62
  78.6 4.8 %all-to-all-start.1 = ((bf16[32,8,2048]{2,1,0:T(8,128)(2,1)}), bf16[32,8,2048]{2,1,0:T(8,128)(2,1)}, u32[]{:S(2)}, u32[]{:S(2)}) async-start(bf16[32,8,2048]{2,1,0:T(8,128)(2,1)} %broadcast_in_dim.62), calls=%async_computation.1 | async-start | bytes 2097152 | tf_op jit(solution)/shard_map/all_to_all | solution.py:19
  86.4 1.2 fusion.52
  88.8 1.2 fusion.54
  90.8 1.9 collective-permute-start
  92.7 1.5 fusion.68
  94.3 16.0 %all-to-all-done.1 = bf16[32,8,2048]{2,1,0:T(8,128)(2,1)} async-done(((bf16[32,8,2048]{2,1,0:T(8,128)(2,1)}), bf16[32,8,2048]{2,1,0:T(8,128)(2,1)}, u32[]{:S(2)}, u32[]{:S(2)}) %all-to-all-start.1) | async-done | bytes 1048608 | tf_op jit(solution)/shard_map/all_to_all | solution.py:19
  111.1 5.6 %all-to-all-start.3 = ((bf16[32,8,1024]{2,1,0:T(8,128)(2,1)}), bf16[32,8,1024]{2,1,0:T(8,128)(2,1)S(1)}, u32[]{:S(2)}, u32[]{:S(2)}) async-start(bf16[32,8,1024]{2,1,0:T(8,128)(2,1)} %broadcast_in_dim.63), calls=%async_computation.3 | async-start | bytes 1048576 | tf_op jit(solution)/shard_map/all_to_all | solution.py:19
  116.8 2.4 %fusion.65 = f32[256,256]{0,1:T(8,128)} fusion(bf16[256,2048]{1,0:T(8,128)(2,1)} %bitcast.12), kind=kOutput, calls=%fused_computation.107 | convolution fusion | flops 134217728 | bytes 786432 | tf_op jit(solution)/shard_map/td,ud->tu/dot_general | solution.py:89
  119.2 1.5 fusion.76
  121.8 2.9 %multiply_convert_fusion.5 = (bf16[256,1024]{1,0:T(8,128)(2,1)}, f32[256,1024]{1,0:T(8,128)}) fusion(bf16[1,1024,1024]{2,1,0:T(8,128)(2,1)S(1)} %copy-done.23, bf16[256,2048]{1,0:T(8,128)(2,1)} %bitcast.12), kind=kOutput, calls=%fused_computation.52 | convolution fusion | flops 537919488 | bytes 4194304 | tf_op jit(solution)/shard_map/dot_general | solution.py:81
  124.7 8.5 %all-to-all-done.3 = bf16[32,8,1024]{2,1,0:T(8,128)(2,1)S(1)} async-done(((bf16[32,8,1024]{2,1,0:T(8,128)(2,1)}), bf16[32,8,1024]{2,1,0:T(8,128)(2,1)S(1)}, u32[]{:S(2)}, u32[]{:S(2)}) %all-to-all-start.3) | async-done | bytes 524320 | tf_op jit(solution)/shard_map/all_to_all | solution.py:19
  134.1 1.6 copy-done.1
  136.7 1.2 copy-done.15
  137.9 1.2 shard_map.95
  140.0 4.6 %all-to-all-start.4 = ((bf16[32,8,1024]{2,1,0:T(8,128)(2,1)}), bf16[32,8,1024]{2,1,0:T(8,128)(2,1)}, u32[]{:S(2)}, u32[]{:S(2)}) async-start(bf16[32,8,1024]{2,1,0:T(8,128)(2,1)} %bitcast.99), calls=%async_computation.4 | async-start | bytes 1048576 | tf_op jit(solution)/shard_map/all_to_all | solution.py:84
  144.6 1.3 fusion.45
  145.9 3.5 %multiply_convert_fusion.4 = (bf16[256,1024]{1,0:T(8,128)(2,1)S(1)}, f32[256,1024]{1,0:T(8,128)}) fusion(bf16[1,1024,1024]{2,1,0:T(8,128)(2,1)} %param.12, bf16[256,2048]{1,0:T(8,128)(2,1)} %bitcast.12), kind=kOutput, calls=%fused_computation.51 | convolution fusion | flops 537919488 | bytes 4194304 | tf_op jit(solution)/shard_map/dot_general | solution.py:81
  151.6 9.2 %all-to-all-done.4 = bf16[32,8,1024]{2,1,0:T(8,128)(2,1)} async-done(((bf16[32,8,1024]{2,1,0:T(8,128)(2,1)}), bf16[32,8,1024]{2,1,0:T(8,128)(2,1)}, u32[]{:S(2)}, u32[]{:S(2)}) %all-to-all-start.4) | async-done | bytes 524320 | tf_op jit(solution)/shard_map/all_to_all | solution.py:84
  160.8 1.1 convert_reduce_fusion.1
  161.9 1.9 collective-permute-start.1
  164.0 1.3 collective-permute-done.1
  166.2 4.5 %all-to-all-start.5 = ((bf16[32,8,1024]{2,1,0:T(8,128)(2,1)}), bf16[32,8,1024]{2,1,0:T(8,128)(2,1)S(1)}, u32[]{:S(2)}, u32[]{:S(2)}) async-start(bf16[32,8,1024]{2,1,0:T(8,128)(2,1)} %broadcast_in_dim.64), calls=%async_computation.5 | async-start | bytes 1048576 | tf_op jit(solution)/shard_map/all_to_all | solution.py:19
  170.7 2.3 fusion.62
  173.0 2.3 fusion.72
  176.2 11.6 %all-to-all-done.5 = bf16[32,8,1024]{2,1,0:T(8,128)(2,1)S(1)} async-done(((bf16[32,8,1024]{2,1,0:T(8,128)(2,1)}), bf16[32,8,1024]{2,1,0:T(8,128)(2,1)S(1)}, u32[]{:S(2)}, u32[]{:S(2)}) %all-to-all-start.5) | async-done | bytes 524320 | tf_op jit(solution)/shard_map/all_to_all | solution.py:19
  188.7 1.6 copy-done.2
  191.3 1.2 copy-done.14
  192.5 1.2 shard_map.96
  195.4 5.3 %all-to-all-start.6 = ((f32[32,1,128]{2,1,0:T(1,128)}), f32[32,1,128]{2,1,0:T(1,128)S(1)}, u32[]{:S(2)}, u32[]{:S(2)}) async-start(f32[32,1,128]{2,1,0:T(1,128)} %broadcast_in_dim.66), calls=%async_computation.6 | async-start | bytes 32768 | tf_op jit(solution)/shard_map/all_to_all | solution.py:19
  200.8 9.6 %all-to-all-done.6 = f32[32,1,128]{2,1,0:T(1,128)S(1)} async-done(((f32[32,1,128]{2,1,0:T(1,128)}), f32[32,1,128]{2,1,0:T(1,128)S(1)}, u32[]{:S(2)}, u32[]{:S(2)}) %all-to-all-start.6) | async-done | bytes 16416 | tf_op jit(solution)/shard_map/all_to_all | solution.py:19
  210.4 4.6 %all-to-all-start.7 = ((bf16[32,8,1024]{2,1,0:T(8,128)(2,1)}), bf16[32,8,1024]{2,1,0:T(8,128)(2,1)}, u32[]{:S(2)}, u32[]{:S(2)}) async-start(bf16[32,8,1024]{2,1,0:T(8,128)(2,1)} %bitcast.98), calls=%async_computation.7 | async-start | bytes 1048576 | tf_op jit(solution)/shard_map/all_to_all | solution.py:84
  215.8 1.8 fusion.55
  217.6 3.7 %fusion.51 = (f32[256]{0:T(256)S(1)}, f32[256]{0:T(256)S(1)}) fusion(f32[]{:T(128)} %bitcast.28, f32[]{:T(128)} %bitcast.27, s32[]{:T(128)} %bitcast.21, f32[]{:T(128)} %bitcast.26, f32[]{:T(128)} %bitcast.25, s32[]{:T(128)} %bitcast.20), kind=kLoop, calls=%fused_computation.84 | loop fusion | flops 1024 | bytes 2072 | tf_op jit(solution)/shard_map/jit(_where)/select_n | solution.py:114
  221.4 4.7 %convert_bitcast_fusion = bf16[1,1024,1024]{2,1,0:T(8,128)(2,1)} fusion(bf16[256,1024]{1,0:T(8,128)(2,1)} %copy-done.21, bf16[256,1024]{1,0:T(8,128)(2,1)} %get-tuple-element.23, bf16[256,1024]{1,0:T(8,128)(2,1)} %get-tuple-element.21, bf16[256,1024]{1,0:T(8,128)(2,1)S(1)} %bitcast.97, bf16[256,1024]{1,0:T(8,128)(2,1)S(1)} %bitcast.95, ...), kind=kOutput, calls=%fused_computation.8 | convolution fusion | flops 1622671360 | bytes 5245952 | tf_op jit(solution)/shard_map/tf,td->fd/dot_general | solution.py:123
  226.2 3.2 %convert_bitcast_fusion.1 = bf16[1,1024,1024]{2,1,0:T(8,128)(2,1)} fusion(bf16[256,1024]{1,0:T(8,128)(2,1)S(1)} %copy-done.26, bf16[256,1024]{1,0:T(8,128)(2,1)S(1)} %copy-done.25, bf16[256,1024]{1,0:T(8,128)(2,1)S(1)} %copy-done.24, bf16[256,1024]{1,0:T(8,128)(2,1)S(1)} %get-tuple-element.19, bf16[256,1024]{1,0:T(8,128)(2,1)S(1)} %get-tuple-element.17, ...), kind=kOutput, calls=%fused_computation.9 | convolution fusion | flops 1622671360 | bytes 5245952 | tf_op jit(solution)/shard_map/td,tf->df/dot_general | solution.py:120
  229.4 3.2 %all-to-all-done.7 = bf16[32,8,1024]{2,1,0:T(8,128)(2,1)} async-done(((bf16[32,8,1024]{2,1,0:T(8,128)(2,1)}), bf16[32,8,1024]{2,1,0:T(8,128)(2,1)}, u32[]{:S(2)}, u32[]{:S(2)}) %all-to-all-start.7) | async-done | bytes 524320 | tf_op jit(solution)/shard_map/all_to_all | solution.py:84
  232.6 1.1 convert_reduce_fusion
  (105 shorter events, 21.2 us)
Async XLA Ops:
  10.4 39.4 %all-to-all-start = ((bf16[32,8,2048]{2,1,0:T(8,128)(2,1)}), bf16[32,8,2048]{2,1,0:T(8,128)(2,1)S(1)}, u32[]{:S(2)}, u32[]{:S(2)}) async-start(bf16[32,8,2048]{2,1,0:T(8,128)(2,1)} %broadcast_in_dim.61), calls=%async_computation | async-start | bytes 2097152 | tf_op jit(solution)/shard_map/all_to_all | solution.py:19
  49.9 3.7 %copy-start.18 = (bf16[32,8,2048]{2,1,0:T(8,128)(2,1)}, bf16[32,8,2048]{2,1,0:T(8,128)(2,1)S(1)}, u32[]{:S(2)}) copy-start(bf16[32,8,2048]{2,1,0:T(8,128)(2,1)S(1)} %all-to-all-done) | copy-start | bytes 3145732
  49.9 2.2 copy-start.22
  52.0 1.5 copy-start.12
  52.0 2.0 copy-start
  55.2 89.4 %copy-start.3 = (bf16[256,1024]{1,0:T(8,128)(2,1)}, bf16[256,1024]{1,0:T(8,128)(2,1)S(1)}, u32[]{:S(2)}) copy-start(bf16[256,1024]{1,0:T(8,128)(2,1)S(1)} %get-tuple-element.15) | copy-start | bytes 1572868
  55.3 28.1 %copy-start.32 = (s32[1,3,2]{1,2,0:T(2,128)S(1)}, s32[1,3,2]{1,2,0:T(2,128)}, u32[]{:S(2)}) copy-start(s32[1,3,2]{1,2,0:T(2,128)} %param.9) | copy-start | bytes 76
  77.5 13.3 %copy-start.30 = (bf16[1,8,1024]{2,1,0:T(8,128)(2,1)S(1)}, bf16[1,8,1024]{2,1,0:T(8,128)(2,1)}, u32[]{:S(2)}) copy-start(bf16[1,8,1024]{2,1,0:T(8,128)(2,1)} %param.10) | copy-start | bytes 49156
  78.6 15.7 %copy-start.31 = (bf16[2,8,1024]{2,1,0:T(8,128)(2,1)S(1)}, bf16[2,8,1024]{2,1,0:T(8,128)(2,1)}, u32[]{:S(2)}) copy-start(bf16[2,8,1024]{2,1,0:T(8,128)(2,1)} %param.11) | copy-start | bytes 98308
  78.6 31.7 %all-to-all-start.1 = ((bf16[32,8,2048]{2,1,0:T(8,128)(2,1)}), bf16[32,8,2048]{2,1,0:T(8,128)(2,1)}, u32[]{:S(2)}, u32[]{:S(2)}) async-start(bf16[32,8,2048]{2,1,0:T(8,128)(2,1)} %broadcast_in_dim.62), calls=%async_computation.1 | async-start | bytes 2097152 | tf_op jit(solution)/shard_map/all_to_all | solution.py:19
  90.8 3.5 %collective-permute-start = (bf16[8,1024]{1,0:T(8,128)(2,1)S(1)}, bf16[8,1024]{1,0:T(8,128)(2,1)S(1)}, u32[]{:S(2)}, u32[]{:S(2)}) collective-permute-start(bf16[8,1024]{1,0:T(8,128)(2,1)S(1)} %add_convert_fusion.2), channel_id=1, source_target_pairs={{32,0},{64,32},{96,64},{128,96},{160,128},{192,160},{224,192},{33,... | collective-permute-start | bytes 49160 | tf_op jit(solution)/shard_map/ppermute | solution.py:102
  111.1 22.1 %all-to-all-start.3 = ((bf16[32,8,1024]{2,1,0:T(8,128)(2,1)}), bf16[32,8,1024]{2,1,0:T(8,128)(2,1)S(1)}, u32[]{:S(2)}, u32[]{:S(2)}) async-start(bf16[32,8,1024]{2,1,0:T(8,128)(2,1)} %broadcast_in_dim.63), calls=%async_computation.3 | async-start | bytes 1048576 | tf_op jit(solution)/shard_map/all_to_all | solution.py:19
  116.7 4.0 %copy-start.19 = (bf16[32,8,2048]{2,1,0:T(8,128)(2,1)S(1)}, bf16[32,8,2048]{2,1,0:T(8,128)(2,1)}, u32[]{:S(2)}) copy-start(bf16[32,8,2048]{2,1,0:T(8,128)(2,1)} %copy-done.18) | copy-start | bytes 3145732
  116.7 5.0 %copy-start.23 = (bf16[1,1024,1024]{2,1,0:T(8,128)(2,1)S(1)}, bf16[1,1024,1024]{2,1,0:T(8,128)(2,1)}, u32[]{:S(2)}) copy-start(bf16[1,1024,1024]{2,1,0:T(8,128)(2,1)} %param.12) | copy-start | bytes 6291460
  133.2 0.8 copy-start.5
  134.1 1.6 copy-start.1
  135.7 1.0 copy-start.6
  136.7 1.2 copy-start.15
  139.2 0.8 copy-start.17
  140.0 20.8 %all-to-all-start.4 = ((bf16[32,8,1024]{2,1,0:T(8,128)(2,1)}), bf16[32,8,1024]{2,1,0:T(8,128)(2,1)}, u32[]{:S(2)}, u32[]{:S(2)}) async-start(bf16[32,8,1024]{2,1,0:T(8,128)(2,1)} %bitcast.99), calls=%async_computation.4 | async-start | bytes 1048576 | tf_op jit(solution)/shard_map/all_to_all | solution.py:84
  145.9 4.7 %copy-start.20 = (bf16[256,1024]{1,0:T(8,128)(2,1)S(1)}, bf16[256,1024]{1,0:T(8,128)(2,1)}, u32[]{:S(2)}) copy-start(bf16[256,1024]{1,0:T(8,128)(2,1)} %get-tuple-element.23) | copy-start | bytes 1572868
  149.4 0.8 copy-start.21
  161.9 3.4 %collective-permute-start.1 = (bf16[8,1024]{1,0:T(8,128)(2,1)S(1)}, bf16[8,1024]{1,0:T(8,128)(2,1)S(1)}, u32[]{:S(2)}, u32[]{:S(2)}) collective-permute-start(bf16[8,1024]{1,0:T(8,128)(2,1)S(1)} %add_convert_fusion.1), channel_id=1, source_target_pairs={{32,0},{64,32},{96,64},{128,96},{160,128},{192,160},{224,192},{33,... | collective-permute-start | bytes 49160 | tf_op jit(solution)/shard_map/ppermute | solution.py:102
  166.2 21.7 %all-to-all-start.5 = ((bf16[32,8,1024]{2,1,0:T(8,128)(2,1)}), bf16[32,8,1024]{2,1,0:T(8,128)(2,1)S(1)}, u32[]{:S(2)}, u32[]{:S(2)}) async-start(bf16[32,8,1024]{2,1,0:T(8,128)(2,1)} %broadcast_in_dim.64), calls=%async_computation.5 | async-start | bytes 1048576 | tf_op jit(solution)/shard_map/all_to_all | solution.py:19
  170.7 4.7 %copy-start.28 = (f32[256,256]{0,1:T(8,128)S(1)}, f32[256,256]{0,1:T(8,128)}, u32[]{:S(2)}) copy-start(f32[256,256]{0,1:T(8,128)} %fusion.65) | copy-start | bytes 786436
  173.0 2.7 %copy-start.7 = (bf16[32,8,1024]{2,1,0:T(8,128)(2,1)S(1)}, bf16[32,8,1024]{2,1,0:T(8,128)(2,1)}, u32[]{:S(2)}) copy-start(bf16[32,8,1024]{2,1,0:T(8,128)(2,1)} %copy-done.5) | copy-start | bytes 1572868
  173.0 2.7 %copy-start.27 = (f32[256,256]{0,1:T(8,128)S(1)}, f32[256,256]{0,1:T(8,128)}, u32[]{:S(2)}) copy-start(f32[256,256]{0,1:T(8,128)} %fusion.77) | copy-start | bytes 786436
  173.0 2.7 %copy-start.34 = (f32[256]{0:T(256)S(1)}, f32[256]{0:T(256)}, u32[]{:S(2)}) copy-start(f32[256]{0:T(256)} %fusion.54) | copy-start | bytes 3076
  187.9 0.8 copy-start.9
  188.7 1.6 copy-start.2
  190.3 1.0 copy-start.10
  191.3 1.2 copy-start.14
  192.5 1.3 copy-start.29
  192.5 1.7 copy-start.33
  193.8 0.8 copy-start.16
  193.8 27.5 %copy-start.8 = (bf16[32,8,1024]{2,1,0:T(8,128)(2,1)S(1)}, bf16[32,8,1024]{2,1,0:T(8,128)(2,1)}, u32[]{:S(2)}) copy-start(bf16[32,8,1024]{2,1,0:T(8,128)(2,1)} %copy-done.5) | copy-start | bytes 1572868
  193.8 27.5 %copy-start.11 = (bf16[32,8,1024]{2,1,0:T(8,128)(2,1)S(1)}, bf16[32,8,1024]{2,1,0:T(8,128)(2,1)}, u32[]{:S(2)}) copy-start(bf16[32,8,1024]{2,1,0:T(8,128)(2,1)} %copy-done.9) | copy-start | bytes 1572868
  193.8 27.5 %copy-start.13 = (bf16[256,1024]{1,0:T(8,128)(2,1)S(1)}, bf16[256,1024]{1,0:T(8,128)(2,1)}, u32[]{:S(2)}) copy-start(bf16[256,1024]{1,0:T(8,128)(2,1)} %copy-done.12) | copy-start | bytes 1572868
  195.4 15.0 %all-to-all-start.6 = ((f32[32,1,128]{2,1,0:T(1,128)}), f32[32,1,128]{2,1,0:T(1,128)S(1)}, u32[]{:S(2)}, u32[]{:S(2)}) async-start(f32[32,1,128]{2,1,0:T(1,128)} %broadcast_in_dim.66), calls=%async_computation.6 | async-start | bytes 32768 | tf_op jit(solution)/shard_map/all_to_all | solution.py:19
  210.4 22.2 %all-to-all-start.7 = ((bf16[32,8,1024]{2,1,0:T(8,128)(2,1)}), bf16[32,8,1024]{2,1,0:T(8,128)(2,1)}, u32[]{:S(2)}, u32[]{:S(2)}) async-start(bf16[32,8,1024]{2,1,0:T(8,128)(2,1)} %bitcast.98), calls=%async_computation.7 | async-start | bytes 1048576 | tf_op jit(solution)/shard_map/all_to_all | solution.py:84
  221.4 4.8 %copy-start.4 = (bf16[256,1024]{1,0:T(8,128)(2,1)S(1)}, bf16[256,1024]{1,0:T(8,128)(2,1)}, u32[]{:S(2)}) copy-start(bf16[256,1024]{1,0:T(8,128)(2,1)} %copy-done.3) | copy-start | bytes 1572868
  221.4 4.8 %copy-start.24 = (bf16[256,1024]{1,0:T(8,128)(2,1)S(1)}, bf16[256,1024]{1,0:T(8,128)(2,1)}, u32[]{:S(2)}) copy-start(bf16[256,1024]{1,0:T(8,128)(2,1)} %get-tuple-element.28) | copy-start | bytes 1572868
  221.4 4.8 %copy-start.25 = (bf16[256,1024]{1,0:T(8,128)(2,1)S(1)}, bf16[256,1024]{1,0:T(8,128)(2,1)}, u32[]{:S(2)}) copy-start(bf16[256,1024]{1,0:T(8,128)(2,1)} %get-tuple-element.29) | copy-start | bytes 1572868
  221.4 4.8 %copy-start.26 = (bf16[256,1024]{1,0:T(8,128)(2,1)S(1)}, bf16[256,1024]{1,0:T(8,128)(2,1)}, u32[]{:S(2)}) copy-start(bf16[256,1024]{1,0:T(8,128)(2,1)} %get-tuple-element.30) | copy-start | bytes 1572868

commit v2 on v1

v2 whole, which is shorter than its diff:
```python
import jax
import jax.numpy as jnp
from jax import lax
from jax.experimental import pallas as pl
from jax.experimental.pallas import tpu as pltpu
from jax.sharding import PartitionSpec as P

D = 1024
FF = 32768
GAMMA = 0.01
F32 = jnp.float32
BF16 = jnp.bfloat16
MIB = 1 << 20
STEP = 256
LANES = 128

ANY = pl.BlockSpec(memory_space=pl.ANY)
SMEM = pl.BlockSpec(memory_space=pltpu.SMEM)


def shape(*dims, dtype=BF16):
    return jax.ShapeDtypeStruct(dims, dtype)


def call(kernel, outs, operands, scratch, copies, flops, name, smem=0):
    return pl.pallas_call(
        kernel,
        out_shape=outs,
        in_specs=[SMEM] * smem + [ANY] * (len(operands) - smem),
        out_specs=jax.tree.map(lambda _: ANY, outs),
        scratch_shapes=[pltpu.VMEM(dims, dtype) for dims, dtype in scratch]
        + [pltpu.SemaphoreType.DMA((copies,))],
        name=name,
        compiler_params=pltpu.CompilerParams(vmem_limit_bytes=60 * MIB),
        cost_estimate=pl.CostEstimate(flops=flops, bytes_accessed=4 * MIB, transcendentals=0),
    )(*operands)


class Copies:
    def __init__(self, sems):
        self.sems, self.used, self.open = sems, 0, []

    def start(self, source, target):
        copy = pltpu.make_async_copy(source, target, self.sems.at[self.used])
        self.used += 1
        copy.start()
        return copy

    def store(self, source, target):
        self.open.append(self.start(source, target))

    def finish(self):
        for copy in self.open:
            copy.wait()


def parts(extent):
    return [slice(at, at + STEP) for at in range(0, extent, STEP)]


def nt(a, b):
    return lax.dot_general(a, b, (((1,), (1,)), ((), ())), preferred_element_type=F32)


def mm(a, b):
    return jnp.dot(a, b, preferred_element_type=F32)


def start_kernel(index, saved, grads, blocks, saved_v, row_v, sems):
    copies = Copies(sems)
    loads = [copies.start(saved, saved_v), copies.start(grads, row_v.at[:, D:])]
    for load in loads:
        load.wait()
    row_v[:, :D] = saved_v[index[0, 0]]
    for peer in range(blocks.shape[0]):
        copies.store(row_v, blocks.at[peer])
    copies.finish()


def spread_kernel(last, shifted, loss, blocks, chosen, shifted_v, loss_v, sems):
    copies = Copies(sems)
    loads = [copies.start(shifted, shifted_v), copies.start(loss, loss_v)]
    for load in loads:
        load.wait()
    shifted_v[...] = jnp.where(last[0] > 0, loss_v[...], shifted_v[...])
    for peer in range(blocks.shape[0]):
        copies.store(shifted_v, blocks.at[peer])
    copies.store(shifted_v, chosen)
    copies.finish()


def picked(place, index, source):
    if len(source.shape) == 2:
        return source.at[:, :D]
    return source.at[index[0, place]]


def forward_kernel(place, index, source, weights, slope, hidden, x_v, w_v, slope_v, hidden_v, sems):
    copies = Copies(sems)
    x_load = copies.start(picked(place, index, source), x_v)
    chunks = parts(weights.shape[1])
    loads = [copies.start(weights.at[:, cols], w_v.at[:, cols]) for cols in chunks]
    x_load.wait()
    for cols, load in zip(chunks, loads):
        load.wait()
        relu = jnp.maximum(mm(x_v[...], w_v[:, cols]), 0.0)
        slope_v[:, cols] = 2.0 * relu
        hidden_v[:, cols] = (relu * relu).astype(BF16)
        copies.store(slope_v.at[:, cols], slope.at[:, cols])
        copies.store(hidden_v.at[:, cols], hidden.at[:, cols])
    copies.finish()


def masked_sums(slot, lengths, paired):
    cut = lengths[0, 2 * slot]
    tokens = paired.shape[0]
    row = lax.broadcasted_iota(jnp.int32, (tokens, tokens), 0) < cut
    col = lax.broadcasted_iota(jnp.int32, (tokens, tokens), 1) < cut
    before = jnp.sum(jnp.where(row & col, paired, 0.0), axis=(0, 1), keepdims=True)
    after = jnp.sum(jnp.where(row | col, 0.0, paired), axis=(0, 1), keepdims=True)
    lane = lax.broadcasted_iota(jnp.int32, (1, LANES), 1)
    return jnp.where(lane == 2 * slot, before, jnp.where(lane == 2 * slot + 1, after, 0.0))


def back_kernel(
    col, slot, lengths, source, slope, w_out, w_in, *refs
):
    if slot is None:
        dz, share, g_v, slope_v, out_v, in_v, dz_v, share_v, sems = refs
    else:
        gram_x, gram_h, sums = refs[:3]
        dz, share, g_v, slope_v, out_v, in_v, dz_v, share_v, gx_v, gh_v, sums_v, sems = refs[3:]
    copies = Copies(sems)
    g_load = copies.start(source.at[:, col : col + D], g_v)
    hidden_parts, model_parts = parts(w_out.shape[0]), parts(w_in.shape[0])
    firsts = [
        (
            copies.start(w_out.at[part, :], out_v.at[part, :]),
            copies.start(slope.at[:, part], slope_v.at[:, part]),
        )
        for part in hidden_parts
    ]
    seconds = [copies.start(w_in.at[part, :], in_v.at[part, :]) for part in model_parts]
    if slot is not None:
        extra = [
            copies.start(a, b) for a, b in ((gram_x, gx_v), (gram_h, gh_v), (sums, sums_v))
        ]
    g_load.wait()
    for part, loads in zip(hidden_parts, firsts):
        for load in loads:
            load.wait()
        back = nt(g_v[...], out_v[part, :])
        dz_v[:, part] = (slope_v[:, part] * back).astype(BF16)
        copies.store(dz_v.at[:, part], dz.at[:, part])
    for part, load in zip(model_parts, seconds):
        load.wait()
        share_v[:, part] = nt(dz_v[...], in_v[part, :]).astype(BF16)
        copies.store(share_v.at[:, part], share.at[:, part])
    if slot is not None:
        for load in extra:
            load.wait()
        paired = gx_v[...] * nt(dz_v[...], dz_v[...]) + gh_v[...] * nt(g_v[...], g_v[...])
        total = sums_v[...] + masked_sums(slot, lengths, paired)
        high = total.astype(BF16)
        rest = total - high.astype(F32)
        middle = rest.astype(BF16)
        low = (rest - middle.astype(F32)).astype(BF16)
        lane = lax.broadcasted_iota(jnp.int32, (1, LANES), 1)
        line = jnp.zeros((1, LANES), F32)
        for place, piece in enumerate((high, middle, low)):
            line = line + pltpu.roll(piece.astype(F32), place * SPACING, 1)
        tokens = share_v.shape[0]
        share_v[:, D:] = jnp.broadcast_to(line, (tokens, LANES)).astype(BF16)
        copies.store(share_v.at[:, D:], share.at[:, D:])
    copies.finish()


SPACING = 32


def shadow_kernel(
    g_col, slot, lengths, index, x, hidden, grads, dz, x_t, hidden_t, sums,
    x_v, hidden_v, g_v, dz_v, xt_v, ht_v, sums_v, sems,
):
    copies = Copies(sems)
    pairs = (
        (picked(slot, index, x), x_v),
        (hidden, hidden_v),
        (grads.at[:, g_col : g_col + D], g_v),
        (dz, dz_v),
    )
    for load in [copies.start(a, b) for a, b in pairs]:
        load.wait()
    xt_v[...] = x_v[...].T
    copies.store(xt_v, x_t)
    ht_v[...] = hidden_v[...].T
    copies.store(ht_v, hidden_t)
    paired = nt(x_v[...], x_v[...]) * nt(dz_v[...], dz_v[...])
    paired = paired + nt(hidden_v[...], hidden_v[...]) * nt(g_v[...], g_v[...])
    sums_v[...] = masked_sums(slot, lengths, paired)
    copies.store(sums_v, sums)
    copies.finish()


def grams_kernel(
    place, index, x, hidden, x_t, hidden_t, gram_x, gram_h, x_v, hidden_v, xt_v, ht_v, gx_v, gh_v, sems
):
    copies = Copies(sems)
    for load in [copies.start(picked(place, index, x), x_v), copies.start(hidden, hidden_v)]:
        load.wait()
    xt_v[...] = x_v[...].T
    copies.store(xt_v, x_t)
    ht_v[...] = hidden_v[...].T
    copies.store(ht_v, hidden_t)
    gx_v[...] = nt(x_v[...], x_v[...])
    copies.store(gx_v, gram_x)
    gh_v[...] = nt(hidden_v[...], hidden_v[...])
    copies.store(gh_v, gram_h)
    copies.finish()


def sum_kernel(arrived_ref, incoming_ref, *out_refs):
    total = jnp.sum(arrived_ref[:, :, :D].astype(F32), axis=0)
    out_refs[0][...] = (incoming_ref[...].astype(F32) + total).astype(BF16)
    if len(out_refs) > 1:
        line = jnp.sum(arrived_ref[:, 0:1, D:].astype(F32), axis=0)
        back = [pltpu.roll(line, LANES - place * SPACING, 1) for place in (1, 2)]
        out_refs[1][...] = line + (back[0] + back[1])


def add_up(arrived, incoming, with_sums):
    outs = [shape(*incoming.shape)] + ([shape(1, LANES, dtype=F32)] if with_sums else [])
    whole = pl.BlockSpec(memory_space=pltpu.VMEM)
    return pl.pallas_call(
        sum_kernel,
        out_shape=outs,
        in_specs=[whole] * 2,
        out_specs=[whole] * len(outs),
        name="add_up",
        compiler_params=pltpu.CompilerParams(vmem_limit_bytes=60 * MIB),
        cost_estimate=pl.CostEstimate(flops=arrived.size, bytes_accessed=MIB, transcendentals=0),
    )(arrived, incoming)


def final_kernel(slots, lengths_ref, totals_ref, *refs):
    x_t, hidden_t, dz, dy = (refs[i * slots : (i + 1) * slots] for i in range(4))
    grad_in_ref, grad_out_ref, dzc_ref, dyc_ref = refs[4 * slots :]

    @pl.when(pl.program_id(0) == 0)
    def _():
        factor = 1.0 / (jnp.sqrt(totals_ref[...] / (D * FF)) + GAMMA)
        for slot in range(slots):
            tokens = dz[slot].shape[0]
            row = lax.broadcasted_iota(jnp.int32, (tokens, 1), 0) < lengths_ref[0, 2 * slot]
            scale = jnp.where(
                row,
                factor[:, 2 * slot : 2 * slot + 1],
                factor[:, 2 * slot + 1 : 2 * slot + 2],
            )
            rows = slice(slot * tokens, (slot + 1) * tokens)
            dzc_ref[rows, :] = (dz[slot][...].astype(F32) * scale).astype(BF16)
            dyc_ref[rows, :] = (dy[slot][...].astype(F32) * scale).astype(BF16)

    for left, right_ref, out_ref in ((x_t, dzc_ref, grad_in_ref), (hidden_t, dyc_ref, grad_out_ref)):
        lhs = jnp.concatenate([part[...] for part in left], axis=1)
        for cols in parts(right_ref.shape[1]):
            out_ref[:, cols] = mm(lhs, right_ref[:, cols]).astype(BF16)


def final_products(lengths, totals, x_t, hidden_t, dz, dy):
    slots = len(dz)
    rows, tokens = x_t[0].shape
    width = dz[0].shape[1]
    block = 256
    strip = pl.BlockSpec((block, tokens), lambda i: (i, 0))
    whole = pl.BlockSpec((tokens, width), lambda i: (0, 0), pipeline_mode=pl.Buffered(1))
    dy_specs = [
        pl.BlockSpec((tokens, D), lambda i, at=col // D: (0, at), pipeline_mode=pl.Buffered(1))
        for _, col in dy
    ]
    out = pl.BlockSpec((block, width), lambda i: (i, 0))
    return pl.pallas_call(
        lambda *refs: final_kernel(slots, *refs),
        grid=(rows // block,),
        out_shape=(shape(rows, width), shape(rows, width)),
        in_specs=[SMEM, pl.BlockSpec(totals.shape, lambda i: (0, 0))]
        + [strip] * (2 * slots)
        + [whole] * slots
        + dy_specs,
        out_specs=(out, out),
        scratch_shapes=[pltpu.VMEM((slots * tokens, width), BF16)] * 2,
        name="final",
        compiler_params=pltpu.CompilerParams(vmem_limit_bytes=60 * MIB),
        cost_estimate=pl.CostEstimate(
            flops=4 * rows * width * slots * tokens, bytes_accessed=10 * MIB, transcendentals=0
        ),
    )(lengths, totals, *x_t, *hidden_t, *dz, *[array for array, _ in dy])


def exchange(blocks):
    return lax.all_to_all(blocks, "tensor", split_axis=0, concat_axis=0, tiled=True)


def per_device(saved_inputs, slot_index, example_lengths, first_grads, loss_grads, w_in, w_out):
    sections, count = lax.axis_size("section"), lax.axis_size("tensor")
    is_last = (lax.axis_index("section") == sections - 1).astype(jnp.int32).reshape(1)
    first, second = w_in[0], w_out[0]
    slots = loss_grads.shape[0] + 1
    rows = first_grads.shape[1]
    tokens = count * rows
    units = first.shape[1]
    lengths = example_lengths.reshape(1, 2 * slots)
    incoming = first_grads[0]
    product = 2 * tokens * D * units
    wide = (tokens, D)

    later = lax.all_gather(saved_inputs[0], "tensor", axis=1, tiled=True)
    blocks = call(
        start_kernel,
        shape(count, rows, 2 * D),
        (slot_index, saved_inputs[0], incoming),
        [(saved_inputs.shape[1:], BF16), ((rows, 2 * D), BF16)],
        count + 2,
        0,
        "start",
        smem=1,
    )
    begun = exchange(blocks).reshape(tokens, 2 * D)
    inputs = [begun] + [later] * (slots - 1)
    grads = (begun, D)

    x_t, hidden_t, dzs, dys, results = [], [], [], [], []
    sums = jnp.zeros((1, LANES), F32)
    for slot in range(slots):
        final = slot + 1 == slots
        x = inputs[slot]
        g, g_col = grads
        slope, hidden = call(
            lambda *refs, slot=slot: forward_kernel(slot, *refs),
            (shape(tokens, units, dtype=F32), shape(tokens, units)),
            (slot_index, x, first),
            [(wide, BF16), (first.shape, BF16), ((tokens, units), F32), ((tokens, units), BF16)],
            1 + 3 * (units // STEP),
            product,
            "forward",
            smem=1,
        )
        flipped = (shape(D, tokens), shape(units, tokens))
        flipped_v = [((D, tokens), BF16), ((units, tokens), BF16)]
        square = (tokens, tokens)
        width = D + (LANES if final else 0)
        extra, extra_v = (), []
        if final:
            *turned, gram_x, gram_h = call(
                lambda *refs, slot=slot: grams_kernel(slot, *refs),
                flipped + (shape(*square, dtype=F32),) * 2,
                (slot_index, x, hidden),
                [(wide, BF16), ((tokens, units), BF16)] + flipped_v + [(square, F32)] * 2,
                6,
                product,
                "grams",
                smem=1,
            )
            extra, extra_v = (gram_x, gram_h, sums), [(square, F32)] * 2 + [((1, LANES), F32)]
        dz, share = call(
            lambda *refs, col=g_col, slot=slot if final else None: back_kernel(col, slot, *refs),
            (shape(tokens, units), shape(tokens, width)),
            (lengths, g, slope, second, first, *extra),
            [
                (wide, BF16),
                ((tokens, units), F32),
                (second.shape, BF16),
                (first.shape, BF16),
                ((tokens, units), BF16),
                ((tokens, width), BF16),
            ]
            + extra_v,
            1 + 3 * (units // STEP) + 2 * (D // STEP) + 4,
            2 * product,
            "back",
            smem=1,
        )
        arrived = exchange(share.reshape(count, rows, width))
        if not final:
            *turned, one = call(
                lambda *refs, col=g_col, slot=slot: shadow_kernel(col, slot, *refs),
                flipped + (shape(1, LANES, dtype=F32),),
                (lengths, slot_index, x, hidden, g, dz),
                [(wide, BF16), ((tokens, units), BF16), (wide, BF16), ((tokens, units), BF16)]
                + flipped_v
                + [((1, LANES), F32)],
                7,
                product,
                "shadow",
                smem=2,
            )
            sums = sums + one
        x_t.append(turned[0])
        hidden_t.append(turned[1])
        dzs.append(dz)
        dys.append(grads)
        passing, *totals = add_up(arrived, incoming, final)
        results.append(passing)
        if not final:
            shifted = lax.ppermute(
                passing, "section", [(source, source - 1) for source in range(1, sections)]
            )
            blocks, incoming = call(
                spread_kernel,
                (shape(count, rows, D), shape(rows, D)),
                (is_last, shifted, loss_grads[slot]),
                [((rows, D), BF16)] * 2,
                count + 3,
                0,
                "spread",
                smem=1,
            )
            grads = (exchange(blocks).reshape(tokens, D), 0)

    grad_in, grad_out = final_products(lengths, totals[0], x_t, hidden_t, dzs, dys)
    return grad_in[None], grad_out[None], jnp.stack(results)[None]


def solution(mesh):
    return jax.shard_map(
        per_device,
        mesh=mesh,
        in_specs=(
            P("section", None, "tensor", None),
            P("section", None),
            P("section", None, None),
            P("section", "tensor", None),
            P(None, "tensor", None),
            P("section", None, "tensor"),
            P("section", "tensor", None),
        ),
        out_specs=(
            P("section", None, "tensor"),
            P("section", "tensor", None),
            P("section", None, "tensor", None),
        ),
        check_vma=False,
    )
```

time: 237 us -> 235 us (level)
  Pallas kernels: 3.75 us -> 64.9 us
  blocking collectives: 22.2 us -> 74.7 us
  waiting for transfers between devices: 80.8 us -> 45.5 us
  matrix products: 28.8 us -> 0 us
  local copies, waits for them, and re-layouts: 30.8 us -> 5.19 us
  starting transfers between devices: 44.7 us -> 25.5 us
  other arithmetic: 16.3 us -> 2.58 us
  between operations: 7.02 us -> 14.2 us
    pallas_call x3 -> x16, Pallas kernels: 3.75 us -> 64.9 us  [the longest x12 51.4 us: call(): pl.pallas_call(kernel, out_shape=outs, in_specs=[SMEM] * smem + [ANY] * (...]
    all_to_all x1 -> x3, blocking collectives: 22.2 us -> 74.7 us  [exchange(): lax.all_to_all(blocks, 'tensor', split_axis=0, concat_axis=0, tiled=True)]
    all_to_all x7 -> x3, waiting for transfers between devices: 79.5 us -> 34.1 us  [exchange(): lax.all_to_all(blocks, 'tensor', split_axis=0, concat_axis=0, tiled=True)]
    dot_general x17 -> x0, matrix products: 28.8 us -> none  [the longest x3 7.95 us: per_device(): relu = jnp.maximum(jnp.dot(x, first, preferred_element_type=F32), 0.0)]
    all_to_all x7 -> x3, starting transfers between devices: 40.8 us -> 21.7 us  [exchange(): lax.all_to_all(blocks, 'tensor', split_axis=0, concat_axis=0, tiled=True)]
    unnamed x72 -> x21, local copies, waits for them, and re-layouts: 19.6 us -> 3.91 us
    all_gather x0 -> x1, waiting for transfers between devices: none -> 8.07 us  [per_device(): later = lax.all_gather(saved_inputs[0], 'tensor', axis=1, tiled=True)]
    slice x5 -> x0, local copies, waits for them, and re-layouts: 5.82 us -> none  [the longest x1 2.34 us: per_device(): later[:, D * i:D * (i + 1)]]
  transfers between devices with their start and end apart: 9 -> 6, of which waited for: 8 -> 6; matrix products, arithmetic and copies ran while one was open for 21% -> 1% of each run, Pallas kernels for 0% -> 15%
where the time goes in v2:
time: 235 us; the launch traced here: 233 us
  blocking collectives  74.7 us (32%)
  Pallas kernels  64.9 us (28%)
  waiting for transfers between devices  45.5 us (19%)
  starting transfers between devices  25.5 us (11%)
  between operations  14.2 us (6%)
  local copies, waits for them, and re-layouts  5.19 us (2%)
  other arithmetic  2.58 us (1%)
    all_to_all x3, blocking collectives, exchange(): lax.all_to_all(blocks, 'tensor', split_axis=0, concat_axis=0, tiled=True)  74.7 us
    pallas_call x12, Pallas kernels, call(): pl.pallas_call(kernel, out_shape=outs, in_specs=[SMEM] * smem + [ANY] * (...  51.4 us
    all_to_all x3, waiting for transfers between devices, exchange(): lax.all_to_all(blocks, 'tensor', split_axis=0, concat_axis=0, tiled=True)  34.1 us
    all_to_all x3, starting transfers between devices, exchange(): lax.all_to_all(blocks, 'tensor', split_axis=0, concat_axis=0, tiled=True)  21.7 us
    pallas_call x1, Pallas kernels, final_products(): pl.pallas_call(lambda *refs: final_kernel(slots, *refs), grid=(rows // bl...  8.19 us
    all_gather x1, waiting for transfers between devices, per_device(): later = lax.all_gather(saved_inputs[0], 'tensor', axis=1, tiled=True)  8.07 us
    pallas_call x3, Pallas kernels, add_up(): pl.pallas_call(sum_kernel, out_shape=outs, in_specs=[whole] * 2, out_spec...  5.25 us
  transfers between devices with their start and end apart: 6, of which 6 were waited for; matrix products, arithmetic and copies ran while one was open for 1% of the time, Pallas kernels for 15%

profile of v2, /device:TPU:8, one launch (start us, length us, event | category | flops | bytes accessed | tf_op | source)
XLA Modules:
  0.0 232.6 jit_solution(2729690168537572618)
XLA Ops:
  7.2 0.0 copy-start.8
  7.2 2.9 %start.1 = bf16[32,8,2048]{2,1,0:T(8,128)(2,1)} custom-call(s32[1,3]{1,0:T(1,128)} %refs_1_.3, bf16[4,8,1024]{2,1,0:T(8,128)(2,1)} %bitcast.49, bf16[8,1024]{1,0:T(8,128)(2,1)} %bitcast.50), custom_call_target="tpu_custom_call" | custom-call | bytes 4194304 | tf_op jit(solution)/shard_map/start/pallas_call | solution.py:26
  10.1 11.3 %all-to-all-start = ((bf16[32,8,2048]{2,1,0:T(8,128)(2,1)}), bf16[32,8,2048]{2,1,0:T(8,128)(2,1)S(1)}, u32[]{:S(2)}, u32[]{:S(2)}) async-start(bf16[32,8,2048]{2,1,0:T(8,128)(2,1)} %start.1), calls=%async_computation | async-start | bytes 2097152 | tf_op jit(solution)/shard_map/all_to_all | solution.py:301
  21.4 0.0 all-gather.3.cloned.1.call-start
  21.4 0.7 all-gather.3.cloned.1.call-update
  22.1 0.0 copy-done.8
  22.1 0.1 copy.11
  22.2 0.7 reshape.32.refs_0_
  22.9 27.4 %all-to-all-done = bf16[32,8,2048]{2,1,0:T(8,128)(2,1)S(1)} async-done(((bf16[32,8,2048]{2,1,0:T(8,128)(2,1)}), bf16[32,8,2048]{2,1,0:T(8,128)(2,1)S(1)}, u32[]{:S(2)}, u32[]{:S(2)}) %all-to-all-start) | async-done | bytes 1048608 | tf_op jit(solution)/shard_map/all_to_all | solution.py:301
  50.3 1.0 copy-done
  51.3 4.4 %forward.3 = (f32[256,1024]{1,0:T(8,128)}, bf16[256,1024]{1,0:T(8,128)(2,1)}) custom-call(s32[1,3]{1,0:T(1,128)} %refs_1_.3, bf16[256,2048]{1,0:T(8,128)(2,1)} %bitcast.33, bf16[1024,1024]{1,0:T(8,128)(2,1)} %bitcast.23), custom_call_target="tpu_custom_call" | custom-call | flops 536870912 | bytes 4194304 | tf_op jit(solution)/shard_map/forward/pallas_call | solution.py:26
  55.8 0.0 copy-start.5
  55.8 6.6 %back.3 = (bf16[256,1024]{1,0:T(8,128)(2,1)}, bf16[256,1024]{1,0:T(8,128)(2,1)}) custom-call(s32[1,6]{1,0:T(1,128)} %reshape.32.refs_0_, bf16[256,2048]{1,0:T(8,128)(2,1)} %bitcast.34, f32[256,1024]{1,0:T(8,128)} %get-tuple-element.33.refs_2_, bf16[1024,1024]{1,0:T(8,128)(2,1)} %bitcast.38, bf16[1024,1024]{1,0:T(8,128)(2,1)} %bitcast.24), custom_call_target="tpu_custom_call" | custom-call | flops 1073741824 | bytes 4194304 | tf_op jit(solution)/shard_map/back/pallas_call | solution.py:26
  62.4 23.0 %all_to_all.30.arrived_ref = bf16[32,8,1024]{2,1,0:T(8,128)(2,1)} all-to-all(bf16[32,8,1024]{2,1,0:T(8,128)(2,1)} %bitcast.47), channel_id=1, replica_groups=mesh['section'=8,'tensor'=32] {'tensor'}, dimensions={0} | all-to-all | bytes 1048576 | tf_op jit(solution)/shard_map/all_to_all | solution.py:301
  85.4 1.7 add_up.3
  87.2 1.9 collective-permute-start
  89.1 0.0 copy-done.5
  89.1 0.6 slice_bitcast_fusion
  89.7 1.0 collective-permute-done.shifted
  90.7 0.6 copy-done.6
  91.3 1.8 spread.2
  93.2 4.9 %all-to-all-start.2 = ((bf16[32,8,1024]{2,1,0:T(8,128)(2,1)}), bf16[32,8,1024]{2,1,0:T(8,128)(2,1)S(1)}, u32[]{:S(2)}, u32[]{:S(2)}) async-start(bf16[32,8,1024]{2,1,0:T(8,128)(2,1)} %get-tuple-element.35), calls=%async_computation.2 | async-start | bytes 1048576 | tf_op jit(solution)/shard_map/all_to_all | solution.py:301
  98.1 8.1 %all-gather.3.cloned.1.call-done = bf16[1,4,256,1024]{3,2,1,0:T(8,128)(2,1)} async-done(((bf16[1,4,8,1024]{3,2,1,0:T(8,128)(2,1)}), bf16[1,4,256,1024]{3,2,1,0:T(8,128)(2,1)}) %all-gather.3.cloned.1.call-update) | async-done | bytes 2097168 | tf_op jit(solution)/shard_map/all_gather | solution.py:317
  106.2 4.4 %forward.4 = (f32[256,1024]{1,0:T(8,128)}, bf16[256,1024]{1,0:T(8,128)(2,1)}) custom-call(s32[1,3]{1,0:T(1,128)} %refs_1_.3, bf16[4,256,1024]{2,1,0:T(8,128)(2,1)} %bitcast.29, bf16[1024,1024]{1,0:T(8,128)(2,1)} %bitcast.25), custom_call_target="tpu_custom_call" | custom-call | flops 536870912 | bytes 4194304 | tf_op jit(solution)/shard_map/forward/pallas_call | solution.py:26
  110.6 5.5 %all-to-all-done.2 = bf16[32,8,1024]{2,1,0:T(8,128)(2,1)S(1)} async-done(((bf16[32,8,1024]{2,1,0:T(8,128)(2,1)}), bf16[32,8,1024]{2,1,0:T(8,128)(2,1)S(1)}, u32[]{:S(2)}, u32[]{:S(2)}) %all-to-all-start.2) | async-done | bytes 524320 | tf_op jit(solution)/shard_map/all_to_all | solution.py:301
  116.1 0.8 copy-done.1
  116.9 6.5 %back.4 = (bf16[256,1024]{1,0:T(8,128)(2,1)}, bf16[256,1024]{1,0:T(8,128)(2,1)}) custom-call(s32[1,6]{1,0:T(1,128)} %reshape.32.refs_0_, bf16[256,1024]{1,0:T(8,128)(2,1)} %bitcast.41, f32[256,1024]{1,0:T(8,128)} %get-tuple-element.36.refs_2_, bf16[1024,1024]{1,0:T(8,128)(2,1)} %bitcast.39, bf16[1024,1024]{1,0:T(8,128)(2,1)} %bitcast.26), custom_call_target="tpu_custom_call" | custom-call | flops 1073741824 | bytes 4194304 | tf_op jit(solution)/shard_map/back/pallas_call | solution.py:26
  123.4 23.4 %all_to_all.31.arrived_ref = bf16[32,8,1024]{2,1,0:T(8,128)(2,1)} all-to-all(bf16[32,8,1024]{2,1,0:T(8,128)(2,1)} %bitcast.48), channel_id=1, replica_groups=mesh['section'=8,'tensor'=32] {'tensor'}, dimensions={0} | all-to-all | bytes 1048576 | tf_op jit(solution)/shard_map/all_to_all | solution.py:301
  146.8 1.7 add_up.4
  148.6 1.9 collective-permute-start.1
  150.5 1.6 collective-permute-done.1.shifted
  152.1 0.6 copy-done.7
  152.7 1.9 spread.3
  154.6 5.4 %all-to-all-start.4 = ((bf16[32,8,1024]{2,1,0:T(8,128)(2,1)}), bf16[32,8,1024]{2,1,0:T(8,128)(2,1)S(1)}, u32[]{:S(2)}, u32[]{:S(2)}) async-start(bf16[32,8,1024]{2,1,0:T(8,128)(2,1)} %get-tuple-element.39), calls=%async_computation.4 | async-start | bytes 1048576 | tf_op jit(solution)/shard_map/all_to_all | solution.py:301
  160.1 3.9 %shadow.2 = (bf16[1024,256]{1,0:T(8,128)(2,1)}, bf16[1024,256]{1,0:T(8,128)(2,1)}, f32[1,128]{1,0:T(1,128)}) custom-call(s32[1,6]{1,0:T(1,128)} %reshape.32.refs_0_, s32[1,3]{1,0:T(1,128)} %refs_1_.3, bf16[256,2048]{1,0:T(8,128)(2,1)} %bitcast.35, bf16[256,1024]{1,0:T(8,128)(2,1)} %get-tuple-element.44.refs_3_, bf16[256,2048]{1,0:T(8,128)(2,1)} %bitcast.36, ...), custom_call_target="tpu_custom_call" | custom-call | flops 536870912 | bytes 4194304 | tf_op jit(solution)/shard_map/shadow/pallas_call | solution.py:26
  164.0 4.4 %forward.5 = (f32[256,1024]{1,0:T(8,128)}, bf16[256,1024]{1,0:T(8,128)(2,1)}) custom-call(s32[1,3]{1,0:T(1,128)} %refs_1_.3, bf16[4,256,1024]{2,1,0:T(8,128)(2,1)} %bitcast.30, bf16[1024,1024]{1,0:T(8,128)(2,1)} %bitcast.27), custom_call_target="tpu_custom_call" | custom-call | flops 536870912 | bytes 4194304 | tf_op jit(solution)/shard_map/forward/pallas_call | solution.py:26
  168.4 3.3 %grams.1 = (bf16[1024,256]{1,0:T(8,128)(2,1)}, bf16[1024,256]{1,0:T(8,128)(2,1)}, f32[256,256]{1,0:T(8,128)}, f32[256,256]{1,0:T(8,128)}) custom-call(s32[1,3]{1,0:T(1,128)} %refs_1_.3, bf16[4,256,1024]{2,1,0:T(8,128)(2,1)} %bitcast.31, bf16[256,1024]{1,0:T(8,128)(2,1)} %get-tuple-element.41.refs_2_), custom_call_target="tpu_custom_call" | custom-call | flops 536870912 | bytes 4194304 | tf_op jit(solution)/shard_map/grams/pallas_call | solution.py:26
  171.8 0.0 copy-start.9
  171.8 4.0 %shadow.3 = (bf16[1024,256]{1,0:T(8,128)(2,1)}, bf16[1024,256]{1,0:T(8,128)(2,1)}, f32[1,128]{1,0:T(1,128)}) custom-call(s32[1,6]{1,0:T(1,128)} %reshape.32.refs_0_, s32[1,3]{1,0:T(1,128)} %refs_1_.3, bf16[4,256,1024]{2,1,0:T(8,128)(2,1)} %bitcast.32, bf16[256,1024]{1,0:T(8,128)(2,1)} %get-tuple-element.47.refs_3_, bf16[256,1024]{1,0:T(8,128)(2,1)} %bitcast.42, ...), custom_call_target="tpu_custom_call" | custom-call | flops 536870912 | bytes 4194304 | tf_op jit(solution)/shard_map/shadow/pallas_call | solution.py:26
  175.8 1.2 add.3.refs_7_
  177.0 1.2 all-to-all-done.4
  178.2 0.8 copy-done.2
  179.0 7.2 %back.5 = (bf16[256,1024]{1,0:T(8,128)(2,1)}, bf16[256,1152]{1,0:T(8,128)(2,1)}) custom-call(s32[1,6]{1,0:T(1,128)} %reshape.32.refs_0_, bf16[256,1024]{1,0:T(8,128)(2,1)} %bitcast.44, f32[256,1024]{1,0:T(8,128)} %get-tuple-element.40.refs_2_, bf16[1024,1024]{1,0:T(8,128)(2,1)} %bitcast.40, bf16[1024,1024]{1,0:T(8,128)(2,1)} %bitcast.28, ...), custom_call_target="tpu_custom_call" | custom-call | flops 1073741824 | bytes 4194304 | tf_op jit(solution)/shard_map/back/pallas_call | solution.py:26
  186.2 28.2 %all_to_all.32.arrived_ref = bf16[32,8,1152]{2,1,0:T(8,128)(2,1)} all-to-all(bf16[32,8,1152]{2,1,0:T(8,128)(2,1)} %bitcast.46), channel_id=1, replica_groups=mesh['section'=8,'tensor'=32] {'tensor'}, dimensions={0} | all-to-all | bytes 1179648 | tf_op jit(solution)/shard_map/all_to_all | solution.py:301
  214.4 1.8 add_up.5
  216.2 0.0 copy-done.4
  216.2 1.3 maximum_bitcast_fusion
  217.6 8.2 %final.1 = (bf16[1024,1024]{1,0:T(8,128)(2,1)}, bf16[1024,1024]{1,0:T(8,128)(2,1)}) custom-call(s32[1,6]{1,0:T(1,128)} %reshape.32.refs_0_, f32[1,128]{1,0:T(1,128)} %get-tuple-element.52.refs_1_, bf16[1024,256]{1,0:T(8,128)(2,1)} %get-tuple-element.53.refs_2_, bf16[1024,256]{1,0:T(8,128)(2,1)} %get-tuple-element.54.refs_3_, ...), custom_call_target="tpu_custom_call" | custom-call | flops 3221225472 | bytes 10485760 | tf_op jit(solution)/shard_map/final/pallas_call | solution.py:282
  (9 shorter events, 0.0 us)
Async XLA Ops:
  7.2 15.0 %copy-start.8 = (s32[1,3,2]{1,2,0:T(2,128)S(1)}, s32[1,3,2]{1,2,0:T(2,128)}, u32[]{:S(2)}) copy-start(s32[1,3,2]{1,2,0:T(2,128)} %param.9) | copy-start | bytes 76
  10.1 40.3 %all-to-all-start = ((bf16[32,8,2048]{2,1,0:T(8,128)(2,1)}), bf16[32,8,2048]{2,1,0:T(8,128)(2,1)S(1)}, u32[]{:S(2)}, u32[]{:S(2)}) async-start(bf16[32,8,2048]{2,1,0:T(8,128)(2,1)} %start.1), calls=%async_computation | async-start | bytes 2097152 | tf_op jit(solution)/shard_map/all_to_all | solution.py:301
  21.4 84.8 %all-gather.3.cloned.1.call-start = ((), (), s32[]{:S(2)}) async-start(), calls=%async_computation.6 | async-start | bytes 2162688 | tf_op jit(solution)/shard_map/all_gather | solution.py:317
  50.3 1.0 copy-start
  55.8 33.3 %copy-start.5 = (bf16[2,8,1024]{2,1,0:T(8,128)(2,1)S(1)}, bf16[2,8,1024]{2,1,0:T(8,128)(2,1)}, u32[]{:S(2)}) copy-start(bf16[2,8,1024]{2,1,0:T(8,128)(2,1)} %param.11) | copy-start | bytes 98308
  87.2 3.5 %collective-permute-start = (bf16[8,1024]{1,0:T(8,128)(2,1)}, bf16[8,1024]{1,0:T(8,128)(2,1)S(1)}, u32[]{:S(2)}, u32[]{:S(2)}) collective-permute-start(bf16[8,1024]{1,0:T(8,128)(2,1)} %add_up.3), channel_id=1, source_target_pairs={{32,0},{64,32},{96,64},{128,96},{160,128},{192,160},{224,192},{33,... | collective-permute-start | bytes 49160 | tf_op jit(solution)/shard_map/ppermute | solution.py:405
  90.7 0.6 copy-start.6
  93.2 22.9 %all-to-all-start.2 = ((bf16[32,8,1024]{2,1,0:T(8,128)(2,1)}), bf16[32,8,1024]{2,1,0:T(8,128)(2,1)S(1)}, u32[]{:S(2)}, u32[]{:S(2)}) async-start(bf16[32,8,1024]{2,1,0:T(8,128)(2,1)} %get-tuple-element.35), calls=%async_computation.2 | async-start | bytes 1048576 | tf_op jit(solution)/shard_map/all_to_all | solution.py:301
  116.1 0.8 copy-start.1
  148.6 3.5 %collective-permute-start.1 = (bf16[8,1024]{1,0:T(8,128)(2,1)}, bf16[8,1024]{1,0:T(8,128)(2,1)S(1)}, u32[]{:S(2)}, u32[]{:S(2)}) collective-permute-start(bf16[8,1024]{1,0:T(8,128)(2,1)} %add_up.4), channel_id=1, source_target_pairs={{32,0},{64,32},{96,64},{128,96},{160,128},{192,160},{224,192},{33,... | collective-permute-start | bytes 49160 | tf_op jit(solution)/shard_map/ppermute | solution.py:405
  152.1 0.6 copy-start.7
  154.6 23.5 %all-to-all-start.4 = ((bf16[32,8,1024]{2,1,0:T(8,128)(2,1)}), bf16[32,8,1024]{2,1,0:T(8,128)(2,1)S(1)}, u32[]{:S(2)}, u32[]{:S(2)}) async-start(bf16[32,8,1024]{2,1,0:T(8,128)(2,1)} %get-tuple-element.39), calls=%async_computation.4 | async-start | bytes 1048576 | tf_op jit(solution)/shard_map/all_to_all | solution.py:301
  171.8 4.0 %copy-start.9 = (f32[1,128]{1,0:T(1,128)S(1)}, f32[1,128]{1,0:T(1,128)}, u32[]{:S(2)}) copy-start(f32[1,128]{1,0:T(1,128)} %get-tuple-element.46) | copy-start | bytes 1540
  178.1 0.8 copy-start.2
  179.0 37.3 %copy-start.3 = (bf16[8,1024]{1,0:T(8,128)(2,1)S(1)}, bf16[8,1024]{1,0:T(8,128)(2,1)}, u32[]{:S(2)}) copy-start(bf16[8,1024]{1,0:T(8,128)(2,1)} %add_up.3) | copy-start | bytes 49156
  179.0 37.3 %copy-start.4 = (bf16[8,1024]{1,0:T(8,128)(2,1)S(1)}, bf16[8,1024]{1,0:T(8,128)(2,1)}, u32[]{:S(2)}) copy-start(bf16[8,1024]{1,0:T(8,128)(2,1)} %add_up.4) | copy-start | bytes 49156
Sparse Core Ops, SparseCore 0:
  24.8 81.2 all-gather.2

commit v3 on v1

v3 whole, which is shorter than its diff:
```python
import jax
import jax.numpy as jnp
from jax import lax
from jax.experimental import pallas as pl
from jax.experimental.pallas import tpu as pltpu
from jax.sharding import PartitionSpec as P

D = 1024
FF = 32768
GAMMA = 0.01
F32 = jnp.float32
BF16 = jnp.bfloat16
MIB = 1 << 20
STEP = 256
LANES = 128
SPACING = 32

VMEM = pl.BlockSpec(memory_space=pltpu.VMEM)


def shape(*dims, dtype=BF16):
    return jax.ShapeDtypeStruct(dims, dtype)


def call(kernel, outs, operands, flops, name):
    return pl.pallas_call(
        kernel,
        out_shape=outs,
        in_specs=[VMEM] * len(operands),
        out_specs=jax.tree.map(lambda _: VMEM, outs),
        name=name,
        compiler_params=pltpu.CompilerParams(vmem_limit_bytes=8 * MIB),
        cost_estimate=pl.CostEstimate(flops=flops, bytes_accessed=MIB, transcendentals=0),
    )(*operands)


def parts(extent):
    return [slice(at, at + STEP) for at in range(0, extent, STEP)]


def nt(a, b):
    return lax.dot_general(a, b, (((1,), (1,)), ((), ())), preferred_element_type=F32)


def tn(a, b):
    return lax.dot_general(a, b, (((0,), (0,)), ((), ())), preferred_element_type=F32)


def mm(a, b):
    return jnp.dot(a, b, preferred_element_type=F32)


def start_kernel(index_ref, saved_ref, grads_ref, blocks_ref, *later_refs):
    count, rows, _ = blocks_ref.shape
    for slot in range(len(later_refs) + 1):
        wanted = index_ref[:, slot : slot + 1]
        x = saved_ref[0]
        for place in range(1, saved_ref.shape[0]):
            x = jnp.where(wanted == place, saved_ref[place], x)
        if slot:
            later_refs[slot - 1][...] = x
        else:
            blocks_ref[:, :, :D] = jnp.broadcast_to(x[None], (count, rows, D))
    blocks_ref[:, :, D:] = jnp.broadcast_to(grads_ref[...][None], (count, rows, D))


def spread_kernel(sections, place, shifted_ref, loss_ref, blocks_ref, rows_ref):
    last = (lax.axis_index("section") == sections - 1).astype(jnp.int32)
    chosen = jnp.where(jnp.full(rows_ref.shape, last) > 0, loss_ref[place], shifted_ref[...])
    rows_ref[...] = chosen
    blocks_ref[...] = jnp.broadcast_to(chosen[None], blocks_ref.shape)


def forward_kernel(x_ref, weights_ref, slope_ref, hidden_ref):
    x = x_ref[:, :, -D:].reshape(-1, D) if len(x_ref.shape) == 3 else x_ref[...]
    for cols in parts(weights_ref.shape[1]):
        relu = jnp.maximum(mm(x, weights_ref[:, cols]), 0.0)
        slope_ref[:, cols] = 2.0 * relu
        hidden_ref[:, cols] = (relu * relu).astype(BF16)


def masked_sums(slot, lengths_ref, paired):
    cut = lengths_ref[0:1, slot : slot + 1]
    tokens = paired.shape[0]
    row = lax.broadcasted_iota(jnp.int32, (tokens, tokens), 0) < cut
    col = lax.broadcasted_iota(jnp.int32, (tokens, tokens), 1) < cut
    before = jnp.sum(jnp.where(row & col, paired, 0.0), axis=(0, 1), keepdims=True)
    after = jnp.sum(jnp.where(row | col, 0.0, paired), axis=(0, 1), keepdims=True)
    lane = lax.broadcasted_iota(jnp.int32, (1, LANES), 1)
    return jnp.where(lane == 2 * slot, before, jnp.where(lane == 2 * slot + 1, after, 0.0))


def back_products(grads, slope_ref, w_out_ref, w_in_ref, dz_ref, share_ref):
    for part in parts(w_out_ref.shape[0]):
        back = nt(grads, w_out_ref[part, :])
        dz_ref[:, part] = (slope_ref[:, part] * back).astype(BF16)
    dz = dz_ref[...]
    for part in parts(w_in_ref.shape[0]):
        share_ref[:, part] = nt(dz, w_in_ref[part, :]).astype(BF16)
    return dz


def back_kernel(grads_ref, slope_ref, w_out_ref, w_in_ref, riding_ref, dz_ref, share_ref):
    back_products(grads_ref[...], slope_ref, w_out_ref, w_in_ref, dz_ref, share_ref)
    copies = share_ref.shape[0] // riding_ref.shape[0]
    share_ref[:, D:] = jnp.concatenate([riding_ref[...]] * copies, axis=0)


def last_back_kernel(
    slot, lengths_ref, grads_ref, slope_ref, w_out_ref, w_in_ref, gram_x_ref, gram_h_ref, *refs
):
    *sums_refs, dz_ref, share_ref = refs
    grads = grads_ref[...]
    dz = back_products(grads, slope_ref, w_out_ref, w_in_ref, dz_ref, share_ref)
    paired = gram_x_ref[...] * nt(dz, dz) + gram_h_ref[...] * nt(grads, grads)
    total = masked_sums(slot, lengths_ref, paired)
    for sums_ref in sums_refs:
        total = total + sums_ref[...]
    high = total.astype(BF16)
    rest = total - high.astype(F32)
    middle = rest.astype(BF16)
    low = (rest - middle.astype(F32)).astype(BF16)
    line = high.astype(F32)
    for place, piece in ((1, middle), (2, low)):
        line = line + pltpu.roll(piece.astype(F32), place * SPACING, 1)
    share_ref[:, D:] = jnp.broadcast_to(line, (share_ref.shape[0], LANES)).astype(BF16)


def squares_kernel(slot, lengths_ref, x_ref, hidden_ref, grads_ref, dz_ref, sums_ref):
    x, hidden, grads, dz = x_ref[...], hidden_ref[...], grads_ref[...], dz_ref[...]
    paired = nt(x, x) * nt(dz, dz) + nt(hidden, hidden) * nt(grads, grads)
    sums_ref[...] = masked_sums(slot, lengths_ref, paired)


def grams_kernel(x_ref, hidden_ref, gram_x_ref, gram_h_ref):
    x, hidden = x_ref[...], hidden_ref[...]
    gram_x_ref[...] = nt(x, x)
    gram_h_ref[...] = nt(hidden, hidden)


def sum_kernel(arrived_ref, incoming_ref, passing_ref, x_ref):
    total = incoming_ref[...].astype(F32)
    for peer in range(arrived_ref.shape[0]):
        total = total + arrived_ref[peer, :, :D].astype(F32)
    passing_ref[...] = total.astype(BF16)
    x_ref[...] = arrived_ref[:, :, D:].reshape(x_ref.shape)


def last_sum_kernel(arrived_ref, incoming_ref, *refs):
    *earlier_refs, results_ref, line_ref = refs
    total = incoming_ref[...].astype(F32)
    line = jnp.zeros(line_ref.shape, F32)
    for peer in range(arrived_ref.shape[0]):
        total = total + arrived_ref[peer, :, :D].astype(F32)
        line = line + arrived_ref[peer, 0:1, D:].astype(F32)
    for place, earlier_ref in enumerate(earlier_refs):
        results_ref[place] = earlier_ref[...]
    results_ref[len(earlier_refs)] = total.astype(BF16)
    pieces = [pltpu.roll(line, LANES - place * SPACING, 1) for place in (1, 2)]
    line_ref[...] = line + (pieces[0] + pieces[1])


def final_kernel(slots, lengths_ref, totals_ref, *refs):
    x, hidden, dz, dy = (refs[i * slots : (i + 1) * slots] for i in range(4))
    grad_in_ref, grad_out_ref, dzc_ref, dyc_ref = refs[4 * slots :]
    tokens = dz[0].shape[0]
    step = pl.program_id(0)

    @pl.when(step == 0)
    def _():
        factor = 1.0 / (jnp.sqrt(totals_ref[...] / (D * FF)) + GAMMA)
        for slot in range(slots):
            cut = lengths_ref[0:1, slot : slot + 1]
            row = lax.broadcasted_iota(jnp.int32, (tokens, 1), 0) < cut
            scale = jnp.where(
                row,
                factor[:, 2 * slot : 2 * slot + 1],
                factor[:, 2 * slot + 1 : 2 * slot + 2],
            )
            rows = slice(slot * tokens, (slot + 1) * tokens)
            dzc_ref[rows, :] = (dz[slot][...].astype(F32) * scale).astype(BF16)
            dyc_ref[rows, :] = (dy[slot][...].astype(F32) * scale).astype(BF16)

    block = grad_in_ref.shape[0]
    strip = pl.ds(pl.multiple_of(step * block, block), block)
    for left, right_ref, out_ref in ((x, dzc_ref, grad_in_ref), (hidden, dyc_ref, grad_out_ref)):
        for cols in parts(right_ref.shape[1]):
            total = tn(left[0][:, strip], right_ref[:tokens, cols])
            for slot in range(1, slots):
                rows = slice(slot * tokens, (slot + 1) * tokens)
                total = total + tn(left[slot][:, strip], right_ref[rows, cols])
            out_ref[:, cols] = total.astype(BF16)


def final_products(lengths, totals, x, hidden, dz, dy):
    slots = len(dz)
    tokens, width = dz[0].shape
    rows = x[0].shape[1]
    block = 256
    out = pl.BlockSpec((block, width), lambda i: (i, 0))
    return pl.pallas_call(
        lambda *refs: final_kernel(slots, *refs),
        grid=(rows // block,),
        out_shape=(shape(rows, width), shape(rows, width)),
        in_specs=[VMEM] * (2 + 4 * slots),
        out_specs=(out, out),
        scratch_shapes=[pltpu.VMEM((slots * tokens, width), BF16)] * 2,
        name="final",
        compiler_params=pltpu.CompilerParams(vmem_limit_bytes=12 * MIB),
        cost_estimate=pl.CostEstimate(
            flops=4 * rows * width * slots * tokens, bytes_accessed=4 * MIB, transcendentals=0
        ),
    )(lengths, totals, *x, *hidden, *dz, *dy)


def exchange(blocks):
    return lax.all_to_all(blocks, "tensor", split_axis=0, concat_axis=0, tiled=True)


def split_kernel(begun_ref, x_ref, grads_ref):
    x_ref[...] = begun_ref[:, :, :D].reshape(x_ref.shape)
    grads_ref[...] = begun_ref[:, :, D:].reshape(grads_ref.shape)


def per_device(saved_inputs, slot_index, example_lengths, first_grads, loss_grads, w_in, w_out):
    sections, count = lax.axis_size("section"), lax.axis_size("tensor")
    first, second = w_in[0], w_out[0]
    slots = loss_grads.shape[0] + 1
    rows = first_grads.shape[1]
    tokens = count * rows
    units = first.shape[1]
    lengths = example_lengths[0].T
    incoming = first_grads[0]
    product = 2 * tokens * D * units
    square = (tokens, tokens)

    blocks, *riding = call(
        start_kernel,
        (shape(count, rows, 2 * D),) + (shape(rows, D),) * (slots - 1),
        (slot_index, saved_inputs[0], incoming),
        0,
        "start",
    )
    begun = exchange(blocks)
    x, grads = call(split_kernel, (shape(tokens, D),) * 2, (begun,), 0, "split")

    def forward(x):
        outs = (shape(tokens, units, dtype=F32), shape(tokens, units))
        return call(forward_kernel, outs, (x, first), product, "forward")

    slope, hidden = forward(x)
    xs, hiddens, dzs, dys, results, squares = [], [], [], [], [], []
    for slot in range(slots):
        xs.append(x)
        hiddens.append(hidden)
        dys.append(grads)
        if slot + 1 == slots:
            break
        dz, share = call(
            back_kernel,
            (shape(tokens, units), shape(tokens, 2 * D)),
            (grads, slope, second, first, riding[slot]),
            2 * product,
            "back",
        )
        dzs.append(dz)
        arrived = exchange(share.reshape(count, rows, 2 * D))
        passing, next_x = call(
            sum_kernel,
            (shape(rows, D), shape(tokens, D)),
            (arrived, incoming),
            tokens * D,
            "add_up",
        )
        results.append(passing)
        shifted = lax.ppermute(
            passing, "section", [(source, source - 1) for source in range(1, sections)]
        )
        held = lax.optimization_barrier((passing, x, hidden, grads, dz))
        one = call(
            lambda *refs, slot=slot: squares_kernel(slot, *refs),
            shape(1, LANES, dtype=F32),
            (lengths, *held[1:]),
            product,
            "squares",
        )
        squares.append(one)
        x = next_x
        slope, hidden = forward(x)
        ready = [one, slope, hidden]
        if slot + 2 == slots:
            ready += call(
                grams_kernel, (shape(*square, dtype=F32),) * 2, (x, hidden), product // 4, "grams"
            )
        shifted, squares[-1], slope, hidden, *grams = lax.optimization_barrier((shifted, *ready))
        blocks, incoming = call(
            lambda *refs, slot=slot: spread_kernel(sections, slot, *refs),
            (shape(count, rows, D), shape(rows, D)),
            (shifted, loss_grads),
            0,
            "spread",
        )
        grads = exchange(blocks).reshape(tokens, D)

    dz, share = call(
        lambda *refs: last_back_kernel(slots - 1, *refs),
        (shape(tokens, units), shape(tokens, D + LANES)),
        (lengths, grads, slope, second, first, *grams, *squares),
        2 * product,
        "last_back",
    )
    dzs.append(dz)
    arrived = exchange(share.reshape(count, rows, D + LANES))
    results, totals = call(
        last_sum_kernel,
        (shape(slots, rows, D), shape(1, LANES, dtype=F32)),
        (arrived, incoming, *results),
        tokens * D,
        "last_add_up",
    )
    grad_in, grad_out = final_products(lengths, totals, xs, hiddens, dzs, dys)
    return grad_in[None], grad_out[None], results[None]


def solution(mesh):
    return jax.shard_map(
        per_device,
        mesh=mesh,
        in_specs=(
            P("section", None, "tensor", None),
            P("section", None),
            P("section", None, None),
            P("section", "tensor", None),
            P(None, "tensor", None),
            P("section", None, "tensor"),
            P("section", "tensor", None),
        ),
        out_specs=(
            P("section", None, "tensor"),
            P("section", "tensor", None),
            P("section", None, "tensor", None),
        ),
        check_vma=False,
    )
```

time: 237 us -> 200 us (0.84)
  blocking collectives: 22.2 us -> 176 us
  waiting for transfers between devices: 80.8 us -> 0.01 us
  starting transfers between devices: 44.7 us -> 3.83 us
  matrix products: 28.8 us -> 0 us
  local copies, waits for them, and re-layouts: 30.8 us -> 3.15 us
  other arithmetic: 16.3 us -> 0 us
  Pallas kernels: 3.75 us -> 15.7 us
  between operations: 7.02 us -> 0.81 us
    all_to_all x1 -> x6, blocking collectives: 22.2 us -> 176 us  [exchange(): lax.all_to_all(blocks, 'tensor', split_axis=0, concat_axis=0, tiled=True)]
    all_to_all x7 -> x0, waiting for transfers between devices: 79.5 us -> none  [the longest x5 67.1 us: spread(): lax.all_to_all(copies, 'tensor', split_axis=0, concat_axis=0, tiled=True)]
    all_to_all x7 -> x0, starting transfers between devices: 40.8 us -> none  [the longest x5 31.6 us: spread(): lax.all_to_all(copies, 'tensor', split_axis=0, concat_axis=0, tiled=True)]
    dot_general x17 -> x0, matrix products: 28.8 us -> none  [the longest x3 7.95 us: per_device(): relu = jnp.maximum(jnp.dot(x, first, preferred_element_type=F32), 0.0)]
    unnamed x72 -> x16, local copies, waits for them, and re-layouts: 19.6 us -> 3.15 us
    pallas_call x3 -> x17, Pallas kernels: 3.75 us -> 15.7 us  [the longest x16 9.96 us: call(): pl.pallas_call(kernel, out_shape=outs, in_specs=[VMEM] * len(operands), o...]
    slice x5 -> x0, local copies, waits for them, and re-layouts: 5.82 us -> none  [the longest x1 2.34 us: per_device(): later[:, D * i:D * (i + 1)]]
    select_n x4 -> x0, other arithmetic: 5.57 us -> none  [the longest x2 5.55 us: per_device(): jnp.where(position >= example_lengths[0, slot, 0], factor[slot, 1], facto...]
  transfers between devices with their start and end apart: 9 -> 2, of which waited for: 8 -> 0; matrix products, arithmetic and copies ran while one was open for 21% -> 0% of each run, Pallas kernels for 0% -> 2%
where the time goes in v3:
time: 200 us; the launch traced here: 199 us
  blocking collectives  176 us (88%)
  Pallas kernels  15.7 us (8%)
  starting transfers between devices  3.83 us (2%)
  local copies, waits for them, and re-layouts  3.15 us (2%)
    all_to_all x6, blocking collectives, exchange(): lax.all_to_all(blocks, 'tensor', split_axis=0, concat_axis=0, tiled=True)  176 us
    pallas_call x16, Pallas kernels, call(): pl.pallas_call(kernel, out_shape=outs, in_specs=[VMEM] * len(operands), o...  9.96 us
    pallas_call x1, Pallas kernels, final_products(): pl.pallas_call(lambda *refs: final_kernel(slots, *refs), grid=(rows // bl...  5.79 us
  transfers between devices with their start and end apart: 2, of which 0 were waited for; matrix products, arithmetic and copies ran while one was open for 0% of the time, Pallas kernels for 2%

profile of v3, /device:TPU:8, one launch (start us, length us, event | category | flops | bytes accessed | tf_op | source)
XLA Modules:
  0.0 199.1 jit_solution(17566884155325953134)
XLA Ops:
  0.6 0.0 copy-start
  0.6 0.0 copy-start.3
  0.7 0.9 copy-done.3
  1.5 0.0 copy-start.5
  1.5 0.8 copy-done.5
  2.3 0.0 copy-start.7
  2.4 0.7 copy-done.7
  3.0 0.1 start.1
  3.1 39.2 %all_to_all.30.begun_ref = bf16[32,8,2048]{2,1,0:T(8,128)(2,1)S(1)} all-to-all(bf16[32,8,2048]{2,1,0:T(8,128)(2,1)S(1)} %get-tuple-element.52), channel_id=1, replica_groups=mesh['section'=8,'tensor'=32] {'tensor'}, dimensions={0} | all-to-all | bytes 2097152 | tf_op jit(solution)/shard_map/all_to_all | solution.py:217
  42.3 0.0 copy-start.1
  42.3 0.1 split.1
  42.4 0.0 copy-done
  42.4 0.7 forward.3
  43.1 0.8 copy-done.1
  43.9 1.3 back.2
  45.2 0.0 copy-start.4
  45.2 32.3 %all_to_all.31.arrived_ref = bf16[32,8,2048]{2,1,0:T(8,128)(2,1)S(1)} all-to-all(bf16[32,8,2048]{2,1,0:T(8,128)(2,1)S(1)} %bitcast.29), channel_id=1, replica_groups=mesh['section'=8,'tensor'=32] {'tensor'}, dimensions={0} | all-to-all | bytes 2097152 | tf_op jit(solution)/shard_map/all_to_all | solution.py:217
  77.5 0.0 copy-done.4
  77.6 0.0 copy-start.6
  77.6 0.1 add_up.2
  77.6 1.9 collective-permute-start
  79.6 0.0 copy-start.2
  79.6 0.7 forward.4
  80.3 0.0 copy-done.6
  80.3 0.9 squares.2.refs_7_
  81.2 0.0 collective-permute-done.refs_0_
  81.2 0.0 copy-done.2
  81.3 23.6 %all_to_all.32 = bf16[32,8,1024]{2,1,0:T(8,128)(2,1)S(1)} all-to-all(bf16[32,8,1024]{2,1,0:T(8,128)(2,1)S(1)} %get-tuple-element.69), channel_id=1, replica_groups=mesh['section'=8,'tensor'=32] {'tensor'}, dimensions={0} | all-to-all | bytes 1048576 | tf_op jit(solution)/shard_map/all_to_all | solution.py:217
  104.9 1.3 back.3
  106.2 33.4 %all_to_all.33.arrived_ref = bf16[32,8,2048]{2,1,0:T(8,128)(2,1)S(1)} all-to-all(bf16[32,8,2048]{2,1,0:T(8,128)(2,1)S(1)} %bitcast.30), channel_id=1, replica_groups=mesh['section'=8,'tensor'=32] {'tensor'}, dimensions={0} | all-to-all | bytes 2097152 | tf_op jit(solution)/shard_map/all_to_all | solution.py:217
  139.6 0.1 add_up.3
  139.7 1.9 collective-permute-start.1
  141.6 0.7 forward.5
  142.4 0.9 squares.3.refs_8_
  143.3 0.5 grams.1
  143.7 0.0 collective-permute-done.1.refs_0_
  143.8 23.8 %all_to_all.34 = bf16[32,8,1024]{2,1,0:T(8,128)(2,1)S(1)} all-to-all(bf16[32,8,1024]{2,1,0:T(8,128)(2,1)S(1)} %get-tuple-element.87), channel_id=1, replica_groups=mesh['section'=8,'tensor'=32] {'tensor'}, dimensions={0} | all-to-all | bytes 1048576 | tf_op jit(solution)/shard_map/all_to_all | solution.py:217
  167.6 1.8 last_back.1
  169.4 23.2 %all_to_all.35.arrived_ref = bf16[32,8,1152]{2,1,0:T(8,128)(2,1)S(1)} all-to-all(bf16[32,8,1152]{2,1,0:T(8,128)(2,1)S(1)} %bitcast.31), channel_id=1, replica_groups=mesh['section'=8,'tensor'=32] {'tensor'}, dimensions={0} | all-to-all | bytes 1179648 | tf_op jit(solution)/shard_map/all_to_all | solution.py:217
  192.6 0.7 last_add_up.1
  193.3 5.8 %final.1 = (bf16[1024,1024]{1,0:T(8,128)(2,1)}, bf16[1024,1024]{1,0:T(8,128)(2,1)}) custom-call(s32[2,3]{1,0:T(2,128)S(1)} %bitcast.38, f32[1,128]{1,0:T(1,128)S(1)} %get-tuple-element.95.refs_1_, bf16[256,1024]{1,0:T(8,128)(2,1)S(1)} %get-tuple-element.61.x_ref.refs_1_.refs_2_, bf16[256,1024]{1,0:T(8,128)(2,1)S(1)} %get-tuple-element.77.x_ref.refs_1_.refs_3_, ...), custom_call_target="tpu_custom_call" | custom-call | flops 3221225472 | bytes 4194304 | tf_op jit(solution)/shard_map/final/pallas_call | solution.py:201
  (2 shorter events, 0.1 us)
Async XLA Ops:
  0.6 41.8 %copy-start = (bf16[1,1024,1024]{2,1,0:T(8,128)(2,1)S(1)}, bf16[1,1024,1024]{2,1,0:T(8,128)(2,1)}, u32[]{:S(2)}) copy-start(bf16[1,1024,1024]{2,1,0:T(8,128)(2,1)} %param.12) | copy-start | bytes 6291460
  0.6 0.9 copy-start.3
  1.5 0.8 copy-start.5
  2.3 0.7 copy-start.7
  42.3 1.6 copy-start.1
  45.2 32.3 %copy-start.4 = (bf16[1,8,1024]{2,1,0:T(8,128)(2,1)S(1)}, bf16[1,8,1024]{2,1,0:T(8,128)(2,1)}, u32[]{:S(2)}) copy-start(bf16[1,8,1024]{2,1,0:T(8,128)(2,1)} %param.10) | copy-start | bytes 49156
  77.6 2.8 %copy-start.6 = (s32[1,3,2]{1,2,0:T(2,128)S(1)}, s32[1,3,2]{1,2,0:T(2,128)}, u32[]{:S(2)}) copy-start(s32[1,3,2]{1,2,0:T(2,128)} %param.9) | copy-start | bytes 76
  77.6 3.6 %collective-permute-start = (bf16[8,1024]{1,0:T(8,128)(2,1)S(1)}, bf16[8,1024]{1,0:T(8,128)(2,1)S(1)}, u32[]{:S(2)}, u32[]{:S(2)}) collective-permute-start(bf16[8,1024]{1,0:T(8,128)(2,1)S(1)} %get-tuple-element.58.refs_0_), channel_id=1, source_target_pairs={{32,0},{64,32},{96,64},{128,96},{160,128},{192,160},{224,192},{33,... | collective-permute-start | bytes 49160 | tf_op jit(solution)/shard_map/ppermute | solution.py:276
  79.6 1.7 copy-start.2
  139.7 4.0 %collective-permute-start.1 = (bf16[8,1024]{1,0:T(8,128)(2,1)S(1)}, bf16[8,1024]{1,0:T(8,128)(2,1)S(1)}, u32[]{:S(2)}, u32[]{:S(2)}) collective-permute-start(bf16[8,1024]{1,0:T(8,128)(2,1)S(1)} %get-tuple-element.74.refs_1_), channel_id=1, source_target_pairs={{32,0},{64,32},{96,64},{128,96},{160,128},{192,160},{224,192},{33,... | collective-permute-start | bytes 49160 | tf_op jit(solution)/shard_map/ppermute | solution.py:276

commit v4 on v3

--- a/solution.py
+++ b/solution.py
@@ -14,6 +14,7 @@
 STEP = 256
 LANES = 128
 SPACING = 32
+ALONG_X = 4
 
 VMEM = pl.BlockSpec(memory_space=pltpu.VMEM)
 
@@ -50,18 +51,41 @@
     return jnp.dot(a, b, preferred_element_type=F32)
 
 
-def start_kernel(index_ref, saved_ref, grads_ref, blocks_ref, *later_refs):
-    count, rows, _ = blocks_ref.shape
-    for slot in range(len(later_refs) + 1):
-        wanted = index_ref[:, slot : slot + 1]
-        x = saved_ref[0]
-        for place in range(1, saved_ref.shape[0]):
-            x = jnp.where(wanted == place, saved_ref[place], x)
-        if slot:
-            later_refs[slot - 1][...] = x
-        else:
-            blocks_ref[:, :, :D] = jnp.broadcast_to(x[None], (count, rows, D))
-    blocks_ref[:, :, D:] = jnp.broadcast_to(grads_ref[...][None], (count, rows, D))
+def start_kernel(index, saved, grads, blocks_ref, index_v, saved_v, grads_v, sems):
+    loads = [
+        pltpu.make_async_copy(source, target, sems.at[place])
+        for place, (source, target) in enumerate(
+            ((index, index_v), (saved, saved_v), (grads, grads_v))
+        )
+    ]
+    for load in loads:
+        load.start()
+    for load in loads:
+        load.wait()
+    count, rows, width = blocks_ref.shape
+    for slot in range(index_v.shape[1]):
+        wanted = index_v[:, slot : slot + 1]
+        x = saved_v[0]
+        for place in range(1, saved_v.shape[0]):
+            x = jnp.where(wanted == place, saved_v[place], x)
+        at = slot + 1 if slot else 0
+        blocks_ref[:, :, D * at : D * (at + 1)] = jnp.broadcast_to(x[None], (count, rows, D))
+    blocks_ref[:, :, D : 2 * D] = jnp.broadcast_to(grads_v[...][None], (count, rows, D))
+
+
+def split_kernel(begun_ref, *out_refs):
+    width = out_refs[0].shape[-1]
+    for place, out_ref in enumerate(out_refs):
+        out_ref[...] = begun_ref[:, :, width * place : width * (place + 1)]
+
+
+def assemble_kernel(*refs):
+    blocks, out_refs = refs[:ALONG_X], refs[ALONG_X:]
+    mine = lax.axis_index("tensor") % ALONG_X
+    for distance, block_ref in enumerate(blocks):
+        source = (mine + (ALONG_X - distance)) % ALONG_X
+        for place, out_ref in enumerate(out_refs):
+            out_ref[:, pl.ds(source, 1)] = block_ref[:, :, D * place : D * (place + 1)][:, None]
 
 
 def spread_kernel(sections, place, shifted_ref, loss_ref, blocks_ref, rows_ref):
@@ -71,8 +95,9 @@
     blocks_ref[...] = jnp.broadcast_to(chosen[None], blocks_ref.shape)
 
 
-def forward_kernel(x_ref, weights_ref, slope_ref, hidden_ref):
-    x = x_ref[:, :, -D:].reshape(-1, D) if len(x_ref.shape) == 3 else x_ref[...]
+def forward_kernel(x_ref, weights_ref, *refs):
+    slope_ref, hidden_ref = refs[-2:]
+    x = x_ref[...]
     for cols in parts(weights_ref.shape[1]):
         relu = jnp.maximum(mm(x, weights_ref[:, cols]), 0.0)
         slope_ref[:, cols] = 2.0 * relu
@@ -100,10 +125,8 @@
     return dz
 
 
-def back_kernel(grads_ref, slope_ref, w_out_ref, w_in_ref, riding_ref, dz_ref, share_ref):
+def back_kernel(grads_ref, slope_ref, w_out_ref, w_in_ref, dz_ref, share_ref):
     back_products(grads_ref[...], slope_ref, w_out_ref, w_in_ref, dz_ref, share_ref)
-    copies = share_ref.shape[0] // riding_ref.shape[0]
-    share_ref[:, D:] = jnp.concatenate([riding_ref[...]] * copies, axis=0)
 
 
 def last_back_kernel(
@@ -138,12 +161,11 @@
     gram_h_ref[...] = nt(hidden, hidden)
 
 
-def sum_kernel(arrived_ref, incoming_ref, passing_ref, x_ref):
+def sum_kernel(arrived_ref, incoming_ref, passing_ref):
     total = incoming_ref[...].astype(F32)
     for peer in range(arrived_ref.shape[0]):
-        total = total + arrived_ref[peer, :, :D].astype(F32)
+        total = total + arrived_ref[peer].astype(F32)
     passing_ref[...] = total.astype(BF16)
-    x_ref[...] = arrived_ref[:, :, D:].reshape(x_ref.shape)
 
 
 def last_sum_kernel(arrived_ref, incoming_ref, *refs):
@@ -217,9 +239,18 @@
     return lax.all_to_all(blocks, "tensor", split_axis=0, concat_axis=0, tiled=True)
 
 
-def split_kernel(begun_ref, x_ref, grads_ref):
-    x_ref[...] = begun_ref[:, :, :D].reshape(x_ref.shape)
-    grads_ref[...] = begun_ref[:, :, D:].reshape(grads_ref.shape)
+def gather_along_x(block):
+    count = lax.axis_size("tensor")
+    blocks = [block]
+    for distance in range(1, ALONG_X):
+        pairs = [
+            (at, at // ALONG_X * ALONG_X + (at + distance) % ALONG_X) for at in range(count)
+        ]
+        blocks.append(lax.ppermute(block, "tensor", pairs))
+    along_z, rows, width = block.shape
+    outs = (shape(along_z, ALONG_X, rows, D),) * (width // D)
+    gathered = call(assemble_kernel, outs, blocks, 0, "assemble")
+    return [out.reshape(count * rows, D) for out in gathered]
 
 
 def per_device(saved_inputs, slot_index, example_lengths, first_grads, loss_grads, w_in, w_out):
@@ -234,21 +265,35 @@
     product = 2 * tokens * D * units
     square = (tokens, tokens)
 
-    blocks, *riding = call(
+    along_z = count // ALONG_X
+    blocks = pl.pallas_call(
         start_kernel,
-        (shape(count, rows, 2 * D),) + (shape(rows, D),) * (slots - 1),
-        (slot_index, saved_inputs[0], incoming),
-        0,
-        "start",
+        out_shape=shape(along_z, rows, (slots + 1) * D),
+        in_specs=[pl.BlockSpec(memory_space=pl.ANY)] * 3,
+        out_specs=VMEM,
+        scratch_shapes=[
+            pltpu.VMEM(slot_index.shape, jnp.int32),
+            pltpu.VMEM(saved_inputs.shape[1:], BF16),
+            pltpu.VMEM((rows, D), BF16),
+            pltpu.SemaphoreType.DMA((3,)),
+        ],
+        name="start",
+        compiler_params=pltpu.CompilerParams(vmem_limit_bytes=60 * MIB),
+    )(slot_index, saved_inputs[0], incoming)
+    groups = [[z * ALONG_X + x for z in range(along_z)] for x in range(ALONG_X)]
+    begun = lax.all_to_all(
+        blocks, "tensor", split_axis=0, concat_axis=0, axis_index_groups=groups, tiled=True
     )
-    begun = exchange(blocks)
-    x, grads = call(split_kernel, (shape(tokens, D),) * 2, (begun,), 0, "split")
-
-    def forward(x):
+    halves = (shape(along_z, rows, 2 * D), shape(along_z, rows, (slots - 1) * D))
+    urgent, later = call(split_kernel, halves, (begun,), 0, "split")
+    x, grads = gather_along_x(urgent)
+    later = gather_along_x(later)
+
+    def forward(x, *early):
         outs = (shape(tokens, units, dtype=F32), shape(tokens, units))
-        return call(forward_kernel, outs, (x, first), product, "forward")
-
-    slope, hidden = forward(x)
+        return call(forward_kernel, outs, (x, first, *early), product, "forward")
+
+    slope, hidden = forward(x, second)
     xs, hiddens, dzs, dys, results, squares = [], [], [], [], [], []
     for slot in range(slots):
         xs.append(x)
@@ -258,34 +303,28 @@
             break
         dz, share = call(
             back_kernel,
-            (shape(tokens, units), shape(tokens, 2 * D)),
-            (grads, slope, second, first, riding[slot]),
+            (shape(tokens, units), shape(tokens, D)),
+            (grads, slope, second, first),
             2 * product,
             "back",
         )
         dzs.append(dz)
-        arrived = exchange(share.reshape(count, rows, 2 * D))
-        passing, next_x = call(
-            sum_kernel,
-            (shape(rows, D), shape(tokens, D)),
-            (arrived, incoming),
-            tokens * D,
-            "add_up",
-        )
+        arrived = exchange(share.reshape(count, rows, D))
+        passing = call(sum_kernel, shape(rows, D), (arrived, incoming), tokens * D, "add_up")
         results.append(passing)
         shifted = lax.ppermute(
             passing, "section", [(source, source - 1) for source in range(1, sections)]
         )
-        held = lax.optimization_barrier((passing, x, hidden, grads, dz))
+        held = lax.optimization_barrier((passing, x, hidden, grads, dz, later[slot]))
         one = call(
             lambda *refs, slot=slot: squares_kernel(slot, *refs),
             shape(1, LANES, dtype=F32),
-            (lengths, *held[1:]),
+            (lengths, *held[1:5]),
             product,
             "squares",
         )
         squares.append(one)
-        x = next_x
+        x = held[5]
         slope, hidden = forward(x)
         ready = [one, slope, hidden]
         if slot + 2 == slots:

time: 200 us -> 191 us (0.955)
  blocking collectives: 176 us -> 119 us
  waiting for transfers between devices: 0.01 us -> 28.4 us
  starting transfers between devices: 3.83 us -> 17.7 us
  Pallas kernels: 15.7 us -> 19.5 us
  local copies, waits for them, and re-layouts: 3.15 us -> 5.67 us
    all_to_all x6 -> x4, blocking collectives: 176 us -> 92.6 us  [exchange(): lax.all_to_all(blocks, 'tensor', split_axis=0, concat_axis=0, tiled=True)]
    ppermute x0 -> x6, waiting for transfers between devices: none -> 28.4 us  [gather_along_x(): blocks.append(lax.ppermute(block, 'tensor', pairs))]
    all_to_all x0 -> x1, blocking collectives: none -> 26 us  [per_device(): lax.all_to_all(blocks, 'tensor', split_axis=0, concat_axis=0, axis_index_...]
    ppermute x0 -> x6, starting transfers between devices: none -> 9.13 us  [gather_along_x(): blocks.append(lax.ppermute(block, 'tensor', pairs))]
    all_to_all x0 -> x1, starting transfers between devices: none -> 4.74 us  [exchange(): lax.all_to_all(blocks, 'tensor', split_axis=0, concat_axis=0, tiled=True)]
    unnamed x16 -> x30, local copies, waits for them, and re-layouts: 3.15 us -> 5.67 us
    pallas_call x16 -> x17, Pallas kernels: 9.96 us -> 11.8 us  [call(): pl.pallas_call(kernel, out_shape=outs, in_specs=[VMEM] * len(operands), o...]
  transfers between devices with their start and end apart: 2 -> 9, of which waited for: 0 -> 5; matrix products, arithmetic and copies ran while one was open for 0% -> 0% of each run, Pallas kernels for 2% -> 2%
where the time goes in v4:
time: 191 us
  blocking collectives  119 us (62%)
  waiting for transfers between devices  28.4 us (15%)
  Pallas kernels  19.5 us (10%)
  starting transfers between devices  17.7 us (9%)
  local copies, waits for them, and re-layouts  5.67 us (3%)
    all_to_all x4, blocking collectives, exchange(): lax.all_to_all(blocks, 'tensor', split_axis=0, concat_axis=0, tiled=True)  92.6 us
    ppermute x6, waiting for transfers between devices, gather_along_x(): blocks.append(lax.ppermute(block, 'tensor', pairs))  28.4 us
    all_to_all x1, blocking collectives, per_device(): lax.all_to_all(blocks, 'tensor', split_axis=0, concat_axis=0, axis_index_...  26 us
    pallas_call x17, Pallas kernels, call(): pl.pallas_call(kernel, out_shape=outs, in_specs=[VMEM] * len(operands), o...  11.8 us
    ppermute x6, starting transfers between devices, gather_along_x(): blocks.append(lax.ppermute(block, 'tensor', pairs))  9.13 us
    pallas_call x1, Pallas kernels, final_products(): pl.pallas_call(lambda *refs: final_kernel(slots, *refs), grid=(rows // bl...  5.79 us
    unnamed x30, local copies, waits for them, and re-layouts  5.67 us
    all_to_all x1, starting transfers between devices, exchange(): lax.all_to_all(blocks, 'tensor', split_axis=0, concat_axis=0, tiled=True)  4.74 us
  transfers between devices with their start and end apart: 9, of which 5 were waited for; matrix products, arithmetic and copies ran while one was open for 0% of the time, Pallas kernels for 2%

profile of v4, /device:TPU:8, one launch (start us, length us, event | category | flops | bytes accessed | tf_op | source)
XLA Modules:
  0.0 190.8 jit_solution(18143708760940399128)
XLA Ops:
  0.6 1.9 %start.1 = bf16[8,8,4096]{2,1,0:T(8,128)(2,1)} custom-call(s32[1,3]{1,0:T(1,128)} %index.1, bf16[4,8,1024]{2,1,0:T(8,128)(2,1)} %bitcast.54, bf16[8,1024]{1,0:T(8,128)(2,1)} %bitcast.48), custom_call_target="tpu_custom_call" | custom-call | tf_op jit(solution)/shard_map/start/pallas_call | solution.py:269
  2.6 26.0 %all_to_all.30.begun_ref = bf16[8,8,4096]{2,1,0:T(8,128)(2,1)S(1)} all-to-all(bf16[8,8,4096]{2,1,0:T(8,128)(2,1)} %start.1), channel_id=1, replica_groups={{0,4,8,12,16,20,24,28},{1,5,9,13,17,21,25,29},{2,6,10,14,18,22,26,30},{..., dimensions={0} | all-to-all | bytes 1048576 | tf_op jit(solution)/shard_map/all_to_all | solution.py:284
  28.6 2.8 %collective-permute-start.2 = (bf16[8,8,2048]{2,1,0:T(8,128)(2,1)S(1)}, bf16[8,8,2048]{2,1,0:T(8,128)(2,1)S(1)}, u32[]{:S(2)}, u32[]{:S(2)}) collective-permute-start(bf16[8,8,2048]{2,1,0:T(8,128)(2,1)S(1)} %get-tuple-element.51.refs_0_), channel_id=1, source_target_pairs={{0,3},{1,0},{2,1},{3,2},{4,7},{5,4},{6,5},{7,6},{8,11},{9,8},{10,9... | collective-permute-start | bytes 786440 | tf_op jit(solution)/shard_map/ppermute | solution.py:249
  31.4 0.8 collective-permute-start.1
  32.2 0.9 collective-permute-start
  33.1 7.7 %collective-permute-done.2.refs_3_ = bf16[8,8,2048]{2,1,0:T(8,128)(2,1)S(1)} collective-permute-done((bf16[8,8,2048]{2,1,0:T(8,128)(2,1)S(1)}, bf16[8,8,2048]{2,1,0:T(8,128)(2,1)S(1)}, u32[]{:S(2)}, u32[]{:S(2)}) %collective-permute-start.2) | collective-permute-done | bytes 262176 | tf_op jit(solution)/shard_map/ppermute | solution.py:249
  40.8 1.0 collective-permute-done.1.refs_2_
  41.8 2.7 %collective-permute-done.refs_1_ = bf16[8,8,2048]{2,1,0:T(8,128)(2,1)S(1)} collective-permute-done((bf16[8,8,2048]{2,1,0:T(8,128)(2,1)S(1)}, bf16[8,8,2048]{2,1,0:T(8,128)(2,1)S(1)}, u32[]{:S(2)}, u32[]{:S(2)}) %collective-permute-start) | collective-permute-done | bytes 262176 | tf_op jit(solution)/shard_map/ppermute | solution.py:249
  44.5 0.1 assemble.2
  44.6 0.0 copy-start.1
  44.6 1.8 copy-done.1
  46.4 0.7 forward.3
  47.1 0.8 copy-done.8
  47.9 2.1 %back.2 = (bf16[256,1024]{1,0:T(8,128)(2,1)S(1)}, bf16[256,1024]{1,0:T(8,128)(2,1)}) custom-call(bf16[256,1024]{1,0:T(8,128)(2,1)S(1)} %bitcast.43, f32[256,1024]{1,0:T(8,128)S(1)} %get-tuple-element.54.slope_ref, bf16[1024,1024]{1,0:T(8,128)(2,1)S(1)} %bitcast.26, bf16[1024,1024]{1,0:T(8,128)(2,1)S(1)} %bitcast.20), custom_call_target="tpu_custom_call" | custom-call | flops 1073741824 | bytes 1048576 | tf_op jit(solution)/shard_map/back/pallas_call | solution.py:27
  50.0 0.8 copy-done.10
  50.8 4.7 %all-to-all-start.1 = ((bf16[32,8,1024]{2,1,0:T(8,128)(2,1)}), bf16[32,8,1024]{2,1,0:T(8,128)(2,1)}, u32[]{:S(2)}, u32[]{:S(2)}) async-start(bf16[32,8,1024]{2,1,0:T(8,128)(2,1)} %bitcast.9), calls=%async_computation.1 | async-start | bytes 1048576 | tf_op jit(solution)/shard_map/all_to_all | solution.py:239
  55.6 0.0 copy-start.14
  55.6 2.9 %collective-permute-start.6 = (bf16[8,8,2048]{2,1,0:T(8,128)(2,1)S(1)}, bf16[8,8,2048]{2,1,0:T(8,128)(2,1)S(1)}, u32[]{:S(2)}, u32[]{:S(2)}) collective-permute-start(bf16[8,8,2048]{2,1,0:T(8,128)(2,1)S(1)} %get-tuple-element.58.refs_0_), channel_id=1, source_target_pairs={{0,3},{1,0},{2,1},{3,2},{4,7},{5,4},{6,5},{7,6},{8,11},{9,8},{10,9... | collective-permute-start | bytes 786440 | tf_op jit(solution)/shard_map/ppermute | solution.py:249
  58.5 0.8 collective-permute-start.5
  59.3 0.9 collective-permute-start.4
  60.2 13.7 %collective-permute-done.6.refs_3_ = bf16[8,8,2048]{2,1,0:T(8,128)(2,1)S(1)} collective-permute-done((bf16[8,8,2048]{2,1,0:T(8,128)(2,1)S(1)}, bf16[8,8,2048]{2,1,0:T(8,128)(2,1)S(1)}, u32[]{:S(2)}, u32[]{:S(2)}) %collective-permute-start.6) | collective-permute-done | bytes 262176 | tf_op jit(solution)/shard_map/ppermute | solution.py:249
  73.9 3.3 %collective-permute-done.4.refs_1_ = bf16[8,8,2048]{2,1,0:T(8,128)(2,1)S(1)} collective-permute-done((bf16[8,8,2048]{2,1,0:T(8,128)(2,1)S(1)}, bf16[8,8,2048]{2,1,0:T(8,128)(2,1)S(1)}, u32[]{:S(2)}, u32[]{:S(2)}) %collective-permute-start.4) | collective-permute-done | bytes 262176 | tf_op jit(solution)/shard_map/ppermute | solution.py:249
  77.2 0.1 assemble.3
  77.3 0.0 copy-start.3
  77.3 0.8 copy-done.3
  78.1 1.2 add_up.2.refs_0_
  79.3 1.9 %collective-permute-start.3 = (bf16[8,1024]{1,0:T(8,128)(2,1)S(1)}, bf16[8,1024]{1,0:T(8,128)(2,1)S(1)}, u32[]{:S(2)}, u32[]{:S(2)}) collective-permute-start(bf16[8,1024]{1,0:T(8,128)(2,1)S(1)} %add_up.2.refs_0_), channel_id=1, source_target_pairs={{32,0},{64,32},{96,64},{128,96},{160,128},{192,160},{224,192},{33,... | collective-permute-start | bytes 49160 | tf_op jit(solution)/shard_map/ppermute | solution.py:315
  81.2 0.0 copy-start.4
  81.2 1.0 copy-done.4
  82.3 0.7 forward.4
  83.0 0.0 copy-start.2
  83.0 0.3 copy-done.9
  83.3 0.2 copy-done.11
  83.4 0.9 squares.2.refs_7_
  84.4 24.4 %all_to_all.31 = bf16[32,8,1024]{2,1,0:T(8,128)(2,1)S(1)} all-to-all(bf16[32,8,1024]{2,1,0:T(8,128)(2,1)S(1)} %get-tuple-element.68), channel_id=1, replica_groups=mesh['section'=8,'tensor'=32] {'tensor'}, dimensions={0} | all-to-all | bytes 1048576 | tf_op jit(solution)/shard_map/all_to_all | solution.py:239
  108.8 1.3 back.3
  110.1 0.0 copy-start.5
  110.1 21.8 %all_to_all.32.arrived_ref = bf16[32,8,1024]{2,1,0:T(8,128)(2,1)S(1)} all-to-all(bf16[32,8,1024]{2,1,0:T(8,128)(2,1)S(1)} %bitcast.47), channel_id=1, replica_groups=mesh['section'=8,'tensor'=32] {'tensor'}, dimensions={0} | all-to-all | bytes 1048576 | tf_op jit(solution)/shard_map/all_to_all | solution.py:239
  132.0 0.1 add_up.3.refs_1_
  132.1 1.9 %collective-permute-start.7 = (bf16[8,1024]{1,0:T(8,128)(2,1)S(1)}, bf16[8,1024]{1,0:T(8,128)(2,1)S(1)}, u32[]{:S(2)}, u32[]{:S(2)}) collective-permute-start(bf16[8,1024]{1,0:T(8,128)(2,1)S(1)} %add_up.3.refs_1_), channel_id=1, source_target_pairs={{32,0},{64,32},{96,64},{128,96},{160,128},{192,160},{224,192},{33,... | collective-permute-start | bytes 49160 | tf_op jit(solution)/shard_map/ppermute | solution.py:315
  134.0 0.7 forward.5
  134.7 0.9 squares.3.refs_8_
  135.6 0.5 grams.1
  136.2 22.5 %all_to_all.33 = bf16[32,8,1024]{2,1,0:T(8,128)(2,1)S(1)} all-to-all(bf16[32,8,1024]{2,1,0:T(8,128)(2,1)S(1)} %get-tuple-element.85), channel_id=1, replica_groups=mesh['section'=8,'tensor'=32] {'tensor'}, dimensions={0} | all-to-all | bytes 1048576 | tf_op jit(solution)/shard_map/all_to_all | solution.py:239
  158.6 1.8 last_back.1
  160.4 23.9 %all_to_all.34.arrived_ref = bf16[32,8,1152]{2,1,0:T(8,128)(2,1)S(1)} all-to-all(bf16[32,8,1152]{2,1,0:T(8,128)(2,1)S(1)} %bitcast.46), channel_id=1, replica_groups=mesh['section'=8,'tensor'=32] {'tensor'}, dimensions={0} | all-to-all | bytes 1179648 | tf_op jit(solution)/shard_map/all_to_all | solution.py:239
  184.3 0.7 last_add_up.1
  185.0 5.8 %final.1 = (bf16[1024,1024]{1,0:T(8,128)(2,1)}, bf16[1024,1024]{1,0:T(8,128)(2,1)}) custom-call(s32[2,3]{1,0:T(2,128)S(1)} %bitcast.53, f32[1,128]{1,0:T(1,128)S(1)} %get-tuple-element.93.refs_1_, bf16[256,1024]{1,0:T(8,128)(2,1)S(1)} %bitcast.39, bf16[256,1024]{1,0:T(8,128)(2,1)S(1)} %bitcast.42, bf16[256,1024]{1,0:T(8,128)(2,1)S(1)} %bitcast.34, ...), custom_call_target="tpu_custom_call" | custom-call | flops 3221225472 | bytes 4194304 | tf_op jit(solution)/shard_map/final/pallas_call | solution.py:223
  (24 shorter events, 0.2 us)
Async XLA Ops:
  0.6 44.0 %copy-start = (bf16[1,1024,1024]{2,1,0:T(8,128)(2,1)S(1)}, bf16[1,1024,1024]{2,1,0:T(8,128)(2,1)}, u32[]{:S(2)}) copy-start(bf16[1,1024,1024]{2,1,0:T(8,128)(2,1)} %param.12) | copy-start | bytes 6291460
  28.6 12.2 %collective-permute-start.2 = (bf16[8,8,2048]{2,1,0:T(8,128)(2,1)S(1)}, bf16[8,8,2048]{2,1,0:T(8,128)(2,1)S(1)}, u32[]{:S(2)}, u32[]{:S(2)}) collective-permute-start(bf16[8,8,2048]{2,1,0:T(8,128)(2,1)S(1)} %get-tuple-element.51.refs_0_), channel_id=1, source_target_pairs={{0,3},{1,0},{2,1},{3,2},{4,7},{5,4},{6,5},{7,6},{8,11},{9,8},{10,9... | collective-permute-start | bytes 786440 | tf_op jit(solution)/shard_map/ppermute | solution.py:249
  31.4 10.4 %collective-permute-start.1 = (bf16[8,8,2048]{2,1,0:T(8,128)(2,1)S(1)}, bf16[8,8,2048]{2,1,0:T(8,128)(2,1)S(1)}, u32[]{:S(2)}, u32[]{:S(2)}) collective-permute-start(bf16[8,8,2048]{2,1,0:T(8,128)(2,1)S(1)} %get-tuple-element.51.refs_0_), channel_id=1, source_target_pairs={{0,2},{1,3},{2,0},{3,1},{4,6},{5,7},{6,4},{7,5},{8,10},{9,11},{10,... | collective-permute-start | bytes 786440 | tf_op jit(solution)/shard_map/ppermute | solution.py:249
  32.2 12.3 %collective-permute-start = (bf16[8,8,2048]{2,1,0:T(8,128)(2,1)S(1)}, bf16[8,8,2048]{2,1,0:T(8,128)(2,1)S(1)}, u32[]{:S(2)}, u32[]{:S(2)}) collective-permute-start(bf16[8,8,2048]{2,1,0:T(8,128)(2,1)S(1)} %get-tuple-element.51.refs_0_), channel_id=1, source_target_pairs={{0,1},{1,2},{2,3},{3,0},{4,5},{5,6},{6,7},{7,4},{8,9},{9,10},{10,1... | collective-permute-start | bytes 786440 | tf_op jit(solution)/shard_map/ppermute | solution.py:249
  44.6 3.3 %copy-start.6 = (bf16[8,4,8,1024]{3,2,1,0:T(8,128)(2,1)}, bf16[8,4,8,1024]{3,2,1,0:T(8,128)(2,1)S(1)}, u32[]{:S(2)}) copy-start(bf16[8,4,8,1024]{3,2,1,0:T(8,128)(2,1)S(1)} %get-tuple-element.52) | copy-start | bytes 1572868
  44.6 1.8 copy-start.1
  47.1 0.8 copy-start.8
  50.0 0.8 copy-start.10
  50.8 27.3 %copy-start.13 = (bf16[1,8,1024]{2,1,0:T(8,128)(2,1)S(1)}, bf16[1,8,1024]{2,1,0:T(8,128)(2,1)}, u32[]{:S(2)}) copy-start(bf16[1,8,1024]{2,1,0:T(8,128)(2,1)} %param.10) | copy-start | bytes 49156
  50.8 27.3 %all-to-all-start.1 = ((bf16[32,8,1024]{2,1,0:T(8,128)(2,1)}), bf16[32,8,1024]{2,1,0:T(8,128)(2,1)}, u32[]{:S(2)}, u32[]{:S(2)}) async-start(bf16[32,8,1024]{2,1,0:T(8,128)(2,1)} %bitcast.9), calls=%async_computation.1 | async-start | bytes 1048576 | tf_op jit(solution)/shard_map/all_to_all | solution.py:239
  55.6 27.4 %copy-start.14 = (s32[1,3,2]{1,2,0:T(2,128)S(1)}, s32[1,3,2]{1,2,0:T(2,128)}, u32[]{:S(2)}) copy-start(s32[1,3,2]{1,2,0:T(2,128)} %param.9) | copy-start | bytes 76
  55.6 18.3 %collective-permute-start.6 = (bf16[8,8,2048]{2,1,0:T(8,128)(2,1)S(1)}, bf16[8,8,2048]{2,1,0:T(8,128)(2,1)S(1)}, u32[]{:S(2)}, u32[]{:S(2)}) collective-permute-start(bf16[8,8,2048]{2,1,0:T(8,128)(2,1)S(1)} %get-tuple-element.58.refs_0_), channel_id=1, source_target_pairs={{0,3},{1,0},{2,1},{3,2},{4,7},{5,4},{6,5},{7,6},{8,11},{9,8},{10,9... | collective-permute-start | bytes 786440 | tf_op jit(solution)/shard_map/ppermute | solution.py:249
  58.5 15.4 %collective-permute-start.5 = (bf16[8,8,2048]{2,1,0:T(8,128)(2,1)S(1)}, bf16[8,8,2048]{2,1,0:T(8,128)(2,1)S(1)}, u32[]{:S(2)}, u32[]{:S(2)}) collective-permute-start(bf16[8,8,2048]{2,1,0:T(8,128)(2,1)S(1)} %get-tuple-element.58.refs_0_), channel_id=1, source_target_pairs={{0,2},{1,3},{2,0},{3,1},{4,6},{5,7},{6,4},{7,5},{8,10},{9,11},{10,... | collective-permute-start | bytes 786440 | tf_op jit(solution)/shard_map/ppermute | solution.py:249
  59.3 17.9 %collective-permute-start.4 = (bf16[8,8,2048]{2,1,0:T(8,128)(2,1)S(1)}, bf16[8,8,2048]{2,1,0:T(8,128)(2,1)S(1)}, u32[]{:S(2)}, u32[]{:S(2)}) collective-permute-start(bf16[8,8,2048]{2,1,0:T(8,128)(2,1)S(1)} %get-tuple-element.58.refs_0_), channel_id=1, source_target_pairs={{0,1},{1,2},{2,3},{3,0},{4,5},{5,6},{6,7},{7,4},{8,9},{9,10},{10,1... | collective-permute-start | bytes 786440 | tf_op jit(solution)/shard_map/ppermute | solution.py:249
  77.3 0.8 copy-start.3
  78.1 4.9 %copy-start.7 = (bf16[8,4,8,1024]{3,2,1,0:T(8,128)(2,1)S(1)}, bf16[8,4,8,1024]{3,2,1,0:T(8,128)(2,1)}, u32[]{:S(2)}) copy-start(bf16[8,4,8,1024]{3,2,1,0:T(8,128)(2,1)} %copy-done.6) | copy-start | bytes 1572868
  79.3 5.1 %collective-permute-start.3 = (bf16[8,1024]{1,0:T(8,128)(2,1)S(1)}, bf16[8,1024]{1,0:T(8,128)(2,1)S(1)}, u32[]{:S(2)}, u32[]{:S(2)}) collective-permute-start(bf16[8,1024]{1,0:T(8,128)(2,1)S(1)} %add_up.2.refs_0_), channel_id=1, source_target_pairs={{32,0},{64,32},{96,64},{128,96},{160,128},{192,160},{224,192},{33,... | collective-permute-start | bytes 49160 | tf_op jit(solution)/shard_map/ppermute | solution.py:315
  81.2 1.0 copy-start.4
  82.2 1.0 copy-start.9
  82.2 1.2 copy-start.11
  82.3 2.1 %copy-start.12 = (bf16[2,8,1024]{2,1,0:T(8,128)(2,1)S(1)}, bf16[2,8,1024]{2,1,0:T(8,128)(2,1)}, u32[]{:S(2)}) copy-start(bf16[2,8,1024]{2,1,0:T(8,128)(2,1)} %refs_1_.3) | copy-start | bytes 98308
  83.0 25.8 %copy-start.2 = (bf16[1,1024,1024]{2,1,0:T(8,128)(2,1)S(1)}, bf16[1,1024,1024]{2,1,0:T(8,128)(2,1)}, u32[]{:S(2)}) copy-start(bf16[1,1024,1024]{2,1,0:T(8,128)(2,1)} %param.13) | copy-start | bytes 6291460
  110.1 24.6 %copy-start.5 = (bf16[8,4,8,1024]{3,2,1,0:T(8,128)(2,1)S(1)}, bf16[8,4,8,1024]{3,2,1,0:T(8,128)(2,1)}, u32[]{:S(2)}) copy-start(bf16[8,4,8,1024]{3,2,1,0:T(8,128)(2,1)} %copy-done.3) | copy-start | bytes 1572868
  132.1 4.0 %collective-permute-start.7 = (bf16[8,1024]{1,0:T(8,128)(2,1)S(1)}, bf16[8,1024]{1,0:T(8,128)(2,1)S(1)}, u32[]{:S(2)}, u32[]{:S(2)}) collective-permute-start(bf16[8,1024]{1,0:T(8,128)(2,1)S(1)} %add_up.3.refs_1_), channel_id=1, source_target_pairs={{32,0},{64,32},{96,64},{128,96},{160,128},{192,160},{224,192},{33,... | collective-permute-start | bytes 49160 | tf_op jit(solution)/shard_map/ppermute | solution.py:315

commit v5 on v4

--- a/solution.py
+++ b/solution.py
@@ -73,10 +73,12 @@
     blocks_ref[:, :, D : 2 * D] = jnp.broadcast_to(grads_v[...][None], (count, rows, D))
 
 
-def split_kernel(begun_ref, *out_refs):
-    width = out_refs[0].shape[-1]
-    for place, out_ref in enumerate(out_refs):
-        out_ref[...] = begun_ref[:, :, width * place : width * (place + 1)]
+def split_kernel(begun_ref, loss_ref, urgent_ref, later_ref):
+    along_z, _, width = urgent_ref.shape
+    urgent_ref[...] = begun_ref[:, :, :width]
+    later_ref[:along_z] = begun_ref[:, :, width:]
+    for place in range(loss_ref.shape[0]):
+        later_ref[along_z, :, D * place : D * (place + 1)] = loss_ref[place]
 
 
 def assemble_kernel(*refs):
@@ -84,14 +86,41 @@
     mine = lax.axis_index("tensor") % ALONG_X
     for distance, block_ref in enumerate(blocks):
         source = (mine + (ALONG_X - distance)) % ALONG_X
-        for place, out_ref in enumerate(out_refs):
-            out_ref[:, pl.ds(source, 1)] = block_ref[:, :, D * place : D * (place + 1)][:, None]
-
-
-def spread_kernel(sections, place, shifted_ref, loss_ref, blocks_ref, rows_ref):
+        done = {}
+        for out_ref in out_refs:
+            deep = out_ref.shape[0]
+            top = 0 if deep == out_refs[0].shape[0] else out_refs[0].shape[0]
+            at = done.get(top, 0)
+            done[top] = at + D
+            out_ref[:, pl.ds(source, 1)] = block_ref[top : top + deep, :, at : at + D][:, None]
+
+
+def partial_kernel(arrived_ref, grads_ref, partial_ref, both_ref):
+    total = arrived_ref[0].astype(F32)
+    for peer in range(1, arrived_ref.shape[0]):
+        total = total + arrived_ref[peer].astype(F32)
+    total = total.astype(BF16)
+    partial_ref[...] = total
+    both_ref[:, :D] = total
+    both_ref[:, D:] = grads_ref[lax.axis_index("tensor") // ALONG_X]
+
+
+def combine_kernel(sections, both_ref, *refs):
+    *parts_refs, loss_ref, blocks_ref, own_ref = refs
+    first, second, third = [ref[...].astype(F32) for ref in parts_refs]
+    total = (both_ref[:, :D].astype(F32) + second) + (first + third)
+    passing = (both_ref[:, D:].astype(F32) + total).astype(BF16)
+    rows = own_ref.shape[0]
+    mine = lax.axis_index("tensor") % ALONG_X
+    for x in range(ALONG_X):
+
+        @pl.when(mine == x)
+        def _():
+            own_ref[...] = passing[rows * x : rows * (x + 1)]
+
     last = (lax.axis_index("section") == sections - 1).astype(jnp.int32)
-    chosen = jnp.where(jnp.full(rows_ref.shape, last) > 0, loss_ref[place], shifted_ref[...])
-    rows_ref[...] = chosen
+    loss = loss_ref[0].reshape(passing.shape)
+    chosen = jnp.where(jnp.full(passing.shape, last) > 0, loss, passing)
     blocks_ref[...] = jnp.broadcast_to(chosen[None], blocks_ref.shape)
 
 
@@ -161,16 +190,9 @@
     gram_h_ref[...] = nt(hidden, hidden)
 
 
-def sum_kernel(arrived_ref, incoming_ref, passing_ref):
-    total = incoming_ref[...].astype(F32)
-    for peer in range(arrived_ref.shape[0]):
-        total = total + arrived_ref[peer].astype(F32)
-    passing_ref[...] = total.astype(BF16)
-
-
-def last_sum_kernel(arrived_ref, incoming_ref, *refs):
+def last_sum_kernel(arrived_ref, grads_ref, *refs):
     *earlier_refs, results_ref, line_ref = refs
-    total = incoming_ref[...].astype(F32)
+    total = grads_ref[lax.axis_index("tensor")].astype(F32)
     line = jnp.zeros(line_ref.shape, F32)
     for peer in range(arrived_ref.shape[0]):
         total = total + arrived_ref[peer, :, :D].astype(F32)
@@ -239,18 +261,36 @@
     return lax.all_to_all(blocks, "tensor", split_axis=0, concat_axis=0, tiled=True)
 
 
-def gather_along_x(block):
+def exchange_along_z(blocks):
     count = lax.axis_size("tensor")
-    blocks = [block]
-    for distance in range(1, ALONG_X):
-        pairs = [
-            (at, at // ALONG_X * ALONG_X + (at + distance) % ALONG_X) for at in range(count)
-        ]
-        blocks.append(lax.ppermute(block, "tensor", pairs))
-    along_z, rows, width = block.shape
-    outs = (shape(along_z, ALONG_X, rows, D),) * (width // D)
-    gathered = call(assemble_kernel, outs, blocks, 0, "assemble")
-    return [out.reshape(count * rows, D) for out in gathered]
+    groups = [list(range(x, count, ALONG_X)) for x in range(ALONG_X)]
+    return lax.all_to_all(
+        blocks, "tensor", split_axis=0, concat_axis=0, axis_index_groups=groups, tiled=True
+    )
+
+
+def moved(value, sections_back, distance):
+    sections, count = lax.axis_size("section"), lax.axis_size("tensor")
+    pairs = [
+        (
+            section * count + at,
+            (section - sections_back) % sections * count
+            + at // ALONG_X * ALONG_X
+            + (at + distance) % ALONG_X,
+        )
+        for section in range(sections)
+        for at in range(count)
+    ]
+    return lax.ppermute(value, ("section", "tensor"), pairs)
+
+
+def gather_along_x(block, along_z):
+    blocks = [block] + [moved(block, 0, distance) for distance in range(1, ALONG_X)]
+    deep, rows, width = block.shape
+    outs = [shape(along_z, ALONG_X, rows, D)] * (width // D)
+    if deep > along_z:
+        outs += [shape(deep - along_z, ALONG_X, rows, D)] * (width // D)
+    return call(assemble_kernel, outs, blocks, 0, "assemble")
 
 
 def per_device(saved_inputs, slot_index, example_lengths, first_grads, loss_grads, w_in, w_out):
@@ -280,14 +320,10 @@
         name="start",
         compiler_params=pltpu.CompilerParams(vmem_limit_bytes=60 * MIB),
     )(slot_index, saved_inputs[0], incoming)
-    groups = [[z * ALONG_X + x for z in range(along_z)] for x in range(ALONG_X)]
-    begun = lax.all_to_all(
-        blocks, "tensor", split_axis=0, concat_axis=0, axis_index_groups=groups, tiled=True
-    )
-    halves = (shape(along_z, rows, 2 * D), shape(along_z, rows, (slots - 1) * D))
-    urgent, later = call(split_kernel, halves, (begun,), 0, "split")
-    x, grads = gather_along_x(urgent)
-    later = gather_along_x(later)
+    begun = exchange_along_z(blocks)
+    halves = (shape(along_z, rows, 2 * D), shape(along_z + 1, rows, (slots - 1) * D))
+    urgent, later = call(split_kernel, halves, (begun, loss_grads), 0, "split")
+    x, grads = [part.reshape(tokens, D) for part in gather_along_x(urgent, along_z)]
 
     def forward(x, *early):
         outs = (shape(tokens, units, dtype=F32), shape(tokens, units))
@@ -309,13 +345,26 @@
             "back",
         )
         dzs.append(dz)
-        arrived = exchange(share.reshape(count, rows, D))
-        passing = call(sum_kernel, shape(rows, D), (arrived, incoming), tokens * D, "add_up")
-        results.append(passing)
-        shifted = lax.ppermute(
-            passing, "section", [(source, source - 1) for source in range(1, sections)]
-        )
-        held = lax.optimization_barrier((passing, x, hidden, grads, dz, later[slot]))
+        by_z = (along_z, tokens // along_z, D)
+        arrived = exchange_along_z(share.reshape(by_z))
+        partial, both = call(
+            partial_kernel,
+            (shape(*by_z[1:]), shape(by_z[1], 2 * D)),
+            (arrived, grads.reshape(by_z)),
+            tokens * D,
+            "partial",
+        )
+        if slot:
+            partial, both, results[-1] = lax.optimization_barrier((partial, both, results[-1]))
+            results[-1] = moved(results[-1], -1, 0)
+        else:
+            partial, both, later = lax.optimization_barrier((partial, both, later))
+        pieces = [moved(both, 1, 0)]
+        pieces += [moved(partial, 1, distance) for distance in range(1, ALONG_X)]
+        if not slot:
+            later = gather_along_x(later, along_z)
+            later, loss = later[: slots - 1], later[slots - 1 :]
+        held = lax.optimization_barrier((partial, x, hidden, grads, dz, later[slot]))
         one = call(
             lambda *refs, slot=slot: squares_kernel(slot, *refs),
             shape(1, LANES, dtype=F32),
@@ -324,23 +373,30 @@
             "squares",
         )
         squares.append(one)
-        x = held[5]
+        x = held[5].reshape(tokens, D)
         slope, hidden = forward(x)
-        ready = [one, slope, hidden]
+        ready = [one, slope, hidden, results[-1] if slot else later[1]]
         if slot + 2 == slots:
             ready += call(
                 grams_kernel, (shape(*square, dtype=F32),) * 2, (x, hidden), product // 4, "grams"
             )
-        shifted, squares[-1], slope, hidden, *grams = lax.optimization_barrier((shifted, *ready))
-        blocks, incoming = call(
-            lambda *refs, slot=slot: spread_kernel(sections, slot, *refs),
-            (shape(count, rows, D), shape(rows, D)),
-            (shifted, loss_grads),
+        pieces[0], squares[-1], slope, hidden, other, *grams = lax.optimization_barrier(
+            (pieces[0], *ready)
+        )
+        if slot:
+            results[-1] = other
+        blocks, own = call(
+            lambda *refs: combine_kernel(sections, *refs),
+            (shape(*by_z), shape(rows, D)),
+            (*pieces, loss[slot]),
             0,
-            "spread",
-        )
-        grads = exchange(blocks).reshape(tokens, D)
-
+            "combine",
+        )
+        results.append(own)
+        grads = exchange_along_z(blocks).reshape(tokens, D)
+
+    grads, results[-1] = lax.optimization_barrier((grads, results[-1]))
+    results[-1] = moved(results[-1], -1, 0)
     dz, share = call(
         lambda *refs: last_back_kernel(slots - 1, *refs),
         (shape(tokens, units), shape(tokens, D + LANES)),
@@ -349,11 +405,12 @@
         "last_back",
     )
     dzs.append(dz)
+    share, results[-1] = lax.optimization_barrier((share, results[-1]))
     arrived = exchange(share.reshape(count, rows, D + LANES))
     results, totals = call(
         last_sum_kernel,
         (shape(slots, rows, D), shape(1, LANES, dtype=F32)),
-        (arrived, incoming, *results),
+        (arrived, grads.reshape(count, rows, D), *results),
         tokens * D,
         "last_add_up",
     )

time: 191 us -> 192 us (level)
  blocking collectives: 119 us -> 129 us
  local copies, waits for them, and re-layouts: 5.67 us -> 2.36 us
  starting transfers between devices: 17.7 us -> 14.5 us
  waiting for transfers between devices: 28.4 us -> 26.2 us
    all_to_all x1 -> x5, blocking collectives: 26 us -> 108 us  [exchange_along_z(): lax.all_to_all(blocks, 'tensor', split_axis=0, concat_axis=0, axis_index_...]
    all_to_all x4 -> x1, blocking collectives: 92.6 us -> 21.3 us  [exchange(): lax.all_to_all(blocks, 'tensor', split_axis=0, concat_axis=0, tiled=True)]
    all_to_all x1 -> x0, starting transfers between devices: 4.74 us -> none  [exchange(): lax.all_to_all(blocks, 'tensor', split_axis=0, concat_axis=0, tiled=True)]
    unnamed x30 -> x10, local copies, waits for them, and re-layouts: 5.67 us -> 2.36 us
    ppermute x8 -> x16, waiting for transfers between devices: 28.4 us -> 26.2 us  [moved(): return lax.ppermute(value, ('section', 'tensor'), pairs)]
    ppermute x8 -> x16, starting transfers between devices: 13 us -> 14.5 us  [moved(): return lax.ppermute(value, ('section', 'tensor'), pairs)]
  transfers between devices with their start and end apart: 9 -> 16, of which waited for: 5 -> 9; matrix products, arithmetic and copies ran while one was open for 0% -> 0% of each run, Pallas kernels for 2% -> 3%
where the time goes in v5:
time: 192 us; the launch traced here: 191 us
  blocking collectives  129 us (67%)
  waiting for transfers between devices  26.2 us (14%)
  Pallas kernels  17.8 us (9%)
  starting transfers between devices  14.5 us (8%)
  local copies, waits for them, and re-layouts  2.36 us (1%)
    all_to_all x5, blocking collectives, exchange_along_z(): lax.all_to_all(blocks, 'tensor', split_axis=0, concat_axis=0, axis_index_...  108 us
    ppermute x16, waiting for transfers between devices, moved(): return lax.ppermute(value, ('section', 'tensor'), pairs)  26.2 us
    all_to_all x1, blocking collectives, exchange(): lax.all_to_all(blocks, 'tensor', split_axis=0, concat_axis=0, tiled=True)  21.3 us
    ppermute x16, starting transfers between devices, moved(): return lax.ppermute(value, ('section', 'tensor'), pairs)  14.5 us
    pallas_call x17, Pallas kernels, call(): pl.pallas_call(kernel, out_shape=outs, in_specs=[VMEM] * len(operands), o...  10 us
    pallas_call x1, Pallas kernels, final_products(): pl.pallas_call(lambda *refs: final_kernel(slots, *refs), grid=(rows // bl...  5.79 us
  transfers between devices with their start and end apart: 16, of which 9 were waited for; matrix products, arithmetic and copies ran while one was open for 0% of the time, Pallas kernels for 3%

profile of v5, /device:TPU:8, one launch (start us, length us, event | category | flops | bytes accessed | tf_op | source)
XLA Modules:
  0.0 191.0 jit_solution(5976917068797115229)
XLA Ops:
  0.6 1.9 %start.1 = bf16[8,8,4096]{2,1,0:T(8,128)(2,1)} custom-call(s32[1,3]{1,0:T(1,128)} %index.1, bf16[4,8,1024]{2,1,0:T(8,128)(2,1)} %bitcast.57, bf16[8,1024]{1,0:T(8,128)(2,1)} %bitcast.58), custom_call_target="tpu_custom_call" | custom-call | tf_op jit(solution)/shard_map/start/pallas_call | solution.py:309
  2.6 26.0 %all_to_all.30.begun_ref = bf16[8,8,4096]{2,1,0:T(8,128)(2,1)S(1)} all-to-all(bf16[8,8,4096]{2,1,0:T(8,128)(2,1)} %start.1), channel_id=1, replica_groups={{0,4,8,12,16,20,24,28},{1,5,9,13,17,21,25,29},{2,6,10,14,18,22,26,30},{..., dimensions={0} | all-to-all | bytes 1048576 | tf_op jit(solution)/shard_map/all_to_all | solution.py:267
  28.5 0.8 copy-done.3
  29.3 2.8 %collective-permute-start.2 = (bf16[8,8,2048]{2,1,0:T(8,128)(2,1)S(1)}, bf16[8,8,2048]{2,1,0:T(8,128)(2,1)S(1)}, u32[]{:S(2)}, u32[]{:S(2)}) collective-permute-start(bf16[8,8,2048]{2,1,0:T(8,128)(2,1)S(1)} %get-tuple-element.68.refs_0_), channel_id=1, source_target_pairs={{0,3},{1,0},{2,1},{3,2},{4,7},{5,4},{6,5},{7,6},{8,11},{9,8},{10,9... | collective-permute-start | bytes 786440 | tf_op jit(solution)/shard_map/ppermute | solution.py:284
  32.2 0.8 collective-permute-start.1
  33.0 0.9 collective-permute-start
  33.9 7.7 %collective-permute-done.2.refs_3_ = bf16[8,8,2048]{2,1,0:T(8,128)(2,1)S(1)} collective-permute-done((bf16[8,8,2048]{2,1,0:T(8,128)(2,1)S(1)}, bf16[8,8,2048]{2,1,0:T(8,128)(2,1)S(1)}, u32[]{:S(2)}, u32[]{:S(2)}) %collective-permute-start.2) | collective-permute-done | bytes 262176 | tf_op jit(solution)/shard_map/ppermute | solution.py:284
  41.6 1.0 collective-permute-done.1.refs_2_
  42.6 2.7 %collective-permute-done.refs_1_ = bf16[8,8,2048]{2,1,0:T(8,128)(2,1)S(1)} collective-permute-done((bf16[8,8,2048]{2,1,0:T(8,128)(2,1)S(1)}, bf16[8,8,2048]{2,1,0:T(8,128)(2,1)S(1)}, u32[]{:S(2)}, u32[]{:S(2)}) %collective-permute-start) | collective-permute-done | bytes 262176 | tf_op jit(solution)/shard_map/ppermute | solution.py:284
  45.3 0.1 assemble.2
  45.4 0.0 copy-start.1
  45.4 1.6 copy-done.1
  47.0 0.7 forward.3
  47.7 1.3 back.2
  49.0 20.4 %all_to_all.31.arrived_ref = bf16[8,32,1024]{2,1,0:T(8,128)(2,1)S(1)} all-to-all(bf16[8,32,1024]{2,1,0:T(8,128)(2,1)S(1)} %bitcast.51), channel_id=1, replica_groups={{0,4,8,12,16,20,24,28},{1,5,9,13,17,21,25,29},{2,6,10,14,18,22,26,30},{..., dimensions={0} | all-to-all | bytes 1048576 | tf_op jit(solution)/shard_map/all_to_all | solution.py:267
  69.4 0.1 partial.2
  69.5 0.1 collective-permute-start.6
  69.6 0.9 collective-permute-start.5
  70.5 1.3 collective-permute-start.4
  71.8 2.5 %collective-permute-start.9 = (bf16[32,1024]{1,0:T(8,128)(2,1)S(1)}, bf16[32,1024]{1,0:T(8,128)(2,1)S(1)}, u32[]{:S(2)}, u32[]{:S(2)}) collective-permute-start(bf16[32,1024]{1,0:T(8,128)(2,1)S(1)} %get-tuple-element.77), channel_id=1, source_target_pairs={{0,227},{1,224},{2,225},{3,226},{4,231},{5,228},{6,229},{7,230},{8... | collective-permute-start | bytes 196616 | tf_op jit(solution)/shard_map/ppermute | solution.py:284
  74.3 5.2 %collective-permute-done.6.refs_3_ = bf16[9,8,2048]{2,1,0:T(8,128)(2,1)S(1)} collective-permute-done((bf16[9,8,2048]{2,1,0:T(8,128)(2,1)S(1)}, bf16[9,8,2048]{2,1,0:T(8,128)(2,1)S(1)}, u32[]{:S(2)}, u32[]{:S(2)}) %collective-permute-start.6) | collective-permute-done | bytes 294944 | tf_op jit(solution)/shard_map/ppermute | solution.py:284
  79.5 1.6 collective-permute-done.5.refs_2_
  81.1 4.4 %collective-permute-done.4.refs_1_ = bf16[9,8,2048]{2,1,0:T(8,128)(2,1)S(1)} collective-permute-done((bf16[9,8,2048]{2,1,0:T(8,128)(2,1)S(1)}, bf16[9,8,2048]{2,1,0:T(8,128)(2,1)S(1)}, u32[]{:S(2)}, u32[]{:S(2)}) %collective-permute-start.4) | collective-permute-done | bytes 294944 | tf_op jit(solution)/shard_map/ppermute | solution.py:284
  85.5 0.1 assemble.3
  85.6 0.7 forward.4
  86.4 0.9 squares.2.refs_7_
  87.3 0.1 combine.2
  87.4 18.8 %all_to_all.32.grads_ref = bf16[8,32,1024]{2,1,0:T(8,128)(2,1)S(1)} all-to-all(bf16[8,32,1024]{2,1,0:T(8,128)(2,1)S(1)} %get-tuple-element.92), channel_id=1, replica_groups={{0,4,8,12,16,20,24,28},{1,5,9,13,17,21,25,29},{2,6,10,14,18,22,26,30},{..., dimensions={0} | all-to-all | bytes 1048576 | tf_op jit(solution)/shard_map/all_to_all | solution.py:267
  106.2 1.3 back.3
  107.5 22.0 %all_to_all.33.arrived_ref = bf16[8,32,1024]{2,1,0:T(8,128)(2,1)S(1)} all-to-all(bf16[8,32,1024]{2,1,0:T(8,128)(2,1)S(1)} %bitcast.52), channel_id=1, replica_groups={{0,4,8,12,16,20,24,28},{1,5,9,13,17,21,25,29},{2,6,10,14,18,22,26,30},{..., dimensions={0} | all-to-all | bytes 1048576 | tf_op jit(solution)/shard_map/all_to_all | solution.py:267
  129.5 0.1 partial.3
  129.5 0.2 collective-permute-start.10
  129.7 0.1 collective-permute-start.14
  129.8 3.7 %collective-permute-start.13 = (bf16[32,1024]{1,0:T(8,128)(2,1)S(1)}, bf16[32,1024]{1,0:T(8,128)(2,1)S(1)}, u32[]{:S(2)}, u32[]{:S(2)}) collective-permute-start(bf16[32,1024]{1,0:T(8,128)(2,1)S(1)} %get-tuple-element.99), channel_id=1, source_target_pairs={{0,226},{1,227},{2,224},{3,225},{4,230},{5,231},{6,228},{7,229},{8... | collective-permute-start | bytes 196616 | tf_op jit(solution)/shard_map/ppermute | solution.py:284
  133.6 1.1 collective-permute-start.12
  134.7 0.7 forward.5
  135.4 0.9 squares.3.refs_8_
  136.3 0.5 grams.1
  136.8 1.1 collective-permute-done.11.refs_0_
  137.9 0.6 collective-permute-done.12.refs_1_
  138.5 0.1 combine.3
  138.6 20.8 %all_to_all.34 = bf16[8,32,1024]{2,1,0:T(8,128)(2,1)S(1)} all-to-all(bf16[8,32,1024]{2,1,0:T(8,128)(2,1)S(1)} %get-tuple-element.114), channel_id=1, replica_groups={{0,4,8,12,16,20,24,28},{1,5,9,13,17,21,25,29},{2,6,10,14,18,22,26,30},{..., dimensions={0} | all-to-all | bytes 1048576 | tf_op jit(solution)/shard_map/all_to_all | solution.py:267
  159.3 0.1 collective-permute-start.15
  159.4 1.8 last_back.1
  161.2 1.9 %collective-permute-done.15.refs_1_ = bf16[8,1024]{1,0:T(8,128)(2,1)S(1)} collective-permute-done((bf16[8,1024]{1,0:T(8,128)(2,1)S(1)}, bf16[8,1024]{1,0:T(8,128)(2,1)S(1)}, u32[]{:S(2)}, u32[]{:S(2)}) %collective-permute-start.15) | collective-permute-done | bytes 16416 | tf_op jit(solution)/shard_map/ppermute | solution.py:284
  163.1 21.3 %all_to_all.35.arrived_ref = bf16[32,8,1152]{2,1,0:T(8,128)(2,1)S(1)} all-to-all(bf16[32,8,1152]{2,1,0:T(8,128)(2,1)S(1)} %bitcast.50), channel_id=1, replica_groups=mesh['section'=8,'tensor'=32] {'tensor'}, dimensions={0} | all-to-all | bytes 1179648 | tf_op jit(solution)/shard_map/all_to_all | solution.py:261
  184.5 0.7 last_add_up.1
  185.2 5.8 %final.1 = (bf16[1024,1024]{1,0:T(8,128)(2,1)}, bf16[1024,1024]{1,0:T(8,128)(2,1)}) custom-call(s32[2,3]{1,0:T(2,128)S(1)} %bitcast.56, f32[1,128]{1,0:T(1,128)S(1)} %get-tuple-element.127.refs_1_, bf16[256,1024]{1,0:T(8,128)(2,1)S(1)} %bitcast.46, bf16[256,1024]{1,0:T(8,128)(2,1)S(1)} %bitcast.49, bf16[256,1024]{1,0:T(8,128)(2,1)S(1)} %bitcast.43, ...), custom_call_target="tpu_custom_call" | custom-call | flops 3221225472 | bytes 4194304 | tf_op jit(solution)/shard_map/final/pallas_call | solution.py:245
  (19 shorter events, 0.1 us)
Async XLA Ops:
  0.6 44.7 %copy-start = (bf16[1,1024,1024]{2,1,0:T(8,128)(2,1)S(1)}, bf16[1,1024,1024]{2,1,0:T(8,128)(2,1)}, u32[]{:S(2)}) copy-start(bf16[1,1024,1024]{2,1,0:T(8,128)(2,1)} %param.12) | copy-start | bytes 6291460
  28.5 0.8 copy-start.3
  29.3 12.2 %collective-permute-start.2 = (bf16[8,8,2048]{2,1,0:T(8,128)(2,1)S(1)}, bf16[8,8,2048]{2,1,0:T(8,128)(2,1)S(1)}, u32[]{:S(2)}, u32[]{:S(2)}) collective-permute-start(bf16[8,8,2048]{2,1,0:T(8,128)(2,1)S(1)} %get-tuple-element.68.refs_0_), channel_id=1, source_target_pairs={{0,3},{1,0},{2,1},{3,2},{4,7},{5,4},{6,5},{7,6},{8,11},{9,8},{10,9... | collective-permute-start | bytes 786440 | tf_op jit(solution)/shard_map/ppermute | solution.py:284
  32.2 10.4 %collective-permute-start.1 = (bf16[8,8,2048]{2,1,0:T(8,128)(2,1)S(1)}, bf16[8,8,2048]{2,1,0:T(8,128)(2,1)S(1)}, u32[]{:S(2)}, u32[]{:S(2)}) collective-permute-start(bf16[8,8,2048]{2,1,0:T(8,128)(2,1)S(1)} %get-tuple-element.68.refs_0_), channel_id=1, source_target_pairs={{0,2},{1,3},{2,0},{3,1},{4,6},{5,7},{6,4},{7,5},{8,10},{9,11},{10,... | collective-permute-start | bytes 786440 | tf_op jit(solution)/shard_map/ppermute | solution.py:284
  33.0 12.3 %collective-permute-start = (bf16[8,8,2048]{2,1,0:T(8,128)(2,1)S(1)}, bf16[8,8,2048]{2,1,0:T(8,128)(2,1)S(1)}, u32[]{:S(2)}, u32[]{:S(2)}) collective-permute-start(bf16[8,8,2048]{2,1,0:T(8,128)(2,1)S(1)} %get-tuple-element.68.refs_0_), channel_id=1, source_target_pairs={{0,1},{1,2},{2,3},{3,0},{4,5},{5,6},{6,7},{7,4},{8,9},{9,10},{10,1... | collective-permute-start | bytes 786440 | tf_op jit(solution)/shard_map/ppermute | solution.py:284
  45.4 1.6 copy-start.1
  69.5 16.9 %copy-start.4 = (s32[1,3,2]{1,2,0:T(2,128)S(1)}, s32[1,3,2]{1,2,0:T(2,128)}, u32[]{:S(2)}) copy-start(s32[1,3,2]{1,2,0:T(2,128)} %param.9) | copy-start | bytes 76
  69.5 10.0 %collective-permute-start.6 = (bf16[9,8,2048]{2,1,0:T(8,128)(2,1)S(1)}, bf16[9,8,2048]{2,1,0:T(8,128)(2,1)S(1)}, u32[]{:S(2)}, u32[]{:S(2)}) collective-permute-start(bf16[9,8,2048]{2,1,0:T(8,128)(2,1)S(1)} %get-tuple-element.80.refs_0_), channel_id=1, source_target_pairs={{0,3},{1,0},{2,1},{3,2},{4,7},{5,4},{6,5},{7,6},{8,11},{9,8},{10,9... | collective-permute-start | bytes 884744 | tf_op jit(solution)/shard_map/ppermute | solution.py:284
  69.6 11.5 %collective-permute-start.5 = (bf16[9,8,2048]{2,1,0:T(8,128)(2,1)S(1)}, bf16[9,8,2048]{2,1,0:T(8,128)(2,1)S(1)}, u32[]{:S(2)}, u32[]{:S(2)}) collective-permute-start(bf16[9,8,2048]{2,1,0:T(8,128)(2,1)S(1)} %get-tuple-element.80.refs_0_), channel_id=1, source_target_pairs={{0,2},{1,3},{2,0},{3,1},{4,6},{5,7},{6,4},{7,5},{8,10},{9,11},{10,... | collective-permute-start | bytes 884744 | tf_op jit(solution)/shard_map/ppermute | solution.py:284
  70.5 15.0 %collective-permute-start.4 = (bf16[9,8,2048]{2,1,0:T(8,128)(2,1)S(1)}, bf16[9,8,2048]{2,1,0:T(8,128)(2,1)S(1)}, u32[]{:S(2)}, u32[]{:S(2)}) collective-permute-start(bf16[9,8,2048]{2,1,0:T(8,128)(2,1)S(1)} %get-tuple-element.80.refs_0_), channel_id=1, source_target_pairs={{0,1},{1,2},{2,3},{3,0},{4,5},{5,6},{6,7},{7,4},{8,9},{9,10},{10,1... | collective-permute-start | bytes 884744 | tf_op jit(solution)/shard_map/ppermute | solution.py:284
  71.8 15.5 %collective-permute-start.3 = (bf16[32,2048]{1,0:T(8,128)(2,1)S(1)}, bf16[32,2048]{1,0:T(8,128)(2,1)S(1)}, u32[]{:S(2)}, u32[]{:S(2)}) collective-permute-start(bf16[32,2048]{1,0:T(8,128)(2,1)S(1)} %get-tuple-element.76), channel_id=1, source_target_pairs={{0,224},{1,225},{2,226},{3,227},{4,228},{5,229},{6,230},{7,231},{8... | collective-permute-start | bytes 393224 | tf_op jit(solution)/shard_map/ppermute | solution.py:284
  71.8 15.5 %collective-permute-start.9 = (bf16[32,1024]{1,0:T(8,128)(2,1)S(1)}, bf16[32,1024]{1,0:T(8,128)(2,1)S(1)}, u32[]{:S(2)}, u32[]{:S(2)}) collective-permute-start(bf16[32,1024]{1,0:T(8,128)(2,1)S(1)} %get-tuple-element.77), channel_id=1, source_target_pairs={{0,227},{1,224},{2,225},{3,226},{4,231},{5,228},{6,229},{7,230},{8... | collective-permute-start | bytes 196616 | tf_op jit(solution)/shard_map/ppermute | solution.py:284
  79.5 7.8 %collective-permute-start.8 = (bf16[32,1024]{1,0:T(8,128)(2,1)S(1)}, bf16[32,1024]{1,0:T(8,128)(2,1)S(1)}, u32[]{:S(2)}, u32[]{:S(2)}) collective-permute-start(bf16[32,1024]{1,0:T(8,128)(2,1)S(1)} %get-tuple-element.77), channel_id=1, source_target_pairs={{0,226},{1,227},{2,224},{3,225},{4,230},{5,231},{6,228},{7,229},{8... | collective-permute-start | bytes 196616 | tf_op jit(solution)/shard_map/ppermute | solution.py:284
  81.1 6.1 %collective-permute-start.7 = (bf16[32,1024]{1,0:T(8,128)(2,1)S(1)}, bf16[32,1024]{1,0:T(8,128)(2,1)S(1)}, u32[]{:S(2)}, u32[]{:S(2)}) collective-permute-start(bf16[32,1024]{1,0:T(8,128)(2,1)S(1)} %get-tuple-element.77), channel_id=1, source_target_pairs={{0,225},{1,226},{2,227},{3,224},{4,229},{5,230},{6,231},{7,228},{8... | collective-permute-start | bytes 196616 | tf_op jit(solution)/shard_map/ppermute | solution.py:284
  86.3 19.9 %copy-start.2 = (bf16[1,1024,1024]{2,1,0:T(8,128)(2,1)S(1)}, bf16[1,1024,1024]{2,1,0:T(8,128)(2,1)}, u32[]{:S(2)}) copy-start(bf16[1,1024,1024]{2,1,0:T(8,128)(2,1)} %param.13) | copy-start | bytes 6291460
  129.5 8.3 %collective-permute-start.10 = (bf16[32,2048]{1,0:T(8,128)(2,1)S(1)}, bf16[32,2048]{1,0:T(8,128)(2,1)S(1)}, u32[]{:S(2)}, u32[]{:S(2)}) collective-permute-start(bf16[32,2048]{1,0:T(8,128)(2,1)S(1)} %get-tuple-element.98), channel_id=1, source_target_pairs={{0,224},{1,225},{2,226},{3,227},{4,228},{5,229},{6,230},{7,231},{8... | collective-permute-start | bytes 393224 | tf_op jit(solution)/shard_map/ppermute | solution.py:284
  129.7 8.2 %collective-permute-start.14 = (bf16[32,1024]{1,0:T(8,128)(2,1)S(1)}, bf16[32,1024]{1,0:T(8,128)(2,1)S(1)}, u32[]{:S(2)}, u32[]{:S(2)}) collective-permute-start(bf16[32,1024]{1,0:T(8,128)(2,1)S(1)} %get-tuple-element.99), channel_id=1, source_target_pairs={{0,227},{1,224},{2,225},{3,226},{4,231},{5,228},{6,229},{7,230},{8... | collective-permute-start | bytes 196616 | tf_op jit(solution)/shard_map/ppermute | solution.py:284
  129.8 8.1 %collective-permute-start.13 = (bf16[32,1024]{1,0:T(8,128)(2,1)S(1)}, bf16[32,1024]{1,0:T(8,128)(2,1)S(1)}, u32[]{:S(2)}, u32[]{:S(2)}) collective-permute-start(bf16[32,1024]{1,0:T(8,128)(2,1)S(1)} %get-tuple-element.99), channel_id=1, source_target_pairs={{0,226},{1,227},{2,224},{3,225},{4,230},{5,231},{6,228},{7,229},{8... | collective-permute-start | bytes 196616 | tf_op jit(solution)/shard_map/ppermute | solution.py:284
  133.6 4.9 %collective-permute-start.12 = (bf16[32,1024]{1,0:T(8,128)(2,1)S(1)}, bf16[32,1024]{1,0:T(8,128)(2,1)S(1)}, u32[]{:S(2)}, u32[]{:S(2)}) collective-permute-start(bf16[32,1024]{1,0:T(8,128)(2,1)S(1)} %get-tuple-element.99), channel_id=1, source_target_pairs={{0,225},{1,226},{2,227},{3,224},{4,229},{5,230},{6,231},{7,228},{8... | collective-permute-start | bytes 196616 | tf_op jit(solution)/shard_map/ppermute | solution.py:284
  134.7 3.2 %collective-permute-start.11 = (bf16[8,1024]{1,0:T(8,128)(2,1)S(1)}, bf16[8,1024]{1,0:T(8,128)(2,1)S(1)}, u32[]{:S(2)}, u32[]{:S(2)}) collective-permute-start(bf16[8,1024]{1,0:T(8,128)(2,1)S(1)} %get-tuple-element.109), channel_id=1, source_target_pairs={{0,32},{1,33},{2,34},{3,35},{4,36},{5,37},{6,38},{7,39},{8,40},{9,... | collective-permute-start | bytes 49160 | tf_op jit(solution)/shard_map/ppermute | solution.py:284
  159.3 3.8 %collective-permute-start.15 = (bf16[8,1024]{1,0:T(8,128)(2,1)S(1)}, bf16[8,1024]{1,0:T(8,128)(2,1)S(1)}, u32[]{:S(2)}, u32[]{:S(2)}) collective-permute-start(bf16[8,1024]{1,0:T(8,128)(2,1)S(1)} %get-tuple-element.123), channel_id=1, source_target_pairs={{0,32},{1,33},{2,34},{3,35},{4,36},{5,37},{6,38},{7,39},{8,40},{9,... | collective-permute-start | bytes 49160 | tf_op jit(solution)/shard_map/ppermute | solution.py:284

commit v6 on v4

--- a/solution.py
+++ b/solution.py
@@ -88,15 +88,7 @@
             out_ref[:, pl.ds(source, 1)] = block_ref[:, :, D * place : D * (place + 1)][:, None]
 
 
-def spread_kernel(sections, place, shifted_ref, loss_ref, blocks_ref, rows_ref):
-    last = (lax.axis_index("section") == sections - 1).astype(jnp.int32)
-    chosen = jnp.where(jnp.full(rows_ref.shape, last) > 0, loss_ref[place], shifted_ref[...])
-    rows_ref[...] = chosen
-    blocks_ref[...] = jnp.broadcast_to(chosen[None], blocks_ref.shape)
-
-
-def forward_kernel(x_ref, weights_ref, *refs):
-    slope_ref, hidden_ref = refs[-2:]
+def forward_kernel(x_ref, weights_ref, slope_ref, hidden_ref):
     x = x_ref[...]
     for cols in parts(weights_ref.shape[1]):
         relu = jnp.maximum(mm(x, weights_ref[:, cols]), 0.0)
@@ -161,16 +153,20 @@
     gram_h_ref[...] = nt(hidden, hidden)
 
 
-def sum_kernel(arrived_ref, incoming_ref, passing_ref):
-    total = incoming_ref[...].astype(F32)
+def sum_kernel(place, arrived_ref, grads_ref, loss_ref, passing_ref, blocks_ref):
+    total = grads_ref[lax.axis_index("tensor")].astype(F32)
     for peer in range(arrived_ref.shape[0]):
         total = total + arrived_ref[peer].astype(F32)
-    passing_ref[...] = total.astype(BF16)
-
-
-def last_sum_kernel(arrived_ref, incoming_ref, *refs):
+    passing = total.astype(BF16)
+    passing_ref[...] = passing
+    first = (lax.axis_index("section") == 0).astype(jnp.int32)
+    chosen = jnp.where(jnp.full(passing.shape, first) > 0, loss_ref[place], passing)
+    blocks_ref[...] = jnp.broadcast_to(chosen[None], blocks_ref.shape)
+
+
+def last_sum_kernel(arrived_ref, grads_ref, *refs):
     *earlier_refs, results_ref, line_ref = refs
-    total = incoming_ref[...].astype(F32)
+    total = grads_ref[lax.axis_index("tensor")].astype(F32)
     line = jnp.zeros(line_ref.shape, F32)
     for peer in range(arrived_ref.shape[0]):
         total = total + arrived_ref[peer, :, :D].astype(F32)
@@ -239,18 +235,34 @@
     return lax.all_to_all(blocks, "tensor", split_axis=0, concat_axis=0, tiled=True)
 
 
-def gather_along_x(block):
+def exchange_along_z(blocks):
     count = lax.axis_size("tensor")
-    blocks = [block]
-    for distance in range(1, ALONG_X):
-        pairs = [
-            (at, at // ALONG_X * ALONG_X + (at + distance) % ALONG_X) for at in range(count)
-        ]
-        blocks.append(lax.ppermute(block, "tensor", pairs))
-    along_z, rows, width = block.shape
+    groups = [list(range(x, count, ALONG_X)) for x in range(ALONG_X)]
+    return lax.all_to_all(
+        blocks, "tensor", split_axis=0, concat_axis=0, axis_index_groups=groups, tiled=True
+    )
+
+
+def moved(value, sections_back, distance):
+    sections, count = lax.axis_size("section"), lax.axis_size("tensor")
+    pairs = [
+        (
+            section * count + at,
+            (section - sections_back) % sections * count
+            + at // ALONG_X * ALONG_X
+            + (at + distance) % ALONG_X,
+        )
+        for section in range(sections)
+        for at in range(count)
+    ]
+    return lax.ppermute(value, ("section", "tensor"), pairs)
+
+
+def assemble(blocks):
+    along_z, rows, width = blocks[0].shape
     outs = (shape(along_z, ALONG_X, rows, D),) * (width // D)
     gathered = call(assemble_kernel, outs, blocks, 0, "assemble")
-    return [out.reshape(count * rows, D) for out in gathered]
+    return [out.reshape(along_z * ALONG_X * rows, D) for out in gathered]
 
 
 def per_device(saved_inputs, slot_index, example_lengths, first_grads, loss_grads, w_in, w_out):
@@ -280,20 +292,19 @@
         name="start",
         compiler_params=pltpu.CompilerParams(vmem_limit_bytes=60 * MIB),
     )(slot_index, saved_inputs[0], incoming)
-    groups = [[z * ALONG_X + x for z in range(along_z)] for x in range(ALONG_X)]
-    begun = lax.all_to_all(
-        blocks, "tensor", split_axis=0, concat_axis=0, axis_index_groups=groups, tiled=True
-    )
+    begun = exchange_along_z(blocks)
     halves = (shape(along_z, rows, 2 * D), shape(along_z, rows, (slots - 1) * D))
     urgent, later = call(split_kernel, halves, (begun,), 0, "split")
-    x, grads = gather_along_x(urgent)
-    later = gather_along_x(later)
-
-    def forward(x, *early):
+    urgent, loss = lax.optimization_barrier((urgent, loss_grads))
+    blocks = [urgent] + [moved(urgent, 0, distance) for distance in range(1, ALONG_X)]
+    blocks[0], loss = lax.optimization_barrier((blocks[0], moved(loss, -1, 0)))
+    x, grads = assemble(blocks)
+
+    def forward(x):
         outs = (shape(tokens, units, dtype=F32), shape(tokens, units))
-        return call(forward_kernel, outs, (x, first, *early), product, "forward")
-
-    slope, hidden = forward(x, second)
+        return call(forward_kernel, outs, (x, first), product, "forward")
+
+    slope, hidden = forward(x)
     xs, hiddens, dzs, dys, results, squares = [], [], [], [], [], []
     for slot in range(slots):
         xs.append(x)
@@ -310,36 +321,41 @@
         )
         dzs.append(dz)
         arrived = exchange(share.reshape(count, rows, D))
-        passing = call(sum_kernel, shape(rows, D), (arrived, incoming), tokens * D, "add_up")
+        held = (x, hidden, grads, dz)
+        if slot == 0:
+            blocks = [later] + [moved(later, 0, distance) for distance in range(1, ALONG_X)]
+            arrived, *later = lax.optimization_barrier((arrived, *assemble(blocks)))
+        passing, blocks = call(
+            lambda *refs, slot=slot: sum_kernel(slot, *refs),
+            (shape(rows, D), shape(along_z, rows, D)),
+            (arrived, grads.reshape(count, rows, D), loss),
+            tokens * D,
+            "add_up",
+        )
         results.append(passing)
-        shifted = lax.ppermute(
-            passing, "section", [(source, source - 1) for source in range(1, sections)]
-        )
-        held = lax.optimization_barrier((passing, x, hidden, grads, dz, later[slot]))
+        block = exchange_along_z(blocks)
+        pieces = [moved(block, 1, distance) for distance in range(ALONG_X)]
+        *late, x = lax.optimization_barrier((block, *held, later[slot]))
+        if slot:
+            held = late[1:]
         one = call(
             lambda *refs, slot=slot: squares_kernel(slot, *refs),
             shape(1, LANES, dtype=F32),
-            (lengths, *held[1:5]),
+            (lengths, *held),
             product,
             "squares",
         )
         squares.append(one)
-        x = held[5]
         slope, hidden = forward(x)
         ready = [one, slope, hidden]
         if slot + 2 == slots:
             ready += call(
                 grams_kernel, (shape(*square, dtype=F32),) * 2, (x, hidden), product // 4, "grams"
             )
-        shifted, squares[-1], slope, hidden, *grams = lax.optimization_barrier((shifted, *ready))
-        blocks, incoming = call(
-            lambda *refs, slot=slot: spread_kernel(sections, slot, *refs),
-            (shape(count, rows, D), shape(rows, D)),
-            (shifted, loss_grads),
-            0,
-            "spread",
-        )
-        grads = exchange(blocks).reshape(tokens, D)
+        pieces[0], squares[-1], slope, hidden, *grams = lax.optimization_barrier(
+            (pieces[0], *ready)
+        )
+        [grads] = assemble(pieces)
 
     dz, share = call(
         lambda *refs: last_back_kernel(slots - 1, *refs),
@@ -353,7 +369,7 @@
     results, totals = call(
         last_sum_kernel,
         (shape(slots, rows, D), shape(1, LANES, dtype=F32)),
-        (arrived, incoming, *results),
+        (arrived, grads.reshape(count, rows, D), *results),
         tokens * D,
         "last_add_up",
     )

time: 191 us -> 183 us (0.958)
  blocking collectives: 119 us -> 101 us
  starting transfers between devices: 17.7 us -> 23.6 us
  waiting for transfers between devices: 28.4 us -> 31 us
    all_to_all x4 -> x2, blocking collectives: 92.6 us -> 48.3 us  [exchange(): lax.all_to_all(blocks, 'tensor', split_axis=0, concat_axis=0, tiled=True)]
    all_to_all x1 -> x3, blocking collectives: 26 us -> 53 us  [exchange_along_z(): lax.all_to_all(blocks, 'tensor', split_axis=0, concat_axis=0, axis_index_...]
    ppermute x8 -> x15, starting transfers between devices: 13 us -> 18.9 us  [moved(): return lax.ppermute(value, ('section', 'tensor'), pairs)]
    ppermute x8 -> x15, waiting for transfers between devices: 28.4 us -> 31 us  [moved(): return lax.ppermute(value, ('section', 'tensor'), pairs)]
    unnamed x30 -> x32, local copies, waits for them, and re-layouts: 5.67 us -> 4.86 us
  transfers between devices with their start and end apart: 9 -> 16, of which waited for: 5 -> 9; matrix products, arithmetic and copies ran while one was open for 0% -> 0% of each run, Pallas kernels for 2% -> 2%
where the time goes in v6:
time: 183 us; the launch traced here: 181 us
  blocking collectives  101 us (55%)
  waiting for transfers between devices  31 us (17%)
  starting transfers between devices  23.6 us (13%)
  Pallas kernels  19.5 us (11%)
  local copies, waits for them, and re-layouts  4.86 us (3%)
    all_to_all x3, blocking collectives, exchange_along_z(): lax.all_to_all(blocks, 'tensor', split_axis=0, concat_axis=0, axis_index_...  53 us
    all_to_all x2, blocking collectives, exchange(): lax.all_to_all(blocks, 'tensor', split_axis=0, concat_axis=0, tiled=True)  48.3 us
    ppermute x15, waiting for transfers between devices, moved(): return lax.ppermute(value, ('section', 'tensor'), pairs)  31 us
    ppermute x15, starting transfers between devices, moved(): return lax.ppermute(value, ('section', 'tensor'), pairs)  18.9 us
    pallas_call x17, Pallas kernels, call(): pl.pallas_call(kernel, out_shape=outs, in_specs=[VMEM] * len(operands), o...  11.8 us
    pallas_call x1, Pallas kernels, final_products(): pl.pallas_call(lambda *refs: final_kernel(slots, *refs), grid=(rows // bl...  5.81 us
    unnamed x32, local copies, waits for them, and re-layouts  4.86 us
    all_to_all x1, starting transfers between devices, exchange(): lax.all_to_all(blocks, 'tensor', split_axis=0, concat_axis=0, tiled=True)  4.75 us
  transfers between devices with their start and end apart: 16, of which 9 were waited for; matrix products, arithmetic and copies ran while one was open for 0% of the time, Pallas kernels for 2%

profile of v6, /device:TPU:8, one launch (start us, length us, event | category | flops | bytes accessed | tf_op | source)
XLA Modules:
  0.0 181.1 jit_solution(13911649919401387436)
XLA Ops:
  0.7 1.9 %start.1 = bf16[8,8,4096]{2,1,0:T(8,128)(2,1)} custom-call(s32[1,3]{1,0:T(1,128)} %index.1, bf16[4,8,1024]{2,1,0:T(8,128)(2,1)} %bitcast.57, bf16[8,1024]{1,0:T(8,128)(2,1)} %bitcast.58), custom_call_target="tpu_custom_call" | custom-call | tf_op jit(solution)/shard_map/start/pallas_call | solution.py:281
  2.6 26.0 %all_to_all.30.begun_ref = bf16[8,8,4096]{2,1,0:T(8,128)(2,1)S(1)} all-to-all(bf16[8,8,4096]{2,1,0:T(8,128)(2,1)} %start.1), channel_id=1, replica_groups={{0,4,8,12,16,20,24,28},{1,5,9,13,17,21,25,29},{2,6,10,14,18,22,26,30},{..., dimensions={0} | all-to-all | bytes 1048576 | tf_op jit(solution)/shard_map/all_to_all | solution.py:241
  28.6 2.8 %collective-permute-start.3 = (bf16[8,8,2048]{2,1,0:T(8,128)(2,1)S(1)}, bf16[8,8,2048]{2,1,0:T(8,128)(2,1)S(1)}, u32[]{:S(2)}, u32[]{:S(2)}) collective-permute-start(bf16[8,8,2048]{2,1,0:T(8,128)(2,1)S(1)} %get-tuple-element.57.refs_0_), channel_id=1, source_target_pairs={{0,3},{1,0},{2,1},{3,2},{4,7},{5,4},{6,5},{7,6},{8,11},{9,8},{10,9... | collective-permute-start | bytes 786440 | tf_op jit(solution)/shard_map/ppermute | solution.py:258
  31.4 0.8 collective-permute-start.2
  32.2 0.9 collective-permute-start.1
  33.1 3.3 %collective-permute-done.refs_2_ = bf16[2,8,1024]{2,1,0:T(8,128)(2,1)S(1)} collective-permute-done((bf16[2,8,1024]{2,1,0:T(8,128)(2,1)S(1)}, bf16[2,8,1024]{2,1,0:T(8,128)(2,1)S(1)}, u32[]{:S(2)}, u32[]{:S(2)}) %collective-permute-start) | collective-permute-done | bytes 32800 | tf_op jit(solution)/shard_map/ppermute | solution.py:258
  36.5 4.4 %collective-permute-done.3.refs_3_ = bf16[8,8,2048]{2,1,0:T(8,128)(2,1)S(1)} collective-permute-done((bf16[8,8,2048]{2,1,0:T(8,128)(2,1)S(1)}, bf16[8,8,2048]{2,1,0:T(8,128)(2,1)S(1)}, u32[]{:S(2)}, u32[]{:S(2)}) %collective-permute-start.3) | collective-permute-done | bytes 262176 | tf_op jit(solution)/shard_map/ppermute | solution.py:258
  40.8 1.0 collective-permute-done.2.refs_2_
  41.8 2.7 %collective-permute-done.1.refs_1_ = bf16[8,8,2048]{2,1,0:T(8,128)(2,1)S(1)} collective-permute-done((bf16[8,8,2048]{2,1,0:T(8,128)(2,1)S(1)}, bf16[8,8,2048]{2,1,0:T(8,128)(2,1)S(1)}, u32[]{:S(2)}, u32[]{:S(2)}) %collective-permute-start.1) | collective-permute-done | bytes 262176 | tf_op jit(solution)/shard_map/ppermute | solution.py:258
  44.5 0.1 assemble.4
  44.6 0.7 forward.3
  45.4 2.1 %back.2 = (bf16[256,1024]{1,0:T(8,128)(2,1)S(1)}, bf16[256,1024]{1,0:T(8,128)(2,1)}) custom-call(bf16[256,1024]{1,0:T(8,128)(2,1)S(1)} %bitcast.38, f32[256,1024]{1,0:T(8,128)S(1)} %get-tuple-element.60.slope_ref, bf16[1024,1024]{1,0:T(8,128)(2,1)S(1)} %bitcast.28, bf16[1024,1024]{1,0:T(8,128)(2,1)S(1)} %bitcast.23), custom_call_target="tpu_custom_call" | custom-call | flops 1073741824 | bytes 1048576 | tf_op jit(solution)/shard_map/back/pallas_call | solution.py:27
  47.5 0.8 copy-done.11
  48.3 4.8 %all-to-all-start.1 = ((bf16[32,8,1024]{2,1,0:T(8,128)(2,1)}), bf16[32,8,1024]{2,1,0:T(8,128)(2,1)}, u32[]{:S(2)}, u32[]{:S(2)}) async-start(bf16[32,8,1024]{2,1,0:T(8,128)(2,1)} %bitcast.9), calls=%async_computation.1 | async-start | bytes 1048576 | tf_op jit(solution)/shard_map/all_to_all | solution.py:235
  53.0 2.9 %collective-permute-start.6 = (bf16[8,8,2048]{2,1,0:T(8,128)(2,1)S(1)}, bf16[8,8,2048]{2,1,0:T(8,128)(2,1)S(1)}, u32[]{:S(2)}, u32[]{:S(2)}) collective-permute-start(bf16[8,8,2048]{2,1,0:T(8,128)(2,1)S(1)} %get-tuple-element.62.refs_0_), channel_id=1, source_target_pairs={{0,3},{1,0},{2,1},{3,2},{4,7},{5,4},{6,5},{7,6},{8,11},{9,8},{10,9... | collective-permute-start | bytes 786440 | tf_op jit(solution)/shard_map/ppermute | solution.py:258
  55.9 0.8 collective-permute-start.5
  56.8 0.9 collective-permute-start.4
  57.7 13.7 %collective-permute-done.6.refs_3_ = bf16[8,8,2048]{2,1,0:T(8,128)(2,1)S(1)} collective-permute-done((bf16[8,8,2048]{2,1,0:T(8,128)(2,1)S(1)}, bf16[8,8,2048]{2,1,0:T(8,128)(2,1)S(1)}, u32[]{:S(2)}, u32[]{:S(2)}) %collective-permute-start.6) | collective-permute-done | bytes 262176 | tf_op jit(solution)/shard_map/ppermute | solution.py:258
  71.4 3.3 %collective-permute-done.4.refs_1_ = bf16[8,8,2048]{2,1,0:T(8,128)(2,1)S(1)} collective-permute-done((bf16[8,8,2048]{2,1,0:T(8,128)(2,1)S(1)}, bf16[8,8,2048]{2,1,0:T(8,128)(2,1)S(1)}, u32[]{:S(2)}, u32[]{:S(2)}) %collective-permute-start.4) | collective-permute-done | bytes 262176 | tf_op jit(solution)/shard_map/ppermute | solution.py:258
  74.8 0.8 copy-done.6
  75.6 1.2 add_up.2
  76.7 15.0 %all_to_all.31 = bf16[8,8,1024]{2,1,0:T(8,128)(2,1)S(1)} all-to-all(bf16[8,8,1024]{2,1,0:T(8,128)(2,1)S(1)} %get-tuple-element.67), channel_id=1, replica_groups={{0,4,8,12,16,20,24,28},{1,5,9,13,17,21,25,29},{2,6,10,14,18,22,26,30},{..., dimensions={0} | all-to-all | bytes 262144 | tf_op jit(solution)/shard_map/all_to_all | solution.py:241
  91.7 0.3 collective-permute-start.10
  92.0 1.7 collective-permute-start.9
  93.7 1.9 %collective-permute-start.8 = (bf16[8,8,1024]{2,1,0:T(8,128)(2,1)S(1)}, bf16[8,8,1024]{2,1,0:T(8,128)(2,1)S(1)}, u32[]{:S(2)}, u32[]{:S(2)}) collective-permute-start(bf16[8,8,1024]{2,1,0:T(8,128)(2,1)S(1)} %all_to_all.31), channel_id=1, source_target_pairs={{0,225},{1,226},{2,227},{3,224},{4,229},{5,230},{6,231},{7,228},{8... | collective-permute-start | bytes 393224 | tf_op jit(solution)/shard_map/ppermute | solution.py:258
  95.7 1.0 copy-done.4
  96.7 1.0 copy-done.9
  97.8 1.0 copy-done.12
  98.8 0.9 squares.2.refs_7_
  99.7 0.7 forward.4
  100.5 0.7 collective-permute-done.8.refs_1_
  101.2 0.1 copy-done.2
  101.3 1.3 back.3
  102.6 23.2 %all_to_all.32.refs_0_ = bf16[32,8,1024]{2,1,0:T(8,128)(2,1)S(1)} all-to-all(bf16[32,8,1024]{2,1,0:T(8,128)(2,1)S(1)} %bitcast.52), channel_id=1, replica_groups=mesh['section'=8,'tensor'=32] {'tensor'}, dimensions={0} | all-to-all | bytes 1048576 | tf_op jit(solution)/shard_map/all_to_all | solution.py:235
  125.8 0.1 add_up.3
  125.9 12.0 %all_to_all.33 = bf16[8,8,1024]{2,1,0:T(8,128)(2,1)S(1)} all-to-all(bf16[8,8,1024]{2,1,0:T(8,128)(2,1)S(1)} %get-tuple-element.77), channel_id=1, replica_groups={{0,4,8,12,16,20,24,28},{1,5,9,13,17,21,25,29},{2,6,10,14,18,22,26,30},{..., dimensions={0} | all-to-all | bytes 262144 | tf_op jit(solution)/shard_map/all_to_all | solution.py:241
  137.9 2.2 %collective-permute-start.14 = (bf16[8,8,1024]{2,1,0:T(8,128)(2,1)S(1)}, bf16[8,8,1024]{2,1,0:T(8,128)(2,1)S(1)}, u32[]{:S(2)}, u32[]{:S(2)}) collective-permute-start(bf16[8,8,1024]{2,1,0:T(8,128)(2,1)S(1)} %all_to_all.33), channel_id=1, source_target_pairs={{0,227},{1,224},{2,225},{3,226},{4,231},{5,228},{6,229},{7,230},{8... | collective-permute-start | bytes 393224 | tf_op jit(solution)/shard_map/ppermute | solution.py:258
  140.1 1.5 collective-permute-start.13
  141.6 2.1 %collective-permute-start.12 = (bf16[8,8,1024]{2,1,0:T(8,128)(2,1)S(1)}, bf16[8,8,1024]{2,1,0:T(8,128)(2,1)S(1)}, u32[]{:S(2)}, u32[]{:S(2)}) collective-permute-start(bf16[8,8,1024]{2,1,0:T(8,128)(2,1)S(1)} %all_to_all.33), channel_id=1, source_target_pairs={{0,225},{1,226},{2,227},{3,224},{4,229},{5,230},{6,231},{7,228},{8... | collective-permute-start | bytes 393224 | tf_op jit(solution)/shard_map/ppermute | solution.py:258
  143.7 0.7 forward.5
  144.4 0.5 grams.1
  144.9 0.9 squares.3.refs_8_
  145.8 0.2 collective-permute-done.13.refs_2_
  146.0 1.6 collective-permute-done.12.refs_1_
  147.7 1.8 last_back.1
  149.5 25.1 %all_to_all.34.arrived_ref = bf16[32,8,1152]{2,1,0:T(8,128)(2,1)S(1)} all-to-all(bf16[32,8,1152]{2,1,0:T(8,128)(2,1)S(1)} %bitcast.51), channel_id=1, replica_groups=mesh['section'=8,'tensor'=32] {'tensor'}, dimensions={0} | all-to-all | bytes 1179648 | tf_op jit(solution)/shard_map/all_to_all | solution.py:235
  174.6 0.7 last_add_up.1
  175.3 5.8 %final.1 = (bf16[1024,1024]{1,0:T(8,128)(2,1)}, bf16[1024,1024]{1,0:T(8,128)(2,1)}) custom-call(s32[2,3]{1,0:T(2,128)S(1)} %bitcast.56, f32[1,128]{1,0:T(1,128)S(1)} %get-tuple-element.99.refs_1_, bf16[256,1024]{1,0:T(8,128)(2,1)S(1)} %bitcast.47, bf16[256,1024]{1,0:T(8,128)(2,1)S(1)} %bitcast.50, bf16[256,1024]{1,0:T(8,128)(2,1)S(1)} %bitcast.44, ...), custom_call_target="tpu_custom_call" | custom-call | flops 3221225472 | bytes 4194304 | tf_op jit(solution)/shard_map/final/pallas_call | solution.py:219
  (40 shorter events, 0.3 us)
Async XLA Ops:
  0.6 32.5 %copy-start.15 = (bf16[2,8,1024]{2,1,0:T(8,128)(2,1)S(1)}, bf16[2,8,1024]{2,1,0:T(8,128)(2,1)}, u32[]{:S(2)}) copy-start(bf16[2,8,1024]{2,1,0:T(8,128)(2,1)} %param.11) | copy-start | bytes 98308
  0.6 44.0 %copy-start = (bf16[1,1024,1024]{2,1,0:T(8,128)(2,1)S(1)}, bf16[1,1024,1024]{2,1,0:T(8,128)(2,1)}, u32[]{:S(2)}) copy-start(bf16[1,1024,1024]{2,1,0:T(8,128)(2,1)} %param.12) | copy-start | bytes 6291460
  28.6 16.8 %copy-start.1 = (bf16[1,1024,1024]{2,1,0:T(8,128)(2,1)S(1)}, bf16[1,1024,1024]{2,1,0:T(8,128)(2,1)}, u32[]{:S(2)}) copy-start(bf16[1,1024,1024]{2,1,0:T(8,128)(2,1)} %param.13) | copy-start | bytes 6291460
  28.6 12.2 %collective-permute-start.3 = (bf16[8,8,2048]{2,1,0:T(8,128)(2,1)S(1)}, bf16[8,8,2048]{2,1,0:T(8,128)(2,1)S(1)}, u32[]{:S(2)}, u32[]{:S(2)}) collective-permute-start(bf16[8,8,2048]{2,1,0:T(8,128)(2,1)S(1)} %get-tuple-element.57.refs_0_), channel_id=1, source_target_pairs={{0,3},{1,0},{2,1},{3,2},{4,7},{5,4},{6,5},{7,6},{8,11},{9,8},{10,9... | collective-permute-start | bytes 786440 | tf_op jit(solution)/shard_map/ppermute | solution.py:258
  31.4 10.4 %collective-permute-start.2 = (bf16[8,8,2048]{2,1,0:T(8,128)(2,1)S(1)}, bf16[8,8,2048]{2,1,0:T(8,128)(2,1)S(1)}, u32[]{:S(2)}, u32[]{:S(2)}) collective-permute-start(bf16[8,8,2048]{2,1,0:T(8,128)(2,1)S(1)} %get-tuple-element.57.refs_0_), channel_id=1, source_target_pairs={{0,2},{1,3},{2,0},{3,1},{4,6},{5,7},{6,4},{7,5},{8,10},{9,11},{10,... | collective-permute-start | bytes 786440 | tf_op jit(solution)/shard_map/ppermute | solution.py:258
  32.2 12.3 %collective-permute-start.1 = (bf16[8,8,2048]{2,1,0:T(8,128)(2,1)S(1)}, bf16[8,8,2048]{2,1,0:T(8,128)(2,1)S(1)}, u32[]{:S(2)}, u32[]{:S(2)}) collective-permute-start(bf16[8,8,2048]{2,1,0:T(8,128)(2,1)S(1)} %get-tuple-element.57.refs_0_), channel_id=1, source_target_pairs={{0,1},{1,2},{2,3},{3,0},{4,5},{5,6},{6,7},{7,4},{8,9},{9,10},{10,1... | collective-permute-start | bytes 786440 | tf_op jit(solution)/shard_map/ppermute | solution.py:258
  33.1 3.3 %collective-permute-start = (bf16[2,8,1024]{2,1,0:T(8,128)(2,1)S(1)}, bf16[2,8,1024]{2,1,0:T(8,128)(2,1)S(1)}, u32[]{:S(2)}, u32[]{:S(2)}) collective-permute-start(bf16[2,8,1024]{2,1,0:T(8,128)(2,1)S(1)} %copy-done.15), channel_id=1, source_target_pairs={{0,32},{1,33},{2,34},{3,35},{4,36},{5,37},{6,38},{7,39},{8,40},{9,... | collective-permute-start | bytes 98312 | tf_op jit(solution)/shard_map/ppermute | solution.py:258
  44.6 2.9 %copy-start.3 = (bf16[8,4,8,1024]{3,2,1,0:T(8,128)(2,1)}, bf16[8,4,8,1024]{3,2,1,0:T(8,128)(2,1)S(1)}, u32[]{:S(2)}) copy-start(bf16[8,4,8,1024]{3,2,1,0:T(8,128)(2,1)S(1)} %get-tuple-element.59) | copy-start | bytes 1572868
  45.4 2.1 %copy-start.8 = (bf16[256,1024]{1,0:T(8,128)(2,1)}, bf16[256,1024]{1,0:T(8,128)(2,1)S(1)}, u32[]{:S(2)}) copy-start(bf16[256,1024]{1,0:T(8,128)(2,1)S(1)} %get-tuple-element.68.refs_2_.refs_5_) | copy-start | bytes 1572868
  47.5 0.8 copy-start.11
  48.3 47.4 %copy-start.14 = (s32[1,3,2]{1,2,0:T(2,128)S(1)}, s32[1,3,2]{1,2,0:T(2,128)}, u32[]{:S(2)}) copy-start(s32[1,3,2]{1,2,0:T(2,128)} %param.9) | copy-start | bytes 76
  48.3 27.3 %all-to-all-start.1 = ((bf16[32,8,1024]{2,1,0:T(8,128)(2,1)}), bf16[32,8,1024]{2,1,0:T(8,128)(2,1)}, u32[]{:S(2)}, u32[]{:S(2)}) async-start(bf16[32,8,1024]{2,1,0:T(8,128)(2,1)} %bitcast.9), calls=%async_computation.1 | async-start | bytes 1048576 | tf_op jit(solution)/shard_map/all_to_all | solution.py:235
  53.0 18.3 %collective-permute-start.6 = (bf16[8,8,2048]{2,1,0:T(8,128)(2,1)S(1)}, bf16[8,8,2048]{2,1,0:T(8,128)(2,1)S(1)}, u32[]{:S(2)}, u32[]{:S(2)}) collective-permute-start(bf16[8,8,2048]{2,1,0:T(8,128)(2,1)S(1)} %get-tuple-element.62.refs_0_), channel_id=1, source_target_pairs={{0,3},{1,0},{2,1},{3,2},{4,7},{5,4},{6,5},{7,6},{8,11},{9,8},{10,9... | collective-permute-start | bytes 786440 | tf_op jit(solution)/shard_map/ppermute | solution.py:258
  55.9 15.4 %collective-permute-start.5 = (bf16[8,8,2048]{2,1,0:T(8,128)(2,1)S(1)}, bf16[8,8,2048]{2,1,0:T(8,128)(2,1)S(1)}, u32[]{:S(2)}, u32[]{:S(2)}) collective-permute-start(bf16[8,8,2048]{2,1,0:T(8,128)(2,1)S(1)} %get-tuple-element.62.refs_0_), channel_id=1, source_target_pairs={{0,2},{1,3},{2,0},{3,1},{4,6},{5,7},{6,4},{7,5},{8,10},{9,11},{10,... | collective-permute-start | bytes 786440 | tf_op jit(solution)/shard_map/ppermute | solution.py:258
  56.8 17.9 %collective-permute-start.4 = (bf16[8,8,2048]{2,1,0:T(8,128)(2,1)S(1)}, bf16[8,8,2048]{2,1,0:T(8,128)(2,1)S(1)}, u32[]{:S(2)}, u32[]{:S(2)}) collective-permute-start(bf16[8,8,2048]{2,1,0:T(8,128)(2,1)S(1)} %get-tuple-element.62.refs_0_), channel_id=1, source_target_pairs={{0,1},{1,2},{2,3},{3,0},{4,5},{5,6},{6,7},{7,4},{8,9},{9,10},{10,1... | collective-permute-start | bytes 786440 | tf_op jit(solution)/shard_map/ppermute | solution.py:258
  74.8 0.8 copy-start.6
  75.6 24.1 %copy-start.7 = (bf16[8,4,8,1024]{3,2,1,0:T(8,128)(2,1)S(1)}, bf16[8,4,8,1024]{3,2,1,0:T(8,128)(2,1)}, u32[]{:S(2)}) copy-start(bf16[8,4,8,1024]{3,2,1,0:T(8,128)(2,1)} %copy-done.6) | copy-start | bytes 1572868
  91.7 8.7 %collective-permute-start.7 = (bf16[8,8,1024]{2,1,0:T(8,128)(2,1)S(1)}, bf16[8,8,1024]{2,1,0:T(8,128)(2,1)S(1)}, u32[]{:S(2)}, u32[]{:S(2)}) collective-permute-start(bf16[8,8,1024]{2,1,0:T(8,128)(2,1)S(1)} %all_to_all.31), channel_id=1, source_target_pairs={{0,224},{1,225},{2,226},{3,227},{4,228},{5,229},{6,230},{7,231},{8... | collective-permute-start | bytes 393224 | tf_op jit(solution)/shard_map/ppermute | solution.py:258
  91.7 8.7 %collective-permute-start.10 = (bf16[8,8,1024]{2,1,0:T(8,128)(2,1)S(1)}, bf16[8,8,1024]{2,1,0:T(8,128)(2,1)S(1)}, u32[]{:S(2)}, u32[]{:S(2)}) collective-permute-start(bf16[8,8,1024]{2,1,0:T(8,128)(2,1)S(1)} %all_to_all.31), channel_id=1, source_target_pairs={{0,227},{1,224},{2,225},{3,226},{4,231},{5,228},{6,229},{7,230},{8... | collective-permute-start | bytes 393224 | tf_op jit(solution)/shard_map/ppermute | solution.py:258
  92.0 8.4 %collective-permute-start.9 = (bf16[8,8,1024]{2,1,0:T(8,128)(2,1)S(1)}, bf16[8,8,1024]{2,1,0:T(8,128)(2,1)S(1)}, u32[]{:S(2)}, u32[]{:S(2)}) collective-permute-start(bf16[8,8,1024]{2,1,0:T(8,128)(2,1)S(1)} %all_to_all.31), channel_id=1, source_target_pairs={{0,226},{1,227},{2,224},{3,225},{4,230},{5,231},{6,228},{7,229},{8... | collective-permute-start | bytes 393224 | tf_op jit(solution)/shard_map/ppermute | solution.py:258
  93.7 7.4 %collective-permute-start.8 = (bf16[8,8,1024]{2,1,0:T(8,128)(2,1)S(1)}, bf16[8,8,1024]{2,1,0:T(8,128)(2,1)S(1)}, u32[]{:S(2)}, u32[]{:S(2)}) collective-permute-start(bf16[8,8,1024]{2,1,0:T(8,128)(2,1)S(1)} %all_to_all.31), channel_id=1, source_target_pairs={{0,225},{1,226},{2,227},{3,224},{4,229},{5,230},{6,231},{7,228},{8... | collective-permute-start | bytes 393224 | tf_op jit(solution)/shard_map/ppermute | solution.py:258
  95.7 1.0 copy-start.4
  96.7 1.0 copy-start.9
  97.8 1.0 copy-start.12
  99.7 1.6 copy-start.2
  137.9 7.9 %collective-permute-start.11 = (bf16[8,8,1024]{2,1,0:T(8,128)(2,1)S(1)}, bf16[8,8,1024]{2,1,0:T(8,128)(2,1)S(1)}, u32[]{:S(2)}, u32[]{:S(2)}) collective-permute-start(bf16[8,8,1024]{2,1,0:T(8,128)(2,1)S(1)} %all_to_all.33), channel_id=1, source_target_pairs={{0,224},{1,225},{2,226},{3,227},{4,228},{5,229},{6,230},{7,231},{8... | collective-permute-start | bytes 393224 | tf_op jit(solution)/shard_map/ppermute | solution.py:258
  137.9 7.9 %collective-permute-start.14 = (bf16[8,8,1024]{2,1,0:T(8,128)(2,1)S(1)}, bf16[8,8,1024]{2,1,0:T(8,128)(2,1)S(1)}, u32[]{:S(2)}, u32[]{:S(2)}) collective-permute-start(bf16[8,8,1024]{2,1,0:T(8,128)(2,1)S(1)} %all_to_all.33), channel_id=1, source_target_pairs={{0,227},{1,224},{2,225},{3,226},{4,231},{5,228},{6,229},{7,230},{8... | collective-permute-start | bytes 393224 | tf_op jit(solution)/shard_map/ppermute | solution.py:258
  140.1 5.9 %collective-permute-start.13 = (bf16[8,8,1024]{2,1,0:T(8,128)(2,1)S(1)}, bf16[8,8,1024]{2,1,0:T(8,128)(2,1)S(1)}, u32[]{:S(2)}, u32[]{:S(2)}) collective-permute-start(bf16[8,8,1024]{2,1,0:T(8,128)(2,1)S(1)} %all_to_all.33), channel_id=1, source_target_pairs={{0,226},{1,227},{2,224},{3,225},{4,230},{5,231},{6,228},{7,229},{8... | collective-permute-start | bytes 393224 | tf_op jit(solution)/shard_map/ppermute | solution.py:258
  141.6 6.1 %collective-permute-start.12 = (bf16[8,8,1024]{2,1,0:T(8,128)(2,1)S(1)}, bf16[8,8,1024]{2,1,0:T(8,128)(2,1)S(1)}, u32[]{:S(2)}, u32[]{:S(2)}) collective-permute-start(bf16[8,8,1024]{2,1,0:T(8,128)(2,1)S(1)} %all_to_all.33), channel_id=1, source_target_pairs={{0,225},{1,226},{2,227},{3,224},{4,229},{5,230},{6,231},{7,228},{8... | collective-permute-start | bytes 393224 | tf_op jit(solution)/shard_map/ppermute | solution.py:258
  149.5 25.8 %copy-start.5 = (bf16[8,4,8,1024]{3,2,1,0:T(8,128)(2,1)S(1)}, bf16[8,4,8,1024]{3,2,1,0:T(8,128)(2,1)}, u32[]{:S(2)}) copy-start(bf16[8,4,8,1024]{3,2,1,0:T(8,128)(2,1)} %copy-done.3) | copy-start | bytes 1572868
  149.5 25.8 %copy-start.10 = (bf16[256,1024]{1,0:T(8,128)(2,1)S(1)}, bf16[256,1024]{1,0:T(8,128)(2,1)}, u32[]{:S(2)}) copy-start(bf16[256,1024]{1,0:T(8,128)(2,1)} %copy-done.8) | copy-start | bytes 1572868
  149.5 25.8 %copy-start.13 = (bf16[256,1024]{1,0:T(8,128)(2,1)S(1)}, bf16[256,1024]{1,0:T(8,128)(2,1)}, u32[]{:S(2)}) copy-start(bf16[256,1024]{1,0:T(8,128)(2,1)} %copy-done.11) | copy-start | bytes 1572868

commit v7 on v6

--- a/solution.py
+++ b/solution.py
@@ -324,7 +324,7 @@
         held = (x, hidden, grads, dz)
         if slot == 0:
             blocks = [later] + [moved(later, 0, distance) for distance in range(1, ALONG_X)]
-            arrived, *later = lax.optimization_barrier((arrived, *assemble(blocks)))
+            later = assemble(blocks)
         passing, blocks = call(
             lambda *refs, slot=slot: sum_kernel(slot, *refs),
             (shape(rows, D), shape(along_z, rows, D)),

time: 183 us -> 176 us (0.962)
  blocking collectives: 101 us -> 96.9 us
  waiting for transfers between devices: 31 us -> 28.3 us
  local copies, waits for them, and re-layouts: 4.86 us -> 2.4 us
  starting transfers between devices: 23.6 us -> 25.7 us
    ppermute x15, waiting for transfers between devices: 31 us -> 15.4 us  [moved(): return lax.ppermute(value, ('section', 'tensor'), pairs)]
    all_to_all x1, waiting for transfers between devices: 0.01 us -> 13 us  [exchange(): lax.all_to_all(blocks, 'tensor', split_axis=0, concat_axis=0, tiled=True)]
    all_to_all x2, blocking collectives: 48.3 us -> 45.4 us  [exchange(): lax.all_to_all(blocks, 'tensor', split_axis=0, concat_axis=0, tiled=True)]
    unnamed x32 -> x20, local copies, waits for them, and re-layouts: 4.86 us -> 2.4 us
    ppermute x15, starting transfers between devices: 18.9 us -> 21.1 us  [moved(): return lax.ppermute(value, ('section', 'tensor'), pairs)]
  transfers between devices with their start and end apart: 16 -> 16, of which waited for: 9 -> 8; matrix products, arithmetic and copies ran while one was open for 0% -> 0% of each run, Pallas kernels for 2% -> 3%
where the time goes in v7:
time: 176 us; the launch traced here: 174 us
  blocking collectives  96.9 us (55%)
  waiting for transfers between devices  28.3 us (16%)
  starting transfers between devices  25.7 us (15%)
  Pallas kernels  19.9 us (11%)
  local copies, waits for them, and re-layouts  2.4 us (1%)
    all_to_all x3, blocking collectives, exchange_along_z(): lax.all_to_all(blocks, 'tensor', split_axis=0, concat_axis=0, axis_index_...  51.5 us
    all_to_all x2, blocking collectives, exchange(): lax.all_to_all(blocks, 'tensor', split_axis=0, concat_axis=0, tiled=True)  45.4 us
    ppermute x15, starting transfers between devices, moved(): return lax.ppermute(value, ('section', 'tensor'), pairs)  21.1 us
    ppermute x15, waiting for transfers between devices, moved(): return lax.ppermute(value, ('section', 'tensor'), pairs)  15.4 us
    all_to_all x1, waiting for transfers between devices, exchange(): lax.all_to_all(blocks, 'tensor', split_axis=0, concat_axis=0, tiled=True)  13 us
    pallas_call x17, Pallas kernels, call(): pl.pallas_call(kernel, out_shape=outs, in_specs=[VMEM] * len(operands), o...  12.2 us
    pallas_call x1, Pallas kernels, final_products(): pl.pallas_call(lambda *refs: final_kernel(slots, *refs), grid=(rows // bl...  5.8 us
    all_to_all x1, starting transfers between devices, exchange(): lax.all_to_all(blocks, 'tensor', split_axis=0, concat_axis=0, tiled=True)  4.61 us
  transfers between devices with their start and end apart: 16, of which 8 were waited for; matrix products, arithmetic and copies ran while one was open for 0% of the time, Pallas kernels for 3%

profile of v7, /device:TPU:8, one launch (start us, length us, event | category | flops | bytes accessed | tf_op | source)
XLA Modules:
  0.0 174.2 jit_solution(18026975593019497887)
XLA Ops:
  0.7 1.9 %start.1 = bf16[8,8,4096]{2,1,0:T(8,128)(2,1)} custom-call(s32[1,3]{1,0:T(1,128)} %index.1, bf16[4,8,1024]{2,1,0:T(8,128)(2,1)} %bitcast.58, bf16[8,1024]{1,0:T(8,128)(2,1)} %bitcast.59), custom_call_target="tpu_custom_call" | custom-call | tf_op jit(solution)/shard_map/start/pallas_call | solution.py:281
  2.6 26.0 %all_to_all.30.begun_ref = bf16[8,8,4096]{2,1,0:T(8,128)(2,1)S(1)} all-to-all(bf16[8,8,4096]{2,1,0:T(8,128)(2,1)} %start.1), channel_id=1, replica_groups={{0,4,8,12,16,20,24,28},{1,5,9,13,17,21,25,29},{2,6,10,14,18,22,26,30},{..., dimensions={0} | all-to-all | bytes 1048576 | tf_op jit(solution)/shard_map/all_to_all | solution.py:241
  28.6 2.8 %collective-permute-start.3 = (bf16[8,8,2048]{2,1,0:T(8,128)(2,1)S(1)}, bf16[8,8,2048]{2,1,0:T(8,128)(2,1)S(1)}, u32[]{:S(2)}, u32[]{:S(2)}) collective-permute-start(bf16[8,8,2048]{2,1,0:T(8,128)(2,1)S(1)} %get-tuple-element.54.refs_0_), channel_id=1, source_target_pairs={{0,3},{1,0},{2,1},{3,2},{4,7},{5,4},{6,5},{7,6},{8,11},{9,8},{10,9... | collective-permute-start | bytes 786440 | tf_op jit(solution)/shard_map/ppermute | solution.py:258
  31.4 0.8 collective-permute-start.2
  32.2 0.9 collective-permute-start.1
  33.1 0.0 collective-permute-start
  33.1 3.3 %collective-permute-done.refs_2_ = bf16[2,8,1024]{2,1,0:T(8,128)(2,1)S(1)} collective-permute-done((bf16[2,8,1024]{2,1,0:T(8,128)(2,1)S(1)}, bf16[2,8,1024]{2,1,0:T(8,128)(2,1)S(1)}, u32[]{:S(2)}, u32[]{:S(2)}) %collective-permute-start) | collective-permute-done | bytes 32800 | tf_op jit(solution)/shard_map/ppermute | solution.py:258
  36.5 4.4 %collective-permute-done.3.refs_3_ = bf16[8,8,2048]{2,1,0:T(8,128)(2,1)S(1)} collective-permute-done((bf16[8,8,2048]{2,1,0:T(8,128)(2,1)S(1)}, bf16[8,8,2048]{2,1,0:T(8,128)(2,1)S(1)}, u32[]{:S(2)}, u32[]{:S(2)}) %collective-permute-start.3) | collective-permute-done | bytes 262176 | tf_op jit(solution)/shard_map/ppermute | solution.py:258
  40.8 1.0 collective-permute-done.2.refs_2_
  41.8 2.7 %collective-permute-done.1.refs_1_ = bf16[8,8,2048]{2,1,0:T(8,128)(2,1)S(1)} collective-permute-done((bf16[8,8,2048]{2,1,0:T(8,128)(2,1)S(1)}, bf16[8,8,2048]{2,1,0:T(8,128)(2,1)S(1)}, u32[]{:S(2)}, u32[]{:S(2)}) %collective-permute-start.1) | collective-permute-done | bytes 262176 | tf_op jit(solution)/shard_map/ppermute | solution.py:258
  44.5 0.1 assemble.4
  44.6 0.7 forward.3
  45.4 0.0 copy-start.4
  45.4 0.8 copy-done.4
  46.2 1.3 back.2
  47.5 0.8 copy-done.6
  48.3 0.8 copy-done.3
  49.0 4.6 %all-to-all-start.1 = ((bf16[32,8,1024]{2,1,0:T(8,128)(2,1)}), bf16[32,8,1024]{2,1,0:T(8,128)(2,1)}, u32[]{:S(2)}, u32[]{:S(2)}) async-start(bf16[32,8,1024]{2,1,0:T(8,128)(2,1)} %bitcast.52), calls=%async_computation.1 | async-start | bytes 1048576 | tf_op jit(solution)/shard_map/all_to_all | solution.py:235
  53.7 2.9 %collective-permute-start.7 = (bf16[8,8,2048]{2,1,0:T(8,128)(2,1)S(1)}, bf16[8,8,2048]{2,1,0:T(8,128)(2,1)}, u32[]{:S(2)}, u32[]{:S(2)}) collective-permute-start(bf16[8,8,2048]{2,1,0:T(8,128)(2,1)S(1)} %get-tuple-element.63.refs_0_), channel_id=1, source_target_pairs={{0,3},{1,0},{2,1},{3,2},{4,7},{5,4},{6,5},{7,6},{8,11},{9,8},{10,9... | collective-permute-start | bytes 786440 | tf_op jit(solution)/shard_map/ppermute | solution.py:258
  56.6 0.8 collective-permute-start.6
  57.4 0.9 collective-permute-start.5
  58.3 13.0 %all-to-all-done.1.refs_0_ = bf16[32,8,1024]{2,1,0:T(8,128)(2,1)} async-done(((bf16[32,8,1024]{2,1,0:T(8,128)(2,1)}), bf16[32,8,1024]{2,1,0:T(8,128)(2,1)}, u32[]{:S(2)}, u32[]{:S(2)}) %all-to-all-start.1) | async-done | bytes 524320 | tf_op jit(solution)/shard_map/all_to_all | solution.py:235
  71.3 1.2 add_up.2
  72.5 12.1 %all_to_all.31 = bf16[8,8,1024]{2,1,0:T(8,128)(2,1)S(1)} all-to-all(bf16[8,8,1024]{2,1,0:T(8,128)(2,1)S(1)} %get-tuple-element.60), channel_id=1, replica_groups={{0,4,8,12,16,20,24,28},{1,5,9,13,17,21,25,29},{2,6,10,14,18,22,26,30},{..., dimensions={0} | all-to-all | bytes 262144 | tf_op jit(solution)/shard_map/all_to_all | solution.py:241
  84.6 1.4 collective-permute-start.10
  86.0 0.8 collective-permute-start.9
  86.8 3.1 %collective-permute-start.8 = (bf16[8,8,1024]{2,1,0:T(8,128)(2,1)S(1)}, bf16[8,8,1024]{2,1,0:T(8,128)(2,1)S(1)}, u32[]{:S(2)}, u32[]{:S(2)}) collective-permute-start(bf16[8,8,1024]{2,1,0:T(8,128)(2,1)S(1)} %all_to_all.31), channel_id=1, source_target_pairs={{0,225},{1,226},{2,227},{3,224},{4,229},{5,230},{6,231},{7,228},{8... | collective-permute-start | bytes 393224 | tf_op jit(solution)/shard_map/ppermute | solution.py:258
  89.9 1.2 assemble.5
  91.1 0.9 squares.2.refs_7_
  92.0 0.0 copy-start.2
  92.0 0.7 forward.4
  92.7 0.5 collective-permute-done.9.refs_2_
  93.2 2.0 %collective-permute-done.8.refs_1_ = bf16[8,8,1024]{2,1,0:T(8,128)(2,1)S(1)} collective-permute-done((bf16[8,8,1024]{2,1,0:T(8,128)(2,1)S(1)}, bf16[8,8,1024]{2,1,0:T(8,128)(2,1)S(1)}, u32[]{:S(2)}, u32[]{:S(2)}) %collective-permute-start.8) | collective-permute-done | bytes 131104 | tf_op jit(solution)/shard_map/ppermute | solution.py:258
  95.2 1.3 back.3
  96.5 20.8 %all_to_all.32.refs_0_ = bf16[32,8,1024]{2,1,0:T(8,128)(2,1)S(1)} all-to-all(bf16[32,8,1024]{2,1,0:T(8,128)(2,1)S(1)} %bitcast.53), channel_id=1, replica_groups=mesh['section'=8,'tensor'=32] {'tensor'}, dimensions={0} | all-to-all | bytes 1048576 | tf_op jit(solution)/shard_map/all_to_all | solution.py:235
  117.3 0.1 add_up.3
  117.4 13.5 %all_to_all.33 = bf16[8,8,1024]{2,1,0:T(8,128)(2,1)S(1)} all-to-all(bf16[8,8,1024]{2,1,0:T(8,128)(2,1)S(1)} %get-tuple-element.71), channel_id=1, replica_groups={{0,4,8,12,16,20,24,28},{1,5,9,13,17,21,25,29},{2,6,10,14,18,22,26,30},{..., dimensions={0} | all-to-all | bytes 262144 | tf_op jit(solution)/shard_map/all_to_all | solution.py:241
  130.8 2.2 %collective-permute-start.14 = (bf16[8,8,1024]{2,1,0:T(8,128)(2,1)S(1)}, bf16[8,8,1024]{2,1,0:T(8,128)(2,1)S(1)}, u32[]{:S(2)}, u32[]{:S(2)}) collective-permute-start(bf16[8,8,1024]{2,1,0:T(8,128)(2,1)S(1)} %all_to_all.33), channel_id=1, source_target_pairs={{0,227},{1,224},{2,225},{3,226},{4,231},{5,228},{6,229},{7,230},{8... | collective-permute-start | bytes 393224 | tf_op jit(solution)/shard_map/ppermute | solution.py:258
  133.1 2.5 %collective-permute-start.13 = (bf16[8,8,1024]{2,1,0:T(8,128)(2,1)S(1)}, bf16[8,8,1024]{2,1,0:T(8,128)(2,1)S(1)}, u32[]{:S(2)}, u32[]{:S(2)}) collective-permute-start(bf16[8,8,1024]{2,1,0:T(8,128)(2,1)S(1)} %all_to_all.33), channel_id=1, source_target_pairs={{0,226},{1,227},{2,224},{3,225},{4,230},{5,231},{6,228},{7,229},{8... | collective-permute-start | bytes 393224 | tf_op jit(solution)/shard_map/ppermute | solution.py:258
  135.6 2.0 %collective-permute-start.12 = (bf16[8,8,1024]{2,1,0:T(8,128)(2,1)S(1)}, bf16[8,8,1024]{2,1,0:T(8,128)(2,1)S(1)}, u32[]{:S(2)}, u32[]{:S(2)}) collective-permute-start(bf16[8,8,1024]{2,1,0:T(8,128)(2,1)S(1)} %all_to_all.33), channel_id=1, source_target_pairs={{0,225},{1,226},{2,227},{3,224},{4,229},{5,230},{6,231},{7,228},{8... | collective-permute-start | bytes 393224 | tf_op jit(solution)/shard_map/ppermute | solution.py:258
  137.6 0.7 forward.5
  138.3 0.5 grams.1
  138.8 0.9 squares.3.refs_8_
  139.7 1.5 collective-permute-done.12.refs_1_
  141.3 1.8 %last_back.1 = (bf16[256,1024]{1,0:T(8,128)(2,1)S(1)}, bf16[256,1152]{1,0:T(8,128)(2,1)S(1)}) custom-call(s32[2,3]{1,0:T(2,128)S(1)} %bitcast.56, bf16[256,1024]{1,0:T(8,128)(2,1)S(1)} %bitcast.35, f32[256,1024]{1,0:T(8,128)S(1)} %get-tuple-element.85.refs_2_, bf16[1024,1024]{1,0:T(8,128)(2,1)S(1)} %bitcast.30, bf16[1024,1024]{1,0:T(8,128)(2,1)S(1)} %bitcast.27, ...), custom_call_target="tpu_custom_call" | custom-call | flops 1073741824 | bytes 1048576 | tf_op jit(solution)/shard_map/last_back/pallas_call | solution.py:27
  143.1 24.6 %all_to_all.34.arrived_ref = bf16[32,8,1152]{2,1,0:T(8,128)(2,1)S(1)} all-to-all(bf16[32,8,1152]{2,1,0:T(8,128)(2,1)S(1)} %bitcast.51), channel_id=1, replica_groups=mesh['section'=8,'tensor'=32] {'tensor'}, dimensions={0} | all-to-all | bytes 1179648 | tf_op jit(solution)/shard_map/all_to_all | solution.py:235
  167.7 0.7 last_add_up.1
  168.4 5.8 %final.1 = (bf16[1024,1024]{1,0:T(8,128)(2,1)}, bf16[1024,1024]{1,0:T(8,128)(2,1)}) custom-call(s32[2,3]{1,0:T(2,128)S(1)} %bitcast.57, f32[1,128]{1,0:T(1,128)S(1)} %get-tuple-element.93.refs_1_, bf16[256,1024]{1,0:T(8,128)(2,1)S(1)} %bitcast.47, bf16[256,1024]{1,0:T(8,128)(2,1)S(1)} %bitcast.50, bf16[256,1024]{1,0:T(8,128)(2,1)S(1)} %bitcast.44, ...), custom_call_target="tpu_custom_call" | custom-call | flops 3221225472 | bytes 4194304 | tf_op jit(solution)/shard_map/final/pallas_call | solution.py:219
  (28 shorter events, 0.2 us)
Async XLA Ops:
  0.6 32.5 %copy-start.9 = (bf16[2,8,1024]{2,1,0:T(8,128)(2,1)S(1)}, bf16[2,8,1024]{2,1,0:T(8,128)(2,1)}, u32[]{:S(2)}) copy-start(bf16[2,8,1024]{2,1,0:T(8,128)(2,1)} %param.11) | copy-start | bytes 98308
  0.6 44.0 %copy-start = (bf16[1,1024,1024]{2,1,0:T(8,128)(2,1)S(1)}, bf16[1,1024,1024]{2,1,0:T(8,128)(2,1)}, u32[]{:S(2)}) copy-start(bf16[1,1024,1024]{2,1,0:T(8,128)(2,1)} %param.12) | copy-start | bytes 6291460
  28.6 17.6 %copy-start.1 = (bf16[1,1024,1024]{2,1,0:T(8,128)(2,1)S(1)}, bf16[1,1024,1024]{2,1,0:T(8,128)(2,1)}, u32[]{:S(2)}) copy-start(bf16[1,1024,1024]{2,1,0:T(8,128)(2,1)} %param.13) | copy-start | bytes 6291460
  28.6 12.2 %collective-permute-start.3 = (bf16[8,8,2048]{2,1,0:T(8,128)(2,1)S(1)}, bf16[8,8,2048]{2,1,0:T(8,128)(2,1)S(1)}, u32[]{:S(2)}, u32[]{:S(2)}) collective-permute-start(bf16[8,8,2048]{2,1,0:T(8,128)(2,1)S(1)} %get-tuple-element.54.refs_0_), channel_id=1, source_target_pairs={{0,3},{1,0},{2,1},{3,2},{4,7},{5,4},{6,5},{7,6},{8,11},{9,8},{10,9... | collective-permute-start | bytes 786440 | tf_op jit(solution)/shard_map/ppermute | solution.py:258
  31.4 10.4 %collective-permute-start.2 = (bf16[8,8,2048]{2,1,0:T(8,128)(2,1)S(1)}, bf16[8,8,2048]{2,1,0:T(8,128)(2,1)S(1)}, u32[]{:S(2)}, u32[]{:S(2)}) collective-permute-start(bf16[8,8,2048]{2,1,0:T(8,128)(2,1)S(1)} %get-tuple-element.54.refs_0_), channel_id=1, source_target_pairs={{0,2},{1,3},{2,0},{3,1},{4,6},{5,7},{6,4},{7,5},{8,10},{9,11},{10,... | collective-permute-start | bytes 786440 | tf_op jit(solution)/shard_map/ppermute | solution.py:258
  32.2 12.3 %collective-permute-start.1 = (bf16[8,8,2048]{2,1,0:T(8,128)(2,1)S(1)}, bf16[8,8,2048]{2,1,0:T(8,128)(2,1)S(1)}, u32[]{:S(2)}, u32[]{:S(2)}) collective-permute-start(bf16[8,8,2048]{2,1,0:T(8,128)(2,1)S(1)} %get-tuple-element.54.refs_0_), channel_id=1, source_target_pairs={{0,1},{1,2},{2,3},{3,0},{4,5},{5,6},{6,7},{7,4},{8,9},{9,10},{10,1... | collective-permute-start | bytes 786440 | tf_op jit(solution)/shard_map/ppermute | solution.py:258
  33.1 3.3 %collective-permute-start = (bf16[2,8,1024]{2,1,0:T(8,128)(2,1)S(1)}, bf16[2,8,1024]{2,1,0:T(8,128)(2,1)S(1)}, u32[]{:S(2)}, u32[]{:S(2)}) collective-permute-start(bf16[2,8,1024]{2,1,0:T(8,128)(2,1)S(1)} %copy-done.9), channel_id=1, source_target_pairs={{0,32},{1,33},{2,34},{3,35},{4,36},{5,37},{6,38},{7,39},{8,40},{9,... | collective-permute-start | bytes 98312 | tf_op jit(solution)/shard_map/ppermute | solution.py:258
  45.4 0.8 copy-start.4
  47.5 0.8 copy-start.6
  48.3 0.8 copy-start.3
  48.3 42.8 %copy-start.8 = (s32[1,3,2]{1,2,0:T(2,128)S(1)}, s32[1,3,2]{1,2,0:T(2,128)}, u32[]{:S(2)}) copy-start(s32[1,3,2]{1,2,0:T(2,128)} %param.9) | copy-start | bytes 76
  49.0 22.2 %all-to-all-start.1 = ((bf16[32,8,1024]{2,1,0:T(8,128)(2,1)}), bf16[32,8,1024]{2,1,0:T(8,128)(2,1)}, u32[]{:S(2)}, u32[]{:S(2)}) async-start(bf16[32,8,1024]{2,1,0:T(8,128)(2,1)} %bitcast.52), calls=%async_computation.1 | async-start | bytes 1048576 | tf_op jit(solution)/shard_map/all_to_all | solution.py:235
  53.7 32.3 %collective-permute-start.7 = (bf16[8,8,2048]{2,1,0:T(8,128)(2,1)S(1)}, bf16[8,8,2048]{2,1,0:T(8,128)(2,1)}, u32[]{:S(2)}, u32[]{:S(2)}) collective-permute-start(bf16[8,8,2048]{2,1,0:T(8,128)(2,1)S(1)} %get-tuple-element.63.refs_0_), channel_id=1, source_target_pairs={{0,3},{1,0},{2,1},{3,2},{4,7},{5,4},{6,5},{7,6},{8,11},{9,8},{10,9... | collective-permute-start | bytes 786440 | tf_op jit(solution)/shard_map/ppermute | solution.py:258
  56.6 30.2 %collective-permute-start.6 = (bf16[8,8,2048]{2,1,0:T(8,128)(2,1)S(1)}, bf16[8,8,2048]{2,1,0:T(8,128)(2,1)}, u32[]{:S(2)}, u32[]{:S(2)}) collective-permute-start(bf16[8,8,2048]{2,1,0:T(8,128)(2,1)S(1)} %get-tuple-element.63.refs_0_), channel_id=1, source_target_pairs={{0,2},{1,3},{2,0},{3,1},{4,6},{5,7},{6,4},{7,5},{8,10},{9,11},{10,... | collective-permute-start | bytes 786440 | tf_op jit(solution)/shard_map/ppermute | solution.py:258
  57.4 32.4 %collective-permute-start.5 = (bf16[8,8,2048]{2,1,0:T(8,128)(2,1)S(1)}, bf16[8,8,2048]{2,1,0:T(8,128)(2,1)}, u32[]{:S(2)}, u32[]{:S(2)}) collective-permute-start(bf16[8,8,2048]{2,1,0:T(8,128)(2,1)S(1)} %get-tuple-element.63.refs_0_), channel_id=1, source_target_pairs={{0,1},{1,2},{2,3},{3,0},{4,5},{5,6},{6,7},{7,4},{8,9},{9,10},{10,1... | collective-permute-start | bytes 786440 | tf_op jit(solution)/shard_map/ppermute | solution.py:258
  71.3 19.8 %copy-start.5 = (bf16[256,1024]{1,0:T(8,128)(2,1)S(1)}, bf16[256,1024]{1,0:T(8,128)(2,1)}, u32[]{:S(2)}) copy-start(bf16[256,1024]{1,0:T(8,128)(2,1)} %copy-done.4) | copy-start | bytes 1572868
  71.3 19.8 %copy-start.7 = (bf16[256,1024]{1,0:T(8,128)(2,1)S(1)}, bf16[256,1024]{1,0:T(8,128)(2,1)}, u32[]{:S(2)}) copy-start(bf16[256,1024]{1,0:T(8,128)(2,1)} %copy-done.6) | copy-start | bytes 1572868
  84.6 8.1 %collective-permute-start.4 = (bf16[8,8,1024]{2,1,0:T(8,128)(2,1)S(1)}, bf16[8,8,1024]{2,1,0:T(8,128)(2,1)S(1)}, u32[]{:S(2)}, u32[]{:S(2)}) collective-permute-start(bf16[8,8,1024]{2,1,0:T(8,128)(2,1)S(1)} %all_to_all.31), channel_id=1, source_target_pairs={{0,224},{1,225},{2,226},{3,227},{4,228},{5,229},{6,230},{7,231},{8... | collective-permute-start | bytes 393224 | tf_op jit(solution)/shard_map/ppermute | solution.py:258
  84.6 8.1 %collective-permute-start.10 = (bf16[8,8,1024]{2,1,0:T(8,128)(2,1)S(1)}, bf16[8,8,1024]{2,1,0:T(8,128)(2,1)S(1)}, u32[]{:S(2)}, u32[]{:S(2)}) collective-permute-start(bf16[8,8,1024]{2,1,0:T(8,128)(2,1)S(1)} %all_to_all.31), channel_id=1, source_target_pairs={{0,227},{1,224},{2,225},{3,226},{4,231},{5,228},{6,229},{7,230},{8... | collective-permute-start | bytes 393224 | tf_op jit(solution)/shard_map/ppermute | solution.py:258
  86.0 7.2 %collective-permute-start.9 = (bf16[8,8,1024]{2,1,0:T(8,128)(2,1)S(1)}, bf16[8,8,1024]{2,1,0:T(8,128)(2,1)S(1)}, u32[]{:S(2)}, u32[]{:S(2)}) collective-permute-start(bf16[8,8,1024]{2,1,0:T(8,128)(2,1)S(1)} %all_to_all.31), channel_id=1, source_target_pairs={{0,226},{1,227},{2,224},{3,225},{4,230},{5,231},{6,228},{7,229},{8... | collective-permute-start | bytes 393224 | tf_op jit(solution)/shard_map/ppermute | solution.py:258
  86.8 8.4 %collective-permute-start.8 = (bf16[8,8,1024]{2,1,0:T(8,128)(2,1)S(1)}, bf16[8,8,1024]{2,1,0:T(8,128)(2,1)S(1)}, u32[]{:S(2)}, u32[]{:S(2)}) collective-permute-start(bf16[8,8,1024]{2,1,0:T(8,128)(2,1)S(1)} %all_to_all.31), channel_id=1, source_target_pairs={{0,225},{1,226},{2,227},{3,224},{4,229},{5,230},{6,231},{7,228},{8... | collective-permute-start | bytes 393224 | tf_op jit(solution)/shard_map/ppermute | solution.py:258
  92.0 3.3 %copy-start.2 = (bf16[1,1024,1024]{2,1,0:T(8,128)(2,1)S(1)}, bf16[1,1024,1024]{2,1,0:T(8,128)(2,1)}, u32[]{:S(2)}) copy-start(bf16[1,1024,1024]{2,1,0:T(8,128)(2,1)} %param.13) | copy-start | bytes 6291460
  130.8 8.8 %collective-permute-start.11 = (bf16[8,8,1024]{2,1,0:T(8,128)(2,1)S(1)}, bf16[8,8,1024]{2,1,0:T(8,128)(2,1)S(1)}, u32[]{:S(2)}, u32[]{:S(2)}) collective-permute-start(bf16[8,8,1024]{2,1,0:T(8,128)(2,1)S(1)} %all_to_all.33), channel_id=1, source_target_pairs={{0,224},{1,225},{2,226},{3,227},{4,228},{5,229},{6,230},{7,231},{8... | collective-permute-start | bytes 393224 | tf_op jit(solution)/shard_map/ppermute | solution.py:258
  130.8 8.8 %collective-permute-start.14 = (bf16[8,8,1024]{2,1,0:T(8,128)(2,1)S(1)}, bf16[8,8,1024]{2,1,0:T(8,128)(2,1)S(1)}, u32[]{:S(2)}, u32[]{:S(2)}) collective-permute-start(bf16[8,8,1024]{2,1,0:T(8,128)(2,1)S(1)} %all_to_all.33), channel_id=1, source_target_pairs={{0,227},{1,224},{2,225},{3,226},{4,231},{5,228},{6,229},{7,230},{8... | collective-permute-start | bytes 393224 | tf_op jit(solution)/shard_map/ppermute | solution.py:258
  133.1 6.6 %collective-permute-start.13 = (bf16[8,8,1024]{2,1,0:T(8,128)(2,1)S(1)}, bf16[8,8,1024]{2,1,0:T(8,128)(2,1)S(1)}, u32[]{:S(2)}, u32[]{:S(2)}) collective-permute-start(bf16[8,8,1024]{2,1,0:T(8,128)(2,1)S(1)} %all_to_all.33), channel_id=1, source_target_pairs={{0,226},{1,227},{2,224},{3,225},{4,230},{5,231},{6,228},{7,229},{8... | collective-permute-start | bytes 393224 | tf_op jit(solution)/shard_map/ppermute | solution.py:258
  135.6 5.6 %collective-permute-start.12 = (bf16[8,8,1024]{2,1,0:T(8,128)(2,1)S(1)}, bf16[8,8,1024]{2,1,0:T(8,128)(2,1)S(1)}, u32[]{:S(2)}, u32[]{:S(2)}) collective-permute-start(bf16[8,8,1024]{2,1,0:T(8,128)(2,1)S(1)} %all_to_all.33), channel_id=1, source_target_pairs={{0,225},{1,226},{2,227},{3,224},{4,229},{5,230},{6,231},{7,228},{8... | collective-permute-start | bytes 393224 | tf_op jit(solution)/shard_map/ppermute | solution.py:258

commit v8 on v7

--- a/solution.py
+++ b/solution.py
@@ -164,29 +164,26 @@
     blocks_ref[...] = jnp.broadcast_to(chosen[None], blocks_ref.shape)
 
 
-def last_sum_kernel(arrived_ref, grads_ref, *refs):
-    *earlier_refs, results_ref, line_ref = refs
-    total = grads_ref[lax.axis_index("tensor")].astype(F32)
-    line = jnp.zeros(line_ref.shape, F32)
-    for peer in range(arrived_ref.shape[0]):
-        total = total + arrived_ref[peer, :, :D].astype(F32)
-        line = line + arrived_ref[peer, 0:1, D:].astype(F32)
-    for place, earlier_ref in enumerate(earlier_refs):
-        results_ref[place] = earlier_ref[...]
-    results_ref[len(earlier_refs)] = total.astype(BF16)
-    pieces = [pltpu.roll(line, LANES - place * SPACING, 1) for place in (1, 2)]
-    line_ref[...] = line + (pieces[0] + pieces[1])
-
-
-def final_kernel(slots, lengths_ref, totals_ref, *refs):
+def final_kernel(slots, lengths_ref, arrived_ref, own_ref, *refs):
+    earlier_refs, refs = refs[: slots - 1], refs[slots - 1 :]
     x, hidden, dz, dy = (refs[i * slots : (i + 1) * slots] for i in range(4))
-    grad_in_ref, grad_out_ref, dzc_ref, dyc_ref = refs[4 * slots :]
+    grad_in_ref, grad_out_ref, results_ref, dzc_ref, dyc_ref = refs[4 * slots :]
     tokens = dz[0].shape[0]
     step = pl.program_id(0)
 
     @pl.when(step == 0)
     def _():
-        factor = 1.0 / (jnp.sqrt(totals_ref[...] / (D * FF)) + GAMMA)
+        total = own_ref[lax.axis_index("tensor")].astype(F32)
+        line = jnp.zeros((1, LANES), F32)
+        for peer in range(arrived_ref.shape[0]):
+            total = total + arrived_ref[peer, :, :D].astype(F32)
+            line = line + arrived_ref[peer, 0:1, D:].astype(F32)
+        for place, earlier_ref in enumerate(earlier_refs):
+            results_ref[place] = earlier_ref[...]
+        results_ref[slots - 1] = total.astype(BF16)
+        pieces = [pltpu.roll(line, LANES - place * SPACING, 1) for place in (1, 2)]
+        squares = line + (pieces[0] + pieces[1])
+        factor = 1.0 / (jnp.sqrt(squares / (D * FF)) + GAMMA)
         for slot in range(slots):
             cut = lengths_ref[0:1, slot : slot + 1]
             row = lax.broadcasted_iota(jnp.int32, (tokens, 1), 0) < cut
@@ -202,33 +199,31 @@
     block = grad_in_ref.shape[0]
     strip = pl.ds(pl.multiple_of(step * block, block), block)
     for left, right_ref, out_ref in ((x, dzc_ref, grad_in_ref), (hidden, dyc_ref, grad_out_ref)):
+        lhs = jnp.concatenate([part[:, strip] for part in left], axis=0)
         for cols in parts(right_ref.shape[1]):
-            total = tn(left[0][:, strip], right_ref[:tokens, cols])
-            for slot in range(1, slots):
-                rows = slice(slot * tokens, (slot + 1) * tokens)
-                total = total + tn(left[slot][:, strip], right_ref[rows, cols])
-            out_ref[:, cols] = total.astype(BF16)
-
-
-def final_products(lengths, totals, x, hidden, dz, dy):
+            out_ref[:, cols] = tn(lhs, right_ref[:, cols]).astype(BF16)
+
+
+def final_products(lengths, arrived, own, earlier, x, hidden, dz, dy):
     slots = len(dz)
     tokens, width = dz[0].shape
     rows = x[0].shape[1]
-    block = 256
+    block = 512
     out = pl.BlockSpec((block, width), lambda i: (i, 0))
+    results = shape(slots, *earlier[0].shape)
     return pl.pallas_call(
         lambda *refs: final_kernel(slots, *refs),
         grid=(rows // block,),
-        out_shape=(shape(rows, width), shape(rows, width)),
-        in_specs=[VMEM] * (2 + 4 * slots),
-        out_specs=(out, out),
+        out_shape=(shape(rows, width), shape(rows, width), results),
+        in_specs=[VMEM] * (3 + slots - 1 + 4 * slots),
+        out_specs=(out, out, pl.BlockSpec(results.shape, lambda i: (0, 0, 0))),
         scratch_shapes=[pltpu.VMEM((slots * tokens, width), BF16)] * 2,
         name="final",
-        compiler_params=pltpu.CompilerParams(vmem_limit_bytes=12 * MIB),
+        compiler_params=pltpu.CompilerParams(vmem_limit_bytes=16 * MIB),
         cost_estimate=pl.CostEstimate(
             flops=4 * rows * width * slots * tokens, bytes_accessed=4 * MIB, transcendentals=0
         ),
-    )(lengths, totals, *x, *hidden, *dz, *dy)
+    )(lengths, arrived, own, *earlier, *x, *hidden, *dz, *dy)
 
 
 def exchange(blocks):
@@ -366,14 +361,10 @@
     )
     dzs.append(dz)
     arrived = exchange(share.reshape(count, rows, D + LANES))
-    results, totals = call(
-        last_sum_kernel,
-        (shape(slots, rows, D), shape(1, LANES, dtype=F32)),
-        (arrived, grads.reshape(count, rows, D), *results),
-        tokens * D,
-        "last_add_up",
+    own = grads.reshape(count, rows, D)
+    grad_in, grad_out, results = final_products(
+        lengths, arrived, own, results, xs, hiddens, dzs, dys
     )
-    grad_in, grad_out = final_products(lengths, totals, xs, hiddens, dzs, dys)
     return grad_in[None], grad_out[None], results[None]
 
 

time: 176 us -> 175 us (level)
    pallas_call x17 -> x16, Pallas kernels: 12.2 us -> 11.5 us  [call(): pl.pallas_call(kernel, out_shape=outs, in_specs=[VMEM] * len(operands), o...]
where the time goes in v8:
time: 175 us; the launch traced here: 173 us
  blocking collectives  96.9 us (55%)
  waiting for transfers between devices  28.3 us (16%)
  starting transfers between devices  25.7 us (15%)
  Pallas kernels  18.9 us (11%)
  local copies, waits for them, and re-layouts  2.39 us (1%)
    all_to_all x3, blocking collectives, exchange_along_z(): lax.all_to_all(blocks, 'tensor', split_axis=0, concat_axis=0, axis_index_...  51.5 us
    all_to_all x2, blocking collectives, exchange(): lax.all_to_all(blocks, 'tensor', split_axis=0, concat_axis=0, tiled=True)  45.4 us
    ppermute x15, starting transfers between devices, moved(): return lax.ppermute(value, ('section', 'tensor'), pairs)  21.1 us
    ppermute x15, waiting for transfers between devices, moved(): return lax.ppermute(value, ('section', 'tensor'), pairs)  15.4 us
    all_to_all x1, waiting for transfers between devices, exchange(): lax.all_to_all(blocks, 'tensor', split_axis=0, concat_axis=0, tiled=True)  13 us
    pallas_call x16, Pallas kernels, call(): pl.pallas_call(kernel, out_shape=outs, in_specs=[VMEM] * len(operands), o...  11.5 us
    pallas_call x1, Pallas kernels, final_products(): pl.pallas_call(lambda *refs: final_kernel(slots, *refs), grid=(rows // bl...  5.52 us
    all_to_all x1, starting transfers between devices, exchange(): lax.all_to_all(blocks, 'tensor', split_axis=0, concat_axis=0, tiled=True)  4.62 us
  transfers between devices with their start and end apart: 16, of which 8 were waited for; matrix products, arithmetic and copies ran while one was open for 0% of the time, Pallas kernels for 3%

profile of v8, /device:TPU:8, one launch (start us, length us, event | category | flops | bytes accessed | tf_op | source)
XLA Modules:
  0.0 173.2 jit_solution(11737767420133402955)
XLA Ops:
  0.7 1.9 %start.1 = bf16[8,8,4096]{2,1,0:T(8,128)(2,1)} custom-call(s32[1,3]{1,0:T(1,128)} %index.1, bf16[4,8,1024]{2,1,0:T(8,128)(2,1)} %bitcast.58, bf16[8,1024]{1,0:T(8,128)(2,1)} %bitcast.59), custom_call_target="tpu_custom_call" | custom-call | tf_op jit(solution)/shard_map/start/pallas_call | solution.py:276
  2.6 26.0 %all_to_all.30.begun_ref = bf16[8,8,4096]{2,1,0:T(8,128)(2,1)S(1)} all-to-all(bf16[8,8,4096]{2,1,0:T(8,128)(2,1)} %start.1), channel_id=1, replica_groups={{0,4,8,12,16,20,24,28},{1,5,9,13,17,21,25,29},{2,6,10,14,18,22,26,30},{..., dimensions={0} | all-to-all | bytes 1048576 | tf_op jit(solution)/shard_map/all_to_all | solution.py:236
  28.6 2.8 %collective-permute-start.3 = (bf16[8,8,2048]{2,1,0:T(8,128)(2,1)S(1)}, bf16[8,8,2048]{2,1,0:T(8,128)(2,1)S(1)}, u32[]{:S(2)}, u32[]{:S(2)}) collective-permute-start(bf16[8,8,2048]{2,1,0:T(8,128)(2,1)S(1)} %get-tuple-element.53.refs_0_), channel_id=1, source_target_pairs={{0,3},{1,0},{2,1},{3,2},{4,7},{5,4},{6,5},{7,6},{8,11},{9,8},{10,9... | collective-permute-start | bytes 786440 | tf_op jit(solution)/shard_map/ppermute | solution.py:253
  31.4 0.8 collective-permute-start.2
  32.2 0.9 collective-permute-start.1
  33.1 3.3 %collective-permute-done.refs_2_ = bf16[2,8,1024]{2,1,0:T(8,128)(2,1)S(1)} collective-permute-done((bf16[2,8,1024]{2,1,0:T(8,128)(2,1)S(1)}, bf16[2,8,1024]{2,1,0:T(8,128)(2,1)S(1)}, u32[]{:S(2)}, u32[]{:S(2)}) %collective-permute-start) | collective-permute-done | bytes 32800 | tf_op jit(solution)/shard_map/ppermute | solution.py:253
  36.5 4.4 %collective-permute-done.3.refs_3_ = bf16[8,8,2048]{2,1,0:T(8,128)(2,1)S(1)} collective-permute-done((bf16[8,8,2048]{2,1,0:T(8,128)(2,1)S(1)}, bf16[8,8,2048]{2,1,0:T(8,128)(2,1)S(1)}, u32[]{:S(2)}, u32[]{:S(2)}) %collective-permute-start.3) | collective-permute-done | bytes 262176 | tf_op jit(solution)/shard_map/ppermute | solution.py:253
  40.8 1.0 collective-permute-done.2.refs_2_
  41.8 2.7 %collective-permute-done.1.refs_1_ = bf16[8,8,2048]{2,1,0:T(8,128)(2,1)S(1)} collective-permute-done((bf16[8,8,2048]{2,1,0:T(8,128)(2,1)S(1)}, bf16[8,8,2048]{2,1,0:T(8,128)(2,1)S(1)}, u32[]{:S(2)}, u32[]{:S(2)}) %collective-permute-start.1) | collective-permute-done | bytes 262176 | tf_op jit(solution)/shard_map/ppermute | solution.py:253
  44.5 0.1 assemble.4
  44.6 0.7 forward.3
  45.4 0.0 copy-start.4
  45.4 0.8 copy-done.4
  46.2 1.3 back.2
  47.5 0.8 copy-done.6
  48.2 0.8 copy-done.3
  49.0 4.6 %all-to-all-start.1 = ((bf16[32,8,1024]{2,1,0:T(8,128)(2,1)}), bf16[32,8,1024]{2,1,0:T(8,128)(2,1)}, u32[]{:S(2)}, u32[]{:S(2)}) async-start(bf16[32,8,1024]{2,1,0:T(8,128)(2,1)} %bitcast.52), calls=%async_computation.1 | async-start | bytes 1048576 | tf_op jit(solution)/shard_map/all_to_all | solution.py:230
  53.7 2.9 %collective-permute-start.7 = (bf16[8,8,2048]{2,1,0:T(8,128)(2,1)S(1)}, bf16[8,8,2048]{2,1,0:T(8,128)(2,1)}, u32[]{:S(2)}, u32[]{:S(2)}) collective-permute-start(bf16[8,8,2048]{2,1,0:T(8,128)(2,1)S(1)} %get-tuple-element.62.refs_0_), channel_id=1, source_target_pairs={{0,3},{1,0},{2,1},{3,2},{4,7},{5,4},{6,5},{7,6},{8,11},{9,8},{10,9... | collective-permute-start | bytes 786440 | tf_op jit(solution)/shard_map/ppermute | solution.py:253
  56.6 0.8 collective-permute-start.6
  57.4 0.9 collective-permute-start.5
  58.3 13.0 %all-to-all-done.1.refs_0_ = bf16[32,8,1024]{2,1,0:T(8,128)(2,1)} async-done(((bf16[32,8,1024]{2,1,0:T(8,128)(2,1)}), bf16[32,8,1024]{2,1,0:T(8,128)(2,1)}, u32[]{:S(2)}, u32[]{:S(2)}) %all-to-all-start.1) | async-done | bytes 524320 | tf_op jit(solution)/shard_map/all_to_all | solution.py:230
  71.3 1.2 add_up.2
  72.5 12.1 %all_to_all.31 = bf16[8,8,1024]{2,1,0:T(8,128)(2,1)S(1)} all-to-all(bf16[8,8,1024]{2,1,0:T(8,128)(2,1)S(1)} %get-tuple-element.59), channel_id=1, replica_groups={{0,4,8,12,16,20,24,28},{1,5,9,13,17,21,25,29},{2,6,10,14,18,22,26,30},{..., dimensions={0} | all-to-all | bytes 262144 | tf_op jit(solution)/shard_map/all_to_all | solution.py:236
  84.6 0.0 collective-permute-start.4
  84.6 1.4 collective-permute-start.10
  86.0 0.0 collective-permute-done.7.refs_3_
  86.0 0.8 collective-permute-start.9
  86.8 3.1 %collective-permute-start.8 = (bf16[8,8,1024]{2,1,0:T(8,128)(2,1)S(1)}, bf16[8,8,1024]{2,1,0:T(8,128)(2,1)S(1)}, u32[]{:S(2)}, u32[]{:S(2)}) collective-permute-start(bf16[8,8,1024]{2,1,0:T(8,128)(2,1)S(1)} %all_to_all.31), channel_id=1, source_target_pairs={{0,225},{1,226},{2,227},{3,224},{4,229},{5,230},{6,231},{7,228},{8... | collective-permute-start | bytes 393224 | tf_op jit(solution)/shard_map/ppermute | solution.py:253
  89.8 1.2 assemble.5
  91.1 0.9 squares.2.refs_7_
  92.0 0.0 copy-start.2
  92.0 0.7 forward.4
  92.7 0.5 collective-permute-done.9.refs_2_
  93.2 2.0 %collective-permute-done.8.refs_1_ = bf16[8,8,1024]{2,1,0:T(8,128)(2,1)S(1)} collective-permute-done((bf16[8,8,1024]{2,1,0:T(8,128)(2,1)S(1)}, bf16[8,8,1024]{2,1,0:T(8,128)(2,1)S(1)}, u32[]{:S(2)}, u32[]{:S(2)}) %collective-permute-start.8) | collective-permute-done | bytes 131104 | tf_op jit(solution)/shard_map/ppermute | solution.py:253
  95.2 1.3 back.3
  96.5 20.8 %all_to_all.32.refs_0_ = bf16[32,8,1024]{2,1,0:T(8,128)(2,1)S(1)} all-to-all(bf16[32,8,1024]{2,1,0:T(8,128)(2,1)S(1)} %bitcast.53), channel_id=1, replica_groups=mesh['section'=8,'tensor'=32] {'tensor'}, dimensions={0} | all-to-all | bytes 1048576 | tf_op jit(solution)/shard_map/all_to_all | solution.py:230
  117.3 0.1 add_up.3
  117.4 13.5 %all_to_all.33 = bf16[8,8,1024]{2,1,0:T(8,128)(2,1)S(1)} all-to-all(bf16[8,8,1024]{2,1,0:T(8,128)(2,1)S(1)} %get-tuple-element.70), channel_id=1, replica_groups={{0,4,8,12,16,20,24,28},{1,5,9,13,17,21,25,29},{2,6,10,14,18,22,26,30},{..., dimensions={0} | all-to-all | bytes 262144 | tf_op jit(solution)/shard_map/all_to_all | solution.py:236
  130.9 2.2 %collective-permute-start.14 = (bf16[8,8,1024]{2,1,0:T(8,128)(2,1)S(1)}, bf16[8,8,1024]{2,1,0:T(8,128)(2,1)S(1)}, u32[]{:S(2)}, u32[]{:S(2)}) collective-permute-start(bf16[8,8,1024]{2,1,0:T(8,128)(2,1)S(1)} %all_to_all.33), channel_id=1, source_target_pairs={{0,227},{1,224},{2,225},{3,226},{4,231},{5,228},{6,229},{7,230},{8... | collective-permute-start | bytes 393224 | tf_op jit(solution)/shard_map/ppermute | solution.py:253
  133.1 2.5 %collective-permute-start.13 = (bf16[8,8,1024]{2,1,0:T(8,128)(2,1)S(1)}, bf16[8,8,1024]{2,1,0:T(8,128)(2,1)S(1)}, u32[]{:S(2)}, u32[]{:S(2)}) collective-permute-start(bf16[8,8,1024]{2,1,0:T(8,128)(2,1)S(1)} %all_to_all.33), channel_id=1, source_target_pairs={{0,226},{1,227},{2,224},{3,225},{4,230},{5,231},{6,228},{7,229},{8... | collective-permute-start | bytes 393224 | tf_op jit(solution)/shard_map/ppermute | solution.py:253
  135.6 2.0 %collective-permute-start.12 = (bf16[8,8,1024]{2,1,0:T(8,128)(2,1)S(1)}, bf16[8,8,1024]{2,1,0:T(8,128)(2,1)S(1)}, u32[]{:S(2)}, u32[]{:S(2)}) collective-permute-start(bf16[8,8,1024]{2,1,0:T(8,128)(2,1)S(1)} %all_to_all.33), channel_id=1, source_target_pairs={{0,225},{1,226},{2,227},{3,224},{4,229},{5,230},{6,231},{7,228},{8... | collective-permute-start | bytes 393224 | tf_op jit(solution)/shard_map/ppermute | solution.py:253
  137.6 0.7 forward.5
  138.3 0.5 grams.1
  138.8 0.9 squares.3.refs_8_
  139.7 1.5 collective-permute-done.12.refs_1_
  141.3 1.8 %last_back.1 = (bf16[256,1024]{1,0:T(8,128)(2,1)S(1)}, bf16[256,1152]{1,0:T(8,128)(2,1)S(1)}) custom-call(s32[2,3]{1,0:T(2,128)S(1)} %bitcast.56, bf16[256,1024]{1,0:T(8,128)(2,1)S(1)} %bitcast.42, f32[256,1024]{1,0:T(8,128)S(1)} %get-tuple-element.84.refs_2_, bf16[1024,1024]{1,0:T(8,128)(2,1)S(1)} %bitcast.30, bf16[1024,1024]{1,0:T(8,128)(2,1)S(1)} %bitcast.27, ...), custom_call_target="tpu_custom_call" | custom-call | flops 1073741824 | bytes 1048576 | tf_op jit(solution)/shard_map/last_back/pallas_call | solution.py:27
  143.1 24.6 %all_to_all.34.refs_1_ = bf16[32,8,1152]{2,1,0:T(8,128)(2,1)S(1)} all-to-all(bf16[32,8,1152]{2,1,0:T(8,128)(2,1)S(1)} %bitcast.51), channel_id=1, replica_groups=mesh['section'=8,'tensor'=32] {'tensor'}, dimensions={0} | all-to-all | bytes 1179648 | tf_op jit(solution)/shard_map/all_to_all | solution.py:230
  167.7 5.5 %final.1 = (bf16[1024,1024]{1,0:T(8,128)(2,1)}, bf16[1024,1024]{1,0:T(8,128)(2,1)}, bf16[3,8,1024]{2,1,0:T(8,128)(2,1)}) custom-call(s32[2,3]{1,0:T(2,128)S(1)} %bitcast.57, bf16[32,8,1152]{2,1,0:T(8,128)(2,1)S(1)} %all_to_all.34.refs_1_, bf16[32,8,1024]{2,1,0:T(8,128)(2,1)S(1)} %bitcast.44, bf16[8,1024]{1,0:T(8,128)(2,1)S(1)} %get-tuple-element.90.refs_3_, ...), custom_call_target="tpu_custom_call" | custom-call | flops 3221225472 | bytes 4194304 | tf_op jit(solution)/shard_map/final/pallas_call | solution.py:214
  (27 shorter events, 0.2 us)
Async XLA Ops:
  0.6 32.5 %copy-start.9 = (bf16[2,8,1024]{2,1,0:T(8,128)(2,1)S(1)}, bf16[2,8,1024]{2,1,0:T(8,128)(2,1)}, u32[]{:S(2)}) copy-start(bf16[2,8,1024]{2,1,0:T(8,128)(2,1)} %param.11) | copy-start | bytes 98308
  0.6 44.0 %copy-start = (bf16[1,1024,1024]{2,1,0:T(8,128)(2,1)S(1)}, bf16[1,1024,1024]{2,1,0:T(8,128)(2,1)}, u32[]{:S(2)}) copy-start(bf16[1,1024,1024]{2,1,0:T(8,128)(2,1)} %param.12) | copy-start | bytes 6291460
  28.6 17.6 %copy-start.1 = (bf16[1,1024,1024]{2,1,0:T(8,128)(2,1)S(1)}, bf16[1,1024,1024]{2,1,0:T(8,128)(2,1)}, u32[]{:S(2)}) copy-start(bf16[1,1024,1024]{2,1,0:T(8,128)(2,1)} %param.13) | copy-start | bytes 6291460
  28.6 12.2 %collective-permute-start.3 = (bf16[8,8,2048]{2,1,0:T(8,128)(2,1)S(1)}, bf16[8,8,2048]{2,1,0:T(8,128)(2,1)S(1)}, u32[]{:S(2)}, u32[]{:S(2)}) collective-permute-start(bf16[8,8,2048]{2,1,0:T(8,128)(2,1)S(1)} %get-tuple-element.53.refs_0_), channel_id=1, source_target_pairs={{0,3},{1,0},{2,1},{3,2},{4,7},{5,4},{6,5},{7,6},{8,11},{9,8},{10,9... | collective-permute-start | bytes 786440 | tf_op jit(solution)/shard_map/ppermute | solution.py:253
  31.4 10.4 %collective-permute-start.2 = (bf16[8,8,2048]{2,1,0:T(8,128)(2,1)S(1)}, bf16[8,8,2048]{2,1,0:T(8,128)(2,1)S(1)}, u32[]{:S(2)}, u32[]{:S(2)}) collective-permute-start(bf16[8,8,2048]{2,1,0:T(8,128)(2,1)S(1)} %get-tuple-element.53.refs_0_), channel_id=1, source_target_pairs={{0,2},{1,3},{2,0},{3,1},{4,6},{5,7},{6,4},{7,5},{8,10},{9,11},{10,... | collective-permute-start | bytes 786440 | tf_op jit(solution)/shard_map/ppermute | solution.py:253
  32.2 12.3 %collective-permute-start.1 = (bf16[8,8,2048]{2,1,0:T(8,128)(2,1)S(1)}, bf16[8,8,2048]{2,1,0:T(8,128)(2,1)S(1)}, u32[]{:S(2)}, u32[]{:S(2)}) collective-permute-start(bf16[8,8,2048]{2,1,0:T(8,128)(2,1)S(1)} %get-tuple-element.53.refs_0_), channel_id=1, source_target_pairs={{0,1},{1,2},{2,3},{3,0},{4,5},{5,6},{6,7},{7,4},{8,9},{9,10},{10,1... | collective-permute-start | bytes 786440 | tf_op jit(solution)/shard_map/ppermute | solution.py:253
  33.1 3.3 %collective-permute-start = (bf16[2,8,1024]{2,1,0:T(8,128)(2,1)S(1)}, bf16[2,8,1024]{2,1,0:T(8,128)(2,1)S(1)}, u32[]{:S(2)}, u32[]{:S(2)}) collective-permute-start(bf16[2,8,1024]{2,1,0:T(8,128)(2,1)S(1)} %copy-done.9), channel_id=1, source_target_pairs={{0,32},{1,33},{2,34},{3,35},{4,36},{5,37},{6,38},{7,39},{8,40},{9,... | collective-permute-start | bytes 98312 | tf_op jit(solution)/shard_map/ppermute | solution.py:253
  45.4 0.8 copy-start.4
  47.5 0.8 copy-start.6
  48.2 0.8 copy-start.3
  48.2 42.8 %copy-start.8 = (s32[1,3,2]{1,2,0:T(2,128)S(1)}, s32[1,3,2]{1,2,0:T(2,128)}, u32[]{:S(2)}) copy-start(s32[1,3,2]{1,2,0:T(2,128)} %param.9) | copy-start | bytes 76
  49.0 22.2 %all-to-all-start.1 = ((bf16[32,8,1024]{2,1,0:T(8,128)(2,1)}), bf16[32,8,1024]{2,1,0:T(8,128)(2,1)}, u32[]{:S(2)}, u32[]{:S(2)}) async-start(bf16[32,8,1024]{2,1,0:T(8,128)(2,1)} %bitcast.52), calls=%async_computation.1 | async-start | bytes 1048576 | tf_op jit(solution)/shard_map/all_to_all | solution.py:230
  53.7 32.3 %collective-permute-start.7 = (bf16[8,8,2048]{2,1,0:T(8,128)(2,1)S(1)}, bf16[8,8,2048]{2,1,0:T(8,128)(2,1)}, u32[]{:S(2)}, u32[]{:S(2)}) collective-permute-start(bf16[8,8,2048]{2,1,0:T(8,128)(2,1)S(1)} %get-tuple-element.62.refs_0_), channel_id=1, source_target_pairs={{0,3},{1,0},{2,1},{3,2},{4,7},{5,4},{6,5},{7,6},{8,11},{9,8},{10,9... | collective-permute-start | bytes 786440 | tf_op jit(solution)/shard_map/ppermute | solution.py:253
  56.6 30.2 %collective-permute-start.6 = (bf16[8,8,2048]{2,1,0:T(8,128)(2,1)S(1)}, bf16[8,8,2048]{2,1,0:T(8,128)(2,1)}, u32[]{:S(2)}, u32[]{:S(2)}) collective-permute-start(bf16[8,8,2048]{2,1,0:T(8,128)(2,1)S(1)} %get-tuple-element.62.refs_0_), channel_id=1, source_target_pairs={{0,2},{1,3},{2,0},{3,1},{4,6},{5,7},{6,4},{7,5},{8,10},{9,11},{10,... | collective-permute-start | bytes 786440 | tf_op jit(solution)/shard_map/ppermute | solution.py:253
  57.4 32.4 %collective-permute-start.5 = (bf16[8,8,2048]{2,1,0:T(8,128)(2,1)S(1)}, bf16[8,8,2048]{2,1,0:T(8,128)(2,1)}, u32[]{:S(2)}, u32[]{:S(2)}) collective-permute-start(bf16[8,8,2048]{2,1,0:T(8,128)(2,1)S(1)} %get-tuple-element.62.refs_0_), channel_id=1, source_target_pairs={{0,1},{1,2},{2,3},{3,0},{4,5},{5,6},{6,7},{7,4},{8,9},{9,10},{10,1... | collective-permute-start | bytes 786440 | tf_op jit(solution)/shard_map/ppermute | solution.py:253
  71.3 19.8 %copy-start.5 = (bf16[256,1024]{1,0:T(8,128)(2,1)S(1)}, bf16[256,1024]{1,0:T(8,128)(2,1)}, u32[]{:S(2)}) copy-start(bf16[256,1024]{1,0:T(8,128)(2,1)} %copy-done.4) | copy-start | bytes 1572868
  71.3 19.8 %copy-start.7 = (bf16[256,1024]{1,0:T(8,128)(2,1)S(1)}, bf16[256,1024]{1,0:T(8,128)(2,1)}, u32[]{:S(2)}) copy-start(bf16[256,1024]{1,0:T(8,128)(2,1)} %copy-done.6) | copy-start | bytes 1572868
  84.6 8.1 %collective-permute-start.4 = (bf16[8,8,1024]{2,1,0:T(8,128)(2,1)S(1)}, bf16[8,8,1024]{2,1,0:T(8,128)(2,1)S(1)}, u32[]{:S(2)}, u32[]{:S(2)}) collective-permute-start(bf16[8,8,1024]{2,1,0:T(8,128)(2,1)S(1)} %all_to_all.31), channel_id=1, source_target_pairs={{0,224},{1,225},{2,226},{3,227},{4,228},{5,229},{6,230},{7,231},{8... | collective-permute-start | bytes 393224 | tf_op jit(solution)/shard_map/ppermute | solution.py:253
  84.6 8.1 %collective-permute-start.10 = (bf16[8,8,1024]{2,1,0:T(8,128)(2,1)S(1)}, bf16[8,8,1024]{2,1,0:T(8,128)(2,1)S(1)}, u32[]{:S(2)}, u32[]{:S(2)}) collective-permute-start(bf16[8,8,1024]{2,1,0:T(8,128)(2,1)S(1)} %all_to_all.31), channel_id=1, source_target_pairs={{0,227},{1,224},{2,225},{3,226},{4,231},{5,228},{6,229},{7,230},{8... | collective-permute-start | bytes 393224 | tf_op jit(solution)/shard_map/ppermute | solution.py:253
  86.0 7.2 %collective-permute-start.9 = (bf16[8,8,1024]{2,1,0:T(8,128)(2,1)S(1)}, bf16[8,8,1024]{2,1,0:T(8,128)(2,1)S(1)}, u32[]{:S(2)}, u32[]{:S(2)}) collective-permute-start(bf16[8,8,1024]{2,1,0:T(8,128)(2,1)S(1)} %all_to_all.31), channel_id=1, source_target_pairs={{0,226},{1,227},{2,224},{3,225},{4,230},{5,231},{6,228},{7,229},{8... | collective-permute-start | bytes 393224 | tf_op jit(solution)/shard_map/ppermute | solution.py:253
  86.8 8.4 %collective-permute-start.8 = (bf16[8,8,1024]{2,1,0:T(8,128)(2,1)S(1)}, bf16[8,8,1024]{2,1,0:T(8,128)(2,1)S(1)}, u32[]{:S(2)}, u32[]{:S(2)}) collective-permute-start(bf16[8,8,1024]{2,1,0:T(8,128)(2,1)S(1)} %all_to_all.31), channel_id=1, source_target_pairs={{0,225},{1,226},{2,227},{3,224},{4,229},{5,230},{6,231},{7,228},{8... | collective-permute-start | bytes 393224 | tf_op jit(solution)/shard_map/ppermute | solution.py:253
  92.0 3.3 %copy-start.2 = (bf16[1,1024,1024]{2,1,0:T(8,128)(2,1)S(1)}, bf16[1,1024,1024]{2,1,0:T(8,128)(2,1)}, u32[]{:S(2)}) copy-start(bf16[1,1024,1024]{2,1,0:T(8,128)(2,1)} %param.13) | copy-start | bytes 6291460
  130.9 8.8 %collective-permute-start.11 = (bf16[8,8,1024]{2,1,0:T(8,128)(2,1)S(1)}, bf16[8,8,1024]{2,1,0:T(8,128)(2,1)S(1)}, u32[]{:S(2)}, u32[]{:S(2)}) collective-permute-start(bf16[8,8,1024]{2,1,0:T(8,128)(2,1)S(1)} %all_to_all.33), channel_id=1, source_target_pairs={{0,224},{1,225},{2,226},{3,227},{4,228},{5,229},{6,230},{7,231},{8... | collective-permute-start | bytes 393224 | tf_op jit(solution)/shard_map/ppermute | solution.py:253
  130.9 8.8 %collective-permute-start.14 = (bf16[8,8,1024]{2,1,0:T(8,128)(2,1)S(1)}, bf16[8,8,1024]{2,1,0:T(8,128)(2,1)S(1)}, u32[]{:S(2)}, u32[]{:S(2)}) collective-permute-start(bf16[8,8,1024]{2,1,0:T(8,128)(2,1)S(1)} %all_to_all.33), channel_id=1, source_target_pairs={{0,227},{1,224},{2,225},{3,226},{4,231},{5,228},{6,229},{7,230},{8... | collective-permute-start | bytes 393224 | tf_op jit(solution)/shard_map/ppermute | solution.py:253
  133.1 6.6 %collective-permute-start.13 = (bf16[8,8,1024]{2,1,0:T(8,128)(2,1)S(1)}, bf16[8,8,1024]{2,1,0:T(8,128)(2,1)S(1)}, u32[]{:S(2)}, u32[]{:S(2)}) collective-permute-start(bf16[8,8,1024]{2,1,0:T(8,128)(2,1)S(1)} %all_to_all.33), channel_id=1, source_target_pairs={{0,226},{1,227},{2,224},{3,225},{4,230},{5,231},{6,228},{7,229},{8... | collective-permute-start | bytes 393224 | tf_op jit(solution)/shard_map/ppermute | solution.py:253
  135.6 5.6 %collective-permute-start.12 = (bf16[8,8,1024]{2,1,0:T(8,128)(2,1)S(1)}, bf16[8,8,1024]{2,1,0:T(8,128)(2,1)S(1)}, u32[]{:S(2)}, u32[]{:S(2)}) collective-permute-start(bf16[8,8,1024]{2,1,0:T(8,128)(2,1)S(1)} %all_to_all.33), channel_id=1, source_target_pairs={{0,225},{1,226},{2,227},{3,224},{4,229},{5,230},{6,231},{7,228},{8... | collective-permute-start | bytes 393224 | tf_op jit(solution)/shard_map/ppermute | solution.py:253

commit v9 on v8

--- a/solution.py
+++ b/solution.py
@@ -23,12 +23,13 @@
     return jax.ShapeDtypeStruct(dims, dtype)
 
 
-def call(kernel, outs, operands, flops, name):
+def call(kernel, outs, operands, flops, name, scratch=()):
     return pl.pallas_call(
         kernel,
         out_shape=outs,
         in_specs=[VMEM] * len(operands),
         out_specs=jax.tree.map(lambda _: VMEM, outs),
+        scratch_shapes=[pltpu.VMEM(dims, BF16) for dims in scratch],
         name=name,
         compiler_params=pltpu.CompilerParams(vmem_limit_bytes=8 * MIB),
         cost_estimate=pl.CostEstimate(flops=flops, bytes_accessed=MIB, transcendentals=0),
@@ -96,6 +97,20 @@
         hidden_ref[:, cols] = (relu * relu).astype(BF16)
 
 
+def slope_kernel(x_ref, weights_ref, slope_ref):
+    x = x_ref[...]
+    for cols in parts(weights_ref.shape[1]):
+        slope_ref[:, cols] = 2.0 * jnp.maximum(mm(x, weights_ref[:, cols]), 0.0)
+
+
+def again_kernel(x_ref, grads_ref, w_in_ref, w_out_ref, hidden_ref, dz_ref):
+    x, grads = x_ref[...], grads_ref[...]
+    for part in parts(w_in_ref.shape[1]):
+        relu = jnp.maximum(mm(x, w_in_ref[:, part]), 0.0)
+        hidden_ref[:, part] = (relu * relu).astype(BF16)
+        dz_ref[:, part] = (2.0 * relu * nt(grads, w_out_ref[part, :])).astype(BF16)
+
+
 def masked_sums(slot, lengths_ref, paired):
     cut = lengths_ref[0:1, slot : slot + 1]
     tokens = paired.shape[0]
@@ -118,6 +133,10 @@
 
 
 def back_kernel(grads_ref, slope_ref, w_out_ref, w_in_ref, dz_ref, share_ref):
+    back_products(grads_ref[...], slope_ref, w_out_ref, w_in_ref, dz_ref, share_ref)
+
+
+def first_back_kernel(grads_ref, slope_ref, w_out_ref, w_in_ref, share_ref, dz_ref):
     back_products(grads_ref[...], slope_ref, w_out_ref, w_in_ref, dz_ref, share_ref)
 
 
@@ -154,7 +173,8 @@
 
 
 def sum_kernel(place, arrived_ref, grads_ref, loss_ref, passing_ref, blocks_ref):
-    total = grads_ref[lax.axis_index("tensor")].astype(F32)
+    own = lax.axis_index("tensor") if grads_ref.shape[0] > 1 else 0
+    total = grads_ref[own].astype(F32)
     for peer in range(arrived_ref.shape[0]):
         total = total + arrived_ref[peer].astype(F32)
     passing = total.astype(BF16)
@@ -299,47 +319,64 @@
         outs = (shape(tokens, units, dtype=F32), shape(tokens, units))
         return call(forward_kernel, outs, (x, first), product, "forward")
 
-    slope, hidden = forward(x)
+    slope = call(
+        slope_kernel, shape(tokens, units, dtype=F32), (x, first), product, "slope"
+    )
     xs, hiddens, dzs, dys, results, squares = [], [], [], [], [], []
-    for slot in range(slots):
-        xs.append(x)
-        hiddens.append(hidden)
-        dys.append(grads)
-        if slot + 1 == slots:
-            break
-        dz, share = call(
-            back_kernel,
-            (shape(tokens, units), shape(tokens, D)),
-            (grads, slope, second, first),
-            2 * product,
-            "back",
-        )
-        dzs.append(dz)
+    for slot in range(slots - 1):
+        if slot:
+            dz, share = call(
+                back_kernel,
+                (shape(tokens, units), shape(tokens, D)),
+                (grads, slope, second, first),
+                2 * product,
+                "back",
+            )
+            own = grads.reshape(count, rows, D)
+        else:
+            share = call(
+                first_back_kernel,
+                shape(tokens, D),
+                (grads, slope, second, first),
+                2 * product,
+                "first_back",
+                scratch=[(tokens, units)],
+            )
+            own = first_grads
         arrived = exchange(share.reshape(count, rows, D))
-        held = (x, hidden, grads, dz)
         if slot == 0:
             blocks = [later] + [moved(later, 0, distance) for distance in range(1, ALONG_X)]
             later = assemble(blocks)
         passing, blocks = call(
             lambda *refs, slot=slot: sum_kernel(slot, *refs),
             (shape(rows, D), shape(along_z, rows, D)),
-            (arrived, grads.reshape(count, rows, D), loss),
+            (arrived, own, loss),
             tokens * D,
             "add_up",
         )
         results.append(passing)
         block = exchange_along_z(blocks)
         pieces = [moved(block, 1, distance) for distance in range(ALONG_X)]
-        *late, x = lax.optimization_barrier((block, *held, later[slot]))
+        made = (hidden, dz) if slot else (first, second)
+        _, next_x, x, grads, *made = lax.optimization_barrier(
+            (block, later[slot], x, grads, *made)
+        )
         if slot:
-            held = late[1:]
+            hidden, dz = made
+        else:
+            hidden, dz = call(
+                again_kernel, (shape(tokens, units),) * 2, (x, grads, *made), 0, "again"
+            )
+        for kept, value in ((xs, x), (hiddens, hidden), (dzs, dz), (dys, grads)):
+            kept.append(value)
         one = call(
             lambda *refs, slot=slot: squares_kernel(slot, *refs),
             shape(1, LANES, dtype=F32),
-            (lengths, *held),
+            (lengths, x, hidden, grads, dz),
             product,
             "squares",
         )
+        x = next_x
         squares.append(one)
         slope, hidden = forward(x)
         ready = [one, slope, hidden]
@@ -359,7 +396,8 @@
         2 * product,
         "last_back",
     )
-    dzs.append(dz)
+    for kept, value in ((xs, x), (hiddens, hidden), (dzs, dz), (dys, grads)):
+        kept.append(value)
     arrived = exchange(share.reshape(count, rows, D + LANES))
     own = grads.reshape(count, rows, D)
     grad_in, grad_out, results = final_products(

time: 175 us -> 174 us (level)
  waiting for transfers between devices: 28.3 us -> 25.9 us
    ppermute x15, waiting for transfers between devices: 15.4 us -> 12.9 us  [moved(): return lax.ppermute(value, ('section', 'tensor'), pairs)]
    unnamed x20 -> x16, local copies, waits for them, and re-layouts: 2.39 us -> 3.84 us
    pallas_call x16 -> x17, Pallas kernels: 11.5 us -> 12.7 us  [call(): pl.pallas_call(kernel, out_shape=outs, in_specs=[VMEM] * len(operands), o...]
  transfers between devices with their start and end apart: 16 -> 16, of which waited for: 8 -> 6; matrix products, arithmetic and copies ran while one was open for 0% -> 0% of each run, Pallas kernels for 3% -> 4%
where the time goes in v9:
time: 174 us; the launch traced here: 173 us
  blocking collectives  97.3 us (56%)
  waiting for transfers between devices  25.9 us (15%)
  starting transfers between devices  24.9 us (14%)
  Pallas kernels  20.1 us (12%)
  local copies, waits for them, and re-layouts  3.84 us (2%)
    all_to_all x3, blocking collectives, exchange_along_z(): lax.all_to_all(blocks, 'tensor', split_axis=0, concat_axis=0, axis_index_...  50.2 us
    all_to_all x2, blocking collectives, exchange(): lax.all_to_all(blocks, 'tensor', split_axis=0, concat_axis=0, tiled=True)  47 us
    ppermute x15, starting transfers between devices, moved(): return lax.ppermute(value, ('section', 'tensor'), pairs)  20.3 us
    all_to_all x1, waiting for transfers between devices, exchange(): lax.all_to_all(blocks, 'tensor', split_axis=0, concat_axis=0, tiled=True)  13 us
    ppermute x15, waiting for transfers between devices, moved(): return lax.ppermute(value, ('section', 'tensor'), pairs)  12.9 us
    pallas_call x17, Pallas kernels, call(): pl.pallas_call(kernel, out_shape=outs, in_specs=[VMEM] * len(operands), o...  12.7 us
    pallas_call x1, Pallas kernels, final_products(): pl.pallas_call(lambda *refs: final_kernel(slots, *refs), grid=(rows // bl...  5.52 us
    all_to_all x1, starting transfers between devices, exchange(): lax.all_to_all(blocks, 'tensor', split_axis=0, concat_axis=0, tiled=True)  4.62 us
  transfers between devices with their start and end apart: 16, of which 6 were waited for; matrix products, arithmetic and copies ran while one was open for 0% of the time, Pallas kernels for 4%

profile of v9, /device:TPU:8, one launch (start us, length us, event | category | flops | bytes accessed | tf_op | source)
XLA Modules:
  0.0 173.0 jit_solution(17458049932246865711)
XLA Ops:
  0.7 1.9 %start.1 = bf16[8,8,4096]{2,1,0:T(8,128)(2,1)} custom-call(s32[1,3]{1,0:T(1,128)} %index.1, bf16[4,8,1024]{2,1,0:T(8,128)(2,1)} %bitcast.61, bf16[8,1024]{1,0:T(8,128)(2,1)} %bitcast.56), custom_call_target="tpu_custom_call" | custom-call | tf_op jit(solution)/shard_map/start/pallas_call | solution.py:296
  2.6 26.0 %all_to_all.30.begun_ref = bf16[8,8,4096]{2,1,0:T(8,128)(2,1)S(1)} all-to-all(bf16[8,8,4096]{2,1,0:T(8,128)(2,1)} %start.1), channel_id=1, replica_groups={{0,4,8,12,16,20,24,28},{1,5,9,13,17,21,25,29},{2,6,10,14,18,22,26,30},{..., dimensions={0} | all-to-all | bytes 1048576 | tf_op jit(solution)/shard_map/all_to_all | solution.py:256
  28.6 2.8 %collective-permute-start.3 = (bf16[8,8,2048]{2,1,0:T(8,128)(2,1)S(1)}, bf16[8,8,2048]{2,1,0:T(8,128)(2,1)S(1)}, u32[]{:S(2)}, u32[]{:S(2)}) collective-permute-start(bf16[8,8,2048]{2,1,0:T(8,128)(2,1)S(1)} %get-tuple-element.55.refs_0_), channel_id=1, source_target_pairs={{0,3},{1,0},{2,1},{3,2},{4,7},{5,4},{6,5},{7,6},{8,11},{9,8},{10,9... | collective-permute-start | bytes 786440 | tf_op jit(solution)/shard_map/ppermute | solution.py:273
  31.4 0.8 collective-permute-start.2
  32.2 0.9 collective-permute-start.1
  33.1 3.3 %collective-permute-done.refs_2_ = bf16[2,8,1024]{2,1,0:T(8,128)(2,1)S(1)} collective-permute-done((bf16[2,8,1024]{2,1,0:T(8,128)(2,1)S(1)}, bf16[2,8,1024]{2,1,0:T(8,128)(2,1)S(1)}, u32[]{:S(2)}, u32[]{:S(2)}) %collective-permute-start) | collective-permute-done | bytes 32800 | tf_op jit(solution)/shard_map/ppermute | solution.py:273
  36.5 4.4 %collective-permute-done.3.refs_3_ = bf16[8,8,2048]{2,1,0:T(8,128)(2,1)S(1)} collective-permute-done((bf16[8,8,2048]{2,1,0:T(8,128)(2,1)S(1)}, bf16[8,8,2048]{2,1,0:T(8,128)(2,1)S(1)}, u32[]{:S(2)}, u32[]{:S(2)}) %collective-permute-start.3) | collective-permute-done | bytes 262176 | tf_op jit(solution)/shard_map/ppermute | solution.py:273
  40.8 1.0 collective-permute-done.2.refs_2_
  41.8 2.7 %collective-permute-done.1.refs_1_ = bf16[8,8,2048]{2,1,0:T(8,128)(2,1)S(1)} collective-permute-done((bf16[8,8,2048]{2,1,0:T(8,128)(2,1)S(1)}, bf16[8,8,2048]{2,1,0:T(8,128)(2,1)S(1)}, u32[]{:S(2)}, u32[]{:S(2)}) %collective-permute-start.1) | collective-permute-done | bytes 262176 | tf_op jit(solution)/shard_map/ppermute | solution.py:273
  44.5 0.1 assemble.4
  44.6 0.0 copy-start.1
  44.6 0.7 slope.1.slope_ref
  45.4 0.9 copy-done.1
  46.2 1.3 first_back.1
  47.5 0.0 copy-start.4
  47.5 0.8 copy-done.4
  48.3 4.6 %all-to-all-start.1 = ((bf16[32,8,1024]{2,1,0:T(8,128)(2,1)}), bf16[32,8,1024]{2,1,0:T(8,128)(2,1)}, u32[]{:S(2)}, u32[]{:S(2)}) async-start(bf16[32,8,1024]{2,1,0:T(8,128)(2,1)} %bitcast.50), calls=%async_computation.1 | async-start | bytes 1048576 | tf_op jit(solution)/shard_map/all_to_all | solution.py:250
  52.9 2.9 %collective-permute-start.7 = (bf16[8,8,2048]{2,1,0:T(8,128)(2,1)S(1)}, bf16[8,8,2048]{2,1,0:T(8,128)(2,1)}, u32[]{:S(2)}, u32[]{:S(2)}) collective-permute-start(bf16[8,8,2048]{2,1,0:T(8,128)(2,1)S(1)} %get-tuple-element.60.refs_0_), channel_id=1, source_target_pairs={{0,3},{1,0},{2,1},{3,2},{4,7},{5,4},{6,5},{7,6},{8,11},{9,8},{10,9... | collective-permute-start | bytes 786440 | tf_op jit(solution)/shard_map/ppermute | solution.py:273
  55.8 0.8 collective-permute-start.6
  56.7 0.9 collective-permute-start.5
  57.5 13.0 %all-to-all-done.1.refs_0_ = bf16[32,8,1024]{2,1,0:T(8,128)(2,1)} async-done(((bf16[32,8,1024]{2,1,0:T(8,128)(2,1)}), bf16[32,8,1024]{2,1,0:T(8,128)(2,1)}, u32[]{:S(2)}, u32[]{:S(2)}) %all-to-all-start.1) | async-done | bytes 524320 | tf_op jit(solution)/shard_map/all_to_all | solution.py:250
  70.5 1.1 add_up.2
  71.7 12.1 %all_to_all.31 = bf16[8,8,1024]{2,1,0:T(8,128)(2,1)S(1)} all-to-all(bf16[8,8,1024]{2,1,0:T(8,128)(2,1)S(1)} %get-tuple-element.59), channel_id=1, replica_groups={{0,4,8,12,16,20,24,28},{1,5,9,13,17,21,25,29},{2,6,10,14,18,22,26,30},{..., dimensions={0} | all-to-all | bytes 262144 | tf_op jit(solution)/shard_map/all_to_all | solution.py:256
  83.8 1.4 collective-permute-start.10
  85.1 0.8 collective-permute-start.9
  86.0 3.1 %collective-permute-start.8 = (bf16[8,8,1024]{2,1,0:T(8,128)(2,1)S(1)}, bf16[8,8,1024]{2,1,0:T(8,128)(2,1)S(1)}, u32[]{:S(2)}, u32[]{:S(2)}) collective-permute-start(bf16[8,8,1024]{2,1,0:T(8,128)(2,1)S(1)} %all_to_all.31), channel_id=1, source_target_pairs={{0,225},{1,226},{2,227},{3,224},{4,229},{5,230},{6,231},{7,228},{8... | collective-permute-start | bytes 393224 | tf_op jit(solution)/shard_map/ppermute | solution.py:273
  89.0 1.2 assemble.5
  90.2 0.0 copy-start.2
  90.2 1.6 copy-done.2
  91.8 1.3 again.1
  93.1 0.7 forward.2
  93.8 0.9 squares.2.refs_7_
  94.8 0.1 assemble.6
  94.8 0.6 copy-done.3
  95.4 1.3 back.1
  96.7 21.9 %all_to_all.32.refs_0_ = bf16[32,8,1024]{2,1,0:T(8,128)(2,1)S(1)} all-to-all(bf16[32,8,1024]{2,1,0:T(8,128)(2,1)S(1)} %bitcast.55), channel_id=1, replica_groups=mesh['section'=8,'tensor'=32] {'tensor'}, dimensions={0} | all-to-all | bytes 1048576 | tf_op jit(solution)/shard_map/all_to_all | solution.py:250
  118.6 0.1 add_up.3
  118.7 12.1 %all_to_all.33 = bf16[8,8,1024]{2,1,0:T(8,128)(2,1)S(1)} all-to-all(bf16[8,8,1024]{2,1,0:T(8,128)(2,1)S(1)} %get-tuple-element.74), channel_id=1, replica_groups={{0,4,8,12,16,20,24,28},{1,5,9,13,17,21,25,29},{2,6,10,14,18,22,26,30},{..., dimensions={0} | all-to-all | bytes 262144 | tf_op jit(solution)/shard_map/all_to_all | solution.py:256
  130.8 2.1 %collective-permute-start.14 = (bf16[8,8,1024]{2,1,0:T(8,128)(2,1)S(1)}, bf16[8,8,1024]{2,1,0:T(8,128)(2,1)S(1)}, u32[]{:S(2)}, u32[]{:S(2)}) collective-permute-start(bf16[8,8,1024]{2,1,0:T(8,128)(2,1)S(1)} %all_to_all.33), channel_id=1, source_target_pairs={{0,227},{1,224},{2,225},{3,226},{4,231},{5,228},{6,229},{7,230},{8... | collective-permute-start | bytes 393224 | tf_op jit(solution)/shard_map/ppermute | solution.py:273
  133.0 1.8 %collective-permute-start.13 = (bf16[8,8,1024]{2,1,0:T(8,128)(2,1)S(1)}, bf16[8,8,1024]{2,1,0:T(8,128)(2,1)S(1)}, u32[]{:S(2)}, u32[]{:S(2)}) collective-permute-start(bf16[8,8,1024]{2,1,0:T(8,128)(2,1)S(1)} %all_to_all.33), channel_id=1, source_target_pairs={{0,226},{1,227},{2,224},{3,225},{4,230},{5,231},{6,228},{7,229},{8... | collective-permute-start | bytes 393224 | tf_op jit(solution)/shard_map/ppermute | solution.py:273
  134.8 2.0 %collective-permute-start.12 = (bf16[8,8,1024]{2,1,0:T(8,128)(2,1)S(1)}, bf16[8,8,1024]{2,1,0:T(8,128)(2,1)S(1)}, u32[]{:S(2)}, u32[]{:S(2)}) collective-permute-start(bf16[8,8,1024]{2,1,0:T(8,128)(2,1)S(1)} %all_to_all.33), channel_id=1, source_target_pairs={{0,225},{1,226},{2,227},{3,224},{4,229},{5,230},{6,231},{7,228},{8... | collective-permute-start | bytes 393224 | tf_op jit(solution)/shard_map/ppermute | solution.py:273
  136.8 0.7 forward.3
  137.5 0.5 grams.1
  138.0 0.9 squares.3.refs_8_
  138.9 1.5 collective-permute-done.12.refs_1_
  140.4 1.8 %last_back.1 = (bf16[256,1024]{1,0:T(8,128)(2,1)S(1)}, bf16[256,1152]{1,0:T(8,128)(2,1)S(1)}) custom-call(s32[2,3]{1,0:T(2,128)S(1)} %bitcast.59, bf16[256,1024]{1,0:T(8,128)(2,1)S(1)} %bitcast.47, f32[256,1024]{1,0:T(8,128)S(1)} %get-tuple-element.88.refs_2_, bf16[1024,1024]{1,0:T(8,128)(2,1)S(1)} %bitcast.31, bf16[1024,1024]{1,0:T(8,128)(2,1)S(1)} %bitcast.27, ...), custom_call_target="tpu_custom_call" | custom-call | flops 1073741824 | bytes 1048576 | tf_op jit(solution)/shard_map/last_back/pallas_call | solution.py:27
  142.3 25.1 %all_to_all.34.refs_1_ = bf16[32,8,1152]{2,1,0:T(8,128)(2,1)S(1)} all-to-all(bf16[32,8,1152]{2,1,0:T(8,128)(2,1)S(1)} %bitcast.54), channel_id=1, replica_groups=mesh['section'=8,'tensor'=32] {'tensor'}, dimensions={0} | all-to-all | bytes 1179648 | tf_op jit(solution)/shard_map/all_to_all | solution.py:250
  167.4 5.5 %final.1 = (bf16[1024,1024]{1,0:T(8,128)(2,1)}, bf16[1024,1024]{1,0:T(8,128)(2,1)}, bf16[3,8,1024]{2,1,0:T(8,128)(2,1)}) custom-call(s32[2,3]{1,0:T(2,128)S(1)} %bitcast.60, bf16[32,8,1152]{2,1,0:T(8,128)(2,1)S(1)} %all_to_all.34.refs_1_, bf16[32,8,1024]{2,1,0:T(8,128)(2,1)S(1)} %bitcast.49, bf16[8,1024]{1,0:T(8,128)(2,1)S(1)} %get-tuple-element.94.refs_3_, ...), custom_call_target="tpu_custom_call" | custom-call | flops 3221225472 | bytes 4194304 | tf_op jit(solution)/shard_map/final/pallas_call | solution.py:234
  (24 shorter events, 0.1 us)
Async XLA Ops:
  0.6 32.5 %copy-start.7 = (bf16[2,8,1024]{2,1,0:T(8,128)(2,1)S(1)}, bf16[2,8,1024]{2,1,0:T(8,128)(2,1)}, u32[]{:S(2)}) copy-start(bf16[2,8,1024]{2,1,0:T(8,128)(2,1)} %param.11) | copy-start | bytes 98308
  0.6 44.0 %copy-start = (bf16[1,1024,1024]{2,1,0:T(8,128)(2,1)S(1)}, bf16[1,1024,1024]{2,1,0:T(8,128)(2,1)}, u32[]{:S(2)}) copy-start(bf16[1,1024,1024]{2,1,0:T(8,128)(2,1)} %param.12) | copy-start | bytes 6291460
  28.6 12.2 %collective-permute-start.3 = (bf16[8,8,2048]{2,1,0:T(8,128)(2,1)S(1)}, bf16[8,8,2048]{2,1,0:T(8,128)(2,1)S(1)}, u32[]{:S(2)}, u32[]{:S(2)}) collective-permute-start(bf16[8,8,2048]{2,1,0:T(8,128)(2,1)S(1)} %get-tuple-element.55.refs_0_), channel_id=1, source_target_pairs={{0,3},{1,0},{2,1},{3,2},{4,7},{5,4},{6,5},{7,6},{8,11},{9,8},{10,9... | collective-permute-start | bytes 786440 | tf_op jit(solution)/shard_map/ppermute | solution.py:273
  31.4 10.4 %collective-permute-start.2 = (bf16[8,8,2048]{2,1,0:T(8,128)(2,1)S(1)}, bf16[8,8,2048]{2,1,0:T(8,128)(2,1)S(1)}, u32[]{:S(2)}, u32[]{:S(2)}) collective-permute-start(bf16[8,8,2048]{2,1,0:T(8,128)(2,1)S(1)} %get-tuple-element.55.refs_0_), channel_id=1, source_target_pairs={{0,2},{1,3},{2,0},{3,1},{4,6},{5,7},{6,4},{7,5},{8,10},{9,11},{10,... | collective-permute-start | bytes 786440 | tf_op jit(solution)/shard_map/ppermute | solution.py:273
  32.2 12.3 %collective-permute-start.1 = (bf16[8,8,2048]{2,1,0:T(8,128)(2,1)S(1)}, bf16[8,8,2048]{2,1,0:T(8,128)(2,1)S(1)}, u32[]{:S(2)}, u32[]{:S(2)}) collective-permute-start(bf16[8,8,2048]{2,1,0:T(8,128)(2,1)S(1)} %get-tuple-element.55.refs_0_), channel_id=1, source_target_pairs={{0,1},{1,2},{2,3},{3,0},{4,5},{5,6},{6,7},{7,4},{8,9},{9,10},{10,1... | collective-permute-start | bytes 786440 | tf_op jit(solution)/shard_map/ppermute | solution.py:273
  33.1 3.3 %collective-permute-start = (bf16[2,8,1024]{2,1,0:T(8,128)(2,1)S(1)}, bf16[2,8,1024]{2,1,0:T(8,128)(2,1)S(1)}, u32[]{:S(2)}, u32[]{:S(2)}) collective-permute-start(bf16[2,8,1024]{2,1,0:T(8,128)(2,1)S(1)} %copy-done.7), channel_id=1, source_target_pairs={{0,32},{1,33},{2,34},{3,35},{4,36},{5,37},{6,38},{7,39},{8,40},{9,... | collective-permute-start | bytes 98312 | tf_op jit(solution)/shard_map/ppermute | solution.py:273
  44.6 1.6 copy-start.1
  46.2 24.3 %copy-start.5 = (bf16[1,8,1024]{2,1,0:T(8,128)(2,1)S(1)}, bf16[1,8,1024]{2,1,0:T(8,128)(2,1)}, u32[]{:S(2)}) copy-start(bf16[1,8,1024]{2,1,0:T(8,128)(2,1)} %refs_1_.1) | copy-start | bytes 49156
  47.5 0.8 copy-start.4
  48.3 22.2 %all-to-all-start.1 = ((bf16[32,8,1024]{2,1,0:T(8,128)(2,1)}), bf16[32,8,1024]{2,1,0:T(8,128)(2,1)}, u32[]{:S(2)}, u32[]{:S(2)}) async-start(bf16[32,8,1024]{2,1,0:T(8,128)(2,1)} %bitcast.50), calls=%async_computation.1 | async-start | bytes 1048576 | tf_op jit(solution)/shard_map/all_to_all | solution.py:250
  52.9 32.2 %collective-permute-start.7 = (bf16[8,8,2048]{2,1,0:T(8,128)(2,1)S(1)}, bf16[8,8,2048]{2,1,0:T(8,128)(2,1)}, u32[]{:S(2)}, u32[]{:S(2)}) collective-permute-start(bf16[8,8,2048]{2,1,0:T(8,128)(2,1)S(1)} %get-tuple-element.60.refs_0_), channel_id=1, source_target_pairs={{0,3},{1,0},{2,1},{3,2},{4,7},{5,4},{6,5},{7,6},{8,11},{9,8},{10,9... | collective-permute-start | bytes 786440 | tf_op jit(solution)/shard_map/ppermute | solution.py:273
  55.8 30.1 %collective-permute-start.6 = (bf16[8,8,2048]{2,1,0:T(8,128)(2,1)S(1)}, bf16[8,8,2048]{2,1,0:T(8,128)(2,1)}, u32[]{:S(2)}, u32[]{:S(2)}) collective-permute-start(bf16[8,8,2048]{2,1,0:T(8,128)(2,1)S(1)} %get-tuple-element.60.refs_0_), channel_id=1, source_target_pairs={{0,2},{1,3},{2,0},{3,1},{4,6},{5,7},{6,4},{7,5},{8,10},{9,11},{10,... | collective-permute-start | bytes 786440 | tf_op jit(solution)/shard_map/ppermute | solution.py:273
  56.7 32.4 %collective-permute-start.5 = (bf16[8,8,2048]{2,1,0:T(8,128)(2,1)S(1)}, bf16[8,8,2048]{2,1,0:T(8,128)(2,1)}, u32[]{:S(2)}, u32[]{:S(2)}) collective-permute-start(bf16[8,8,2048]{2,1,0:T(8,128)(2,1)S(1)} %get-tuple-element.60.refs_0_), channel_id=1, source_target_pairs={{0,1},{1,2},{2,3},{3,0},{4,5},{5,6},{6,7},{7,4},{8,9},{9,10},{10,1... | collective-permute-start | bytes 786440 | tf_op jit(solution)/shard_map/ppermute | solution.py:273
  83.8 10.9 %collective-permute-start.4 = (bf16[8,8,1024]{2,1,0:T(8,128)(2,1)S(1)}, bf16[8,8,1024]{2,1,0:T(8,128)(2,1)S(1)}, u32[]{:S(2)}, u32[]{:S(2)}) collective-permute-start(bf16[8,8,1024]{2,1,0:T(8,128)(2,1)S(1)} %all_to_all.31), channel_id=1, source_target_pairs={{0,224},{1,225},{2,226},{3,227},{4,228},{5,229},{6,230},{7,231},{8... | collective-permute-start | bytes 393224 | tf_op jit(solution)/shard_map/ppermute | solution.py:273
  83.8 11.0 %collective-permute-start.10 = (bf16[8,8,1024]{2,1,0:T(8,128)(2,1)S(1)}, bf16[8,8,1024]{2,1,0:T(8,128)(2,1)S(1)}, u32[]{:S(2)}, u32[]{:S(2)}) collective-permute-start(bf16[8,8,1024]{2,1,0:T(8,128)(2,1)S(1)} %all_to_all.31), channel_id=1, source_target_pairs={{0,227},{1,224},{2,225},{3,226},{4,231},{5,228},{6,229},{7,230},{8... | collective-permute-start | bytes 393224 | tf_op jit(solution)/shard_map/ppermute | solution.py:273
  85.1 9.6 %collective-permute-start.9 = (bf16[8,8,1024]{2,1,0:T(8,128)(2,1)S(1)}, bf16[8,8,1024]{2,1,0:T(8,128)(2,1)S(1)}, u32[]{:S(2)}, u32[]{:S(2)}) collective-permute-start(bf16[8,8,1024]{2,1,0:T(8,128)(2,1)S(1)} %all_to_all.31), channel_id=1, source_target_pairs={{0,226},{1,227},{2,224},{3,225},{4,230},{5,231},{6,228},{7,229},{8... | collective-permute-start | bytes 393224 | tf_op jit(solution)/shard_map/ppermute | solution.py:273
  86.0 8.8 %collective-permute-start.8 = (bf16[8,8,1024]{2,1,0:T(8,128)(2,1)S(1)}, bf16[8,8,1024]{2,1,0:T(8,128)(2,1)S(1)}, u32[]{:S(2)}, u32[]{:S(2)}) collective-permute-start(bf16[8,8,1024]{2,1,0:T(8,128)(2,1)S(1)} %all_to_all.31), channel_id=1, source_target_pairs={{0,225},{1,226},{2,227},{3,224},{4,229},{5,230},{6,231},{7,228},{8... | collective-permute-start | bytes 393224 | tf_op jit(solution)/shard_map/ppermute | solution.py:273
  90.2 1.6 copy-start.2
  93.1 0.8 copy-start.6
  93.8 1.6 copy-start.3
  130.8 8.0 %collective-permute-start.11 = (bf16[8,8,1024]{2,1,0:T(8,128)(2,1)S(1)}, bf16[8,8,1024]{2,1,0:T(8,128)(2,1)S(1)}, u32[]{:S(2)}, u32[]{:S(2)}) collective-permute-start(bf16[8,8,1024]{2,1,0:T(8,128)(2,1)S(1)} %all_to_all.33), channel_id=1, source_target_pairs={{0,224},{1,225},{2,226},{3,227},{4,228},{5,229},{6,230},{7,231},{8... | collective-permute-start | bytes 393224 | tf_op jit(solution)/shard_map/ppermute | solution.py:273
  130.8 8.0 %collective-permute-start.14 = (bf16[8,8,1024]{2,1,0:T(8,128)(2,1)S(1)}, bf16[8,8,1024]{2,1,0:T(8,128)(2,1)S(1)}, u32[]{:S(2)}, u32[]{:S(2)}) collective-permute-start(bf16[8,8,1024]{2,1,0:T(8,128)(2,1)S(1)} %all_to_all.33), channel_id=1, source_target_pairs={{0,227},{1,224},{2,225},{3,226},{4,231},{5,228},{6,229},{7,230},{8... | collective-permute-start | bytes 393224 | tf_op jit(solution)/shard_map/ppermute | solution.py:273
  133.0 5.9 %collective-permute-start.13 = (bf16[8,8,1024]{2,1,0:T(8,128)(2,1)S(1)}, bf16[8,8,1024]{2,1,0:T(8,128)(2,1)S(1)}, u32[]{:S(2)}, u32[]{:S(2)}) collective-permute-start(bf16[8,8,1024]{2,1,0:T(8,128)(2,1)S(1)} %all_to_all.33), channel_id=1, source_target_pairs={{0,226},{1,227},{2,224},{3,225},{4,230},{5,231},{6,228},{7,229},{8... | collective-permute-start | bytes 393224 | tf_op jit(solution)/shard_map/ppermute | solution.py:273
  134.8 5.6 %collective-permute-start.12 = (bf16[8,8,1024]{2,1,0:T(8,128)(2,1)S(1)}, bf16[8,8,1024]{2,1,0:T(8,128)(2,1)S(1)}, u32[]{:S(2)}, u32[]{:S(2)}) collective-permute-start(bf16[8,8,1024]{2,1,0:T(8,128)(2,1)S(1)} %all_to_all.33), channel_id=1, source_target_pairs={{0,225},{1,226},{2,227},{3,224},{4,229},{5,230},{6,231},{7,228},{8... | collective-permute-start | bytes 393224 | tf_op jit(solution)/shard_map/ppermute | solution.py:273

commit v10 on v9

--- a/solution.py
+++ b/solution.py
@@ -75,9 +75,11 @@
 
 
 def split_kernel(begun_ref, *out_refs):
-    width = out_refs[0].shape[-1]
-    for place, out_ref in enumerate(out_refs):
-        out_ref[...] = begun_ref[:, :, width * place : width * (place + 1)]
+    at = 0
+    for out_ref in out_refs:
+        width = out_ref.shape[-1]
+        out_ref[...] = begun_ref[:, :, at : at + width]
+        at += width
 
 
 def assemble_kernel(*refs):
@@ -308,12 +310,13 @@
         compiler_params=pltpu.CompilerParams(vmem_limit_bytes=60 * MIB),
     )(slot_index, saved_inputs[0], incoming)
     begun = exchange_along_z(blocks)
-    halves = (shape(along_z, rows, 2 * D), shape(along_z, rows, (slots - 1) * D))
-    urgent, later = call(split_kernel, halves, (begun,), 0, "split")
-    urgent, loss = lax.optimization_barrier((urgent, loss_grads))
-    blocks = [urgent] + [moved(urgent, 0, distance) for distance in range(1, ALONG_X)]
-    blocks[0], loss = lax.optimization_barrier((blocks[0], moved(loss, -1, 0)))
-    x, grads = assemble(blocks)
+    pieces = [shape(along_z, rows, width * D) for width in (1, 1, slots - 1)]
+    x, grads, later = call(split_kernel, pieces, (begun,), 0, "split")
+    x, grads, loss = lax.optimization_barrier((x, grads, loss_grads))
+    x = [moved(x, 0, distance) if distance else x for distance in range(ALONG_X)]
+    grads = [moved(grads, 0, distance) if distance else grads for distance in range(ALONG_X)]
+    grads[0], loss = lax.optimization_barrier((grads[0], moved(loss, -1, 0)))
+    [x], [grads] = assemble(x), assemble(grads)
 
     def forward(x):
         outs = (shape(tokens, units, dtype=F32), shape(tokens, units))

time: 174 us -> 174 us (level)
  blocking collectives: 97.3 us -> 94.8 us
    all_to_all x2, blocking collectives: 47 us -> 43 us  [exchange(): lax.all_to_all(blocks, 'tensor', split_axis=0, concat_axis=0, tiled=True)]
    ppermute x15 -> x18, starting transfers between devices: 20.3 us -> 21.8 us  [moved(): return lax.ppermute(value, ('section', 'tensor'), pairs)]
    ppermute x15 -> x18, waiting for transfers between devices: 12.9 us -> 13.9 us  [moved(): return lax.ppermute(value, ('section', 'tensor'), pairs)]
    pallas_call x17 -> x18, Pallas kernels: 12.7 us -> 12.7 us  [call(): pl.pallas_call(kernel, out_shape=outs, in_specs=[VMEM] * len(operands), o...]
  transfers between devices with their start and end apart: 16 -> 19, of which waited for: 6 -> 7; matrix products, arithmetic and copies ran while one was open for 0% -> 0% of each run, Pallas kernels for 4% -> 5%
where the time goes in v10:
time: 174 us; the launch traced here: 172 us
  blocking collectives  94.8 us (54%)
  waiting for transfers between devices  27.5 us (16%)
  starting transfers between devices  26.4 us (15%)
  Pallas kernels  20.1 us (12%)
  local copies, waits for them, and re-layouts  2.41 us (1%)
    all_to_all x3, blocking collectives, exchange_along_z(): lax.all_to_all(blocks, 'tensor', split_axis=0, concat_axis=0, axis_index_...  51.7 us
    all_to_all x2, blocking collectives, exchange(): lax.all_to_all(blocks, 'tensor', split_axis=0, concat_axis=0, tiled=True)  43 us
    ppermute x18, starting transfers between devices, moved(): return lax.ppermute(value, ('section', 'tensor'), pairs)  21.8 us
    ppermute x18, waiting for transfers between devices, moved(): return lax.ppermute(value, ('section', 'tensor'), pairs)  13.9 us
    all_to_all x1, waiting for transfers between devices, exchange(): lax.all_to_all(blocks, 'tensor', split_axis=0, concat_axis=0, tiled=True)  13.6 us
    pallas_call x18, Pallas kernels, call(): pl.pallas_call(kernel, out_shape=outs, in_specs=[VMEM] * len(operands), o...  12.7 us
    pallas_call x1, Pallas kernels, final_products(): pl.pallas_call(lambda *refs: final_kernel(slots, *refs), grid=(rows // bl...  5.52 us
    all_to_all x1, starting transfers between devices, exchange(): lax.all_to_all(blocks, 'tensor', split_axis=0, concat_axis=0, tiled=True)  4.61 us
  transfers between devices with their start and end apart: 19, of which 7 were waited for; matrix products, arithmetic and copies ran while one was open for 0% of the time, Pallas kernels for 5%

profile of v10, /device:TPU:8, one launch (start us, length us, event | category | flops | bytes accessed | tf_op | source)
XLA Modules:
  0.0 172.1 jit_solution(8992211713458983802)
XLA Ops:
  0.7 1.9 %start.1 = bf16[8,8,4096]{2,1,0:T(8,128)(2,1)} custom-call(s32[1,3]{1,0:T(1,128)} %index.1, bf16[4,8,1024]{2,1,0:T(8,128)(2,1)} %bitcast.61, bf16[8,1024]{1,0:T(8,128)(2,1)} %bitcast.56), custom_call_target="tpu_custom_call" | custom-call | tf_op jit(solution)/shard_map/start/pallas_call | solution.py:298
  2.6 26.0 %all_to_all.30.begun_ref = bf16[8,8,4096]{2,1,0:T(8,128)(2,1)S(1)} all-to-all(bf16[8,8,4096]{2,1,0:T(8,128)(2,1)} %start.1), channel_id=1, replica_groups={{0,4,8,12,16,20,24,28},{1,5,9,13,17,21,25,29},{2,6,10,14,18,22,26,30},{..., dimensions={0} | all-to-all | bytes 1048576 | tf_op jit(solution)/shard_map/all_to_all | solution.py:258
  28.6 2.8 %collective-permute-start.6 = (bf16[8,8,1024]{2,1,0:T(8,128)(2,1)S(1)}, bf16[8,8,1024]{2,1,0:T(8,128)(2,1)S(1)}, u32[]{:S(2)}, u32[]{:S(2)}) collective-permute-start(bf16[8,8,1024]{2,1,0:T(8,128)(2,1)S(1)} %get-tuple-element.57.refs_0_), channel_id=1, source_target_pairs={{0,3},{1,0},{2,1},{3,2},{4,7},{5,4},{6,5},{7,6},{8,11},{9,8},{10,9... | collective-permute-start | bytes 393224 | tf_op jit(solution)/shard_map/ppermute | solution.py:275
  31.4 0.8 collective-permute-start.5
  32.2 0.9 collective-permute-start.4
  33.1 2.4 %collective-permute-start.3 = (bf16[8,8,1024]{2,1,0:T(8,128)(2,1)S(1)}, bf16[8,8,1024]{2,1,0:T(8,128)(2,1)S(1)}, u32[]{:S(2)}, u32[]{:S(2)}) collective-permute-start(bf16[8,8,1024]{2,1,0:T(8,128)(2,1)S(1)} %get-tuple-element.56.refs_0_), channel_id=1, source_target_pairs={{0,3},{1,0},{2,1},{3,2},{4,7},{5,4},{6,5},{7,6},{8,11},{9,8},{10,9... | collective-permute-start | bytes 393224 | tf_op jit(solution)/shard_map/ppermute | solution.py:275
  35.5 1.0 collective-permute-done.refs_2_
  36.5 1.8 %collective-permute-start.2 = (bf16[8,8,1024]{2,1,0:T(8,128)(2,1)S(1)}, bf16[8,8,1024]{2,1,0:T(8,128)(2,1)S(1)}, u32[]{:S(2)}, u32[]{:S(2)}) collective-permute-start(bf16[8,8,1024]{2,1,0:T(8,128)(2,1)S(1)} %get-tuple-element.56.refs_0_), channel_id=1, source_target_pairs={{0,2},{1,3},{2,0},{3,1},{4,6},{5,7},{6,4},{7,5},{8,10},{9,11},{10,... | collective-permute-start | bytes 393224 | tf_op jit(solution)/shard_map/ppermute | solution.py:275
  38.3 1.4 collective-permute-start.1
  39.7 0.0 copy-start.1
  39.8 0.7 slope.1.slope_ref
  40.5 3.8 %collective-permute-done.2.refs_2_ = bf16[8,8,1024]{2,1,0:T(8,128)(2,1)S(1)} collective-permute-done((bf16[8,8,1024]{2,1,0:T(8,128)(2,1)S(1)}, bf16[8,8,1024]{2,1,0:T(8,128)(2,1)S(1)}, u32[]{:S(2)}, u32[]{:S(2)}) %collective-permute-start.2) | collective-permute-done | bytes 131104 | tf_op jit(solution)/shard_map/ppermute | solution.py:275
  44.3 2.3 %collective-permute-done.1.refs_1_ = bf16[8,8,1024]{2,1,0:T(8,128)(2,1)S(1)} collective-permute-done((bf16[8,8,1024]{2,1,0:T(8,128)(2,1)S(1)}, bf16[8,8,1024]{2,1,0:T(8,128)(2,1)S(1)}, u32[]{:S(2)}, u32[]{:S(2)}) %collective-permute-start.1) | collective-permute-done | bytes 131104 | tf_op jit(solution)/shard_map/ppermute | solution.py:275
  46.7 1.3 first_back.1
  48.0 0.0 copy-start.4
  48.0 0.8 copy-done.4
  48.8 4.6 %all-to-all-start.1 = ((bf16[32,8,1024]{2,1,0:T(8,128)(2,1)}), bf16[32,8,1024]{2,1,0:T(8,128)(2,1)}, u32[]{:S(2)}, u32[]{:S(2)}) async-start(bf16[32,8,1024]{2,1,0:T(8,128)(2,1)} %bitcast.50), calls=%async_computation.1 | async-start | bytes 1048576 | tf_op jit(solution)/shard_map/all_to_all | solution.py:252
  53.4 2.9 %collective-permute-start.10 = (bf16[8,8,2048]{2,1,0:T(8,128)(2,1)S(1)}, bf16[8,8,2048]{2,1,0:T(8,128)(2,1)}, u32[]{:S(2)}, u32[]{:S(2)}) collective-permute-start(bf16[8,8,2048]{2,1,0:T(8,128)(2,1)S(1)} %get-tuple-element.60.refs_0_), channel_id=1, source_target_pairs={{0,3},{1,0},{2,1},{3,2},{4,7},{5,4},{6,5},{7,6},{8,11},{9,8},{10,9... | collective-permute-start | bytes 786440 | tf_op jit(solution)/shard_map/ppermute | solution.py:275
  56.3 0.8 collective-permute-start.9
  57.1 0.9 collective-permute-start.8
  58.0 13.6 %all-to-all-done.1.refs_0_ = bf16[32,8,1024]{2,1,0:T(8,128)(2,1)} async-done(((bf16[32,8,1024]{2,1,0:T(8,128)(2,1)}), bf16[32,8,1024]{2,1,0:T(8,128)(2,1)}, u32[]{:S(2)}, u32[]{:S(2)}) %all-to-all-start.1) | async-done | bytes 524320 | tf_op jit(solution)/shard_map/all_to_all | solution.py:252
  71.6 1.1 add_up.2
  72.7 12.2 %all_to_all.31 = bf16[8,8,1024]{2,1,0:T(8,128)(2,1)S(1)} all-to-all(bf16[8,8,1024]{2,1,0:T(8,128)(2,1)S(1)} %get-tuple-element.59), channel_id=1, replica_groups={{0,4,8,12,16,20,24,28},{1,5,9,13,17,21,25,29},{2,6,10,14,18,22,26,30},{..., dimensions={0} | all-to-all | bytes 262144 | tf_op jit(solution)/shard_map/all_to_all | solution.py:258
  84.9 0.2 collective-permute-start.13
  85.1 0.8 collective-permute-start.12
  85.9 1.3 collective-permute-start.11
  87.2 1.2 assemble.7
  88.4 0.0 copy-start.2
  88.4 1.6 copy-done.2
  90.0 1.3 again.1
  91.3 0.7 forward.2
  92.1 0.9 squares.2.refs_7_
  93.0 2.1 %collective-permute-done.11.refs_1_ = bf16[8,8,1024]{2,1,0:T(8,128)(2,1)S(1)} collective-permute-done((bf16[8,8,1024]{2,1,0:T(8,128)(2,1)S(1)}, bf16[8,8,1024]{2,1,0:T(8,128)(2,1)S(1)}, u32[]{:S(2)}, u32[]{:S(2)}) %collective-permute-start.11) | collective-permute-done | bytes 131104 | tf_op jit(solution)/shard_map/ppermute | solution.py:275
  95.2 1.3 back.1
  96.5 20.6 %all_to_all.32.refs_0_ = bf16[32,8,1024]{2,1,0:T(8,128)(2,1)S(1)} all-to-all(bf16[32,8,1024]{2,1,0:T(8,128)(2,1)S(1)} %bitcast.55), channel_id=1, replica_groups=mesh['section'=8,'tensor'=32] {'tensor'}, dimensions={0} | all-to-all | bytes 1048576 | tf_op jit(solution)/shard_map/all_to_all | solution.py:252
  117.2 0.1 add_up.3
  117.2 13.6 %all_to_all.33 = bf16[8,8,1024]{2,1,0:T(8,128)(2,1)S(1)} all-to-all(bf16[8,8,1024]{2,1,0:T(8,128)(2,1)S(1)} %get-tuple-element.74), channel_id=1, replica_groups={{0,4,8,12,16,20,24,28},{1,5,9,13,17,21,25,29},{2,6,10,14,18,22,26,30},{..., dimensions={0} | all-to-all | bytes 262144 | tf_op jit(solution)/shard_map/all_to_all | solution.py:258
  130.8 1.5 collective-permute-start.17
  132.3 0.7 collective-permute-start.16
  133.1 2.5 %collective-permute-start.15 = (bf16[8,8,1024]{2,1,0:T(8,128)(2,1)S(1)}, bf16[8,8,1024]{2,1,0:T(8,128)(2,1)S(1)}, u32[]{:S(2)}, u32[]{:S(2)}) collective-permute-start(bf16[8,8,1024]{2,1,0:T(8,128)(2,1)S(1)} %all_to_all.33), channel_id=1, source_target_pairs={{0,225},{1,226},{2,227},{3,224},{4,229},{5,230},{6,231},{7,228},{8... | collective-permute-start | bytes 393224 | tf_op jit(solution)/shard_map/ppermute | solution.py:275
  135.6 0.7 forward.3
  136.3 0.5 grams.1
  136.8 0.9 squares.3.refs_8_
  137.7 1.9 %collective-permute-done.16.refs_2_ = bf16[8,8,1024]{2,1,0:T(8,128)(2,1)S(1)} collective-permute-done((bf16[8,8,1024]{2,1,0:T(8,128)(2,1)S(1)}, bf16[8,8,1024]{2,1,0:T(8,128)(2,1)S(1)}, u32[]{:S(2)}, u32[]{:S(2)}) %collective-permute-start.16) | collective-permute-done | bytes 131104 | tf_op jit(solution)/shard_map/ppermute | solution.py:275
  139.6 2.7 %collective-permute-done.15.refs_1_ = bf16[8,8,1024]{2,1,0:T(8,128)(2,1)S(1)} collective-permute-done((bf16[8,8,1024]{2,1,0:T(8,128)(2,1)S(1)}, bf16[8,8,1024]{2,1,0:T(8,128)(2,1)S(1)}, u32[]{:S(2)}, u32[]{:S(2)}) %collective-permute-start.15) | collective-permute-done | bytes 131104 | tf_op jit(solution)/shard_map/ppermute | solution.py:275
  142.3 1.8 %last_back.1 = (bf16[256,1024]{1,0:T(8,128)(2,1)S(1)}, bf16[256,1152]{1,0:T(8,128)(2,1)S(1)}) custom-call(s32[2,3]{1,0:T(2,128)S(1)} %bitcast.59, bf16[256,1024]{1,0:T(8,128)(2,1)S(1)} %bitcast.47, f32[256,1024]{1,0:T(8,128)S(1)} %get-tuple-element.88.refs_2_, bf16[1024,1024]{1,0:T(8,128)(2,1)S(1)} %bitcast.31, bf16[1024,1024]{1,0:T(8,128)(2,1)S(1)} %bitcast.27, ...), custom_call_target="tpu_custom_call" | custom-call | flops 1073741824 | bytes 1048576 | tf_op jit(solution)/shard_map/last_back/pallas_call | solution.py:27
  144.2 22.4 %all_to_all.34.refs_1_ = bf16[32,8,1152]{2,1,0:T(8,128)(2,1)S(1)} all-to-all(bf16[32,8,1152]{2,1,0:T(8,128)(2,1)S(1)} %bitcast.54), channel_id=1, replica_groups=mesh['section'=8,'tensor'=32] {'tensor'}, dimensions={0} | all-to-all | bytes 1179648 | tf_op jit(solution)/shard_map/all_to_all | solution.py:252
  166.6 5.5 %final.1 = (bf16[1024,1024]{1,0:T(8,128)(2,1)}, bf16[1024,1024]{1,0:T(8,128)(2,1)}, bf16[3,8,1024]{2,1,0:T(8,128)(2,1)}) custom-call(s32[2,3]{1,0:T(2,128)S(1)} %bitcast.60, bf16[32,8,1152]{2,1,0:T(8,128)(2,1)S(1)} %all_to_all.34.refs_1_, bf16[32,8,1024]{2,1,0:T(8,128)(2,1)S(1)} %bitcast.49, bf16[8,1024]{1,0:T(8,128)(2,1)S(1)} %get-tuple-element.94.refs_3_, ...), custom_call_target="tpu_custom_call" | custom-call | flops 3221225472 | bytes 4194304 | tf_op jit(solution)/shard_map/final/pallas_call | solution.py:236
  (31 shorter events, 0.3 us)
Async XLA Ops:
  0.6 32.5 %copy-start.7 = (bf16[2,8,1024]{2,1,0:T(8,128)(2,1)S(1)}, bf16[2,8,1024]{2,1,0:T(8,128)(2,1)}, u32[]{:S(2)}) copy-start(bf16[2,8,1024]{2,1,0:T(8,128)(2,1)} %param.11) | copy-start | bytes 98308
  0.6 39.1 %copy-start = (bf16[1,1024,1024]{2,1,0:T(8,128)(2,1)S(1)}, bf16[1,1024,1024]{2,1,0:T(8,128)(2,1)}, u32[]{:S(2)}) copy-start(bf16[1,1024,1024]{2,1,0:T(8,128)(2,1)} %param.12) | copy-start | bytes 6291460
  28.6 9.7 %collective-permute-start.6 = (bf16[8,8,1024]{2,1,0:T(8,128)(2,1)S(1)}, bf16[8,8,1024]{2,1,0:T(8,128)(2,1)S(1)}, u32[]{:S(2)}, u32[]{:S(2)}) collective-permute-start(bf16[8,8,1024]{2,1,0:T(8,128)(2,1)S(1)} %get-tuple-element.57.refs_0_), channel_id=1, source_target_pairs={{0,3},{1,0},{2,1},{3,2},{4,7},{5,4},{6,5},{7,6},{8,11},{9,8},{10,9... | collective-permute-start | bytes 393224 | tf_op jit(solution)/shard_map/ppermute | solution.py:275
  31.4 8.2 %collective-permute-start.5 = (bf16[8,8,1024]{2,1,0:T(8,128)(2,1)S(1)}, bf16[8,8,1024]{2,1,0:T(8,128)(2,1)S(1)}, u32[]{:S(2)}, u32[]{:S(2)}) collective-permute-start(bf16[8,8,1024]{2,1,0:T(8,128)(2,1)S(1)} %get-tuple-element.57.refs_0_), channel_id=1, source_target_pairs={{0,2},{1,3},{2,0},{3,1},{4,6},{5,7},{6,4},{7,5},{8,10},{9,11},{10,... | collective-permute-start | bytes 393224 | tf_op jit(solution)/shard_map/ppermute | solution.py:275
  32.2 7.4 %collective-permute-start.4 = (bf16[8,8,1024]{2,1,0:T(8,128)(2,1)S(1)}, bf16[8,8,1024]{2,1,0:T(8,128)(2,1)S(1)}, u32[]{:S(2)}, u32[]{:S(2)}) collective-permute-start(bf16[8,8,1024]{2,1,0:T(8,128)(2,1)S(1)} %get-tuple-element.57.refs_0_), channel_id=1, source_target_pairs={{0,1},{1,2},{2,3},{3,0},{4,5},{5,6},{6,7},{7,4},{8,9},{9,10},{10,1... | collective-permute-start | bytes 393224 | tf_op jit(solution)/shard_map/ppermute | solution.py:275
  33.1 3.3 %collective-permute-start = (bf16[2,8,1024]{2,1,0:T(8,128)(2,1)S(1)}, bf16[2,8,1024]{2,1,0:T(8,128)(2,1)S(1)}, u32[]{:S(2)}, u32[]{:S(2)}) collective-permute-start(bf16[2,8,1024]{2,1,0:T(8,128)(2,1)S(1)} %copy-done.7), channel_id=1, source_target_pairs={{0,32},{1,33},{2,34},{3,35},{4,36},{5,37},{6,38},{7,39},{8,40},{9,... | collective-permute-start | bytes 98312 | tf_op jit(solution)/shard_map/ppermute | solution.py:275
  33.1 7.4 %collective-permute-start.3 = (bf16[8,8,1024]{2,1,0:T(8,128)(2,1)S(1)}, bf16[8,8,1024]{2,1,0:T(8,128)(2,1)S(1)}, u32[]{:S(2)}, u32[]{:S(2)}) collective-permute-start(bf16[8,8,1024]{2,1,0:T(8,128)(2,1)S(1)} %get-tuple-element.56.refs_0_), channel_id=1, source_target_pairs={{0,3},{1,0},{2,1},{3,2},{4,7},{5,4},{6,5},{7,6},{8,11},{9,8},{10,9... | collective-permute-start | bytes 393224 | tf_op jit(solution)/shard_map/ppermute | solution.py:275
  36.5 7.8 %collective-permute-start.2 = (bf16[8,8,1024]{2,1,0:T(8,128)(2,1)S(1)}, bf16[8,8,1024]{2,1,0:T(8,128)(2,1)S(1)}, u32[]{:S(2)}, u32[]{:S(2)}) collective-permute-start(bf16[8,8,1024]{2,1,0:T(8,128)(2,1)S(1)} %get-tuple-element.56.refs_0_), channel_id=1, source_target_pairs={{0,2},{1,3},{2,0},{3,1},{4,6},{5,7},{6,4},{7,5},{8,10},{9,11},{10,... | collective-permute-start | bytes 393224 | tf_op jit(solution)/shard_map/ppermute | solution.py:275
  38.3 8.3 %collective-permute-start.1 = (bf16[8,8,1024]{2,1,0:T(8,128)(2,1)S(1)}, bf16[8,8,1024]{2,1,0:T(8,128)(2,1)S(1)}, u32[]{:S(2)}, u32[]{:S(2)}) collective-permute-start(bf16[8,8,1024]{2,1,0:T(8,128)(2,1)S(1)} %get-tuple-element.56.refs_0_), channel_id=1, source_target_pairs={{0,1},{1,2},{2,3},{3,0},{4,5},{5,6},{6,7},{7,4},{8,9},{9,10},{10,1... | collective-permute-start | bytes 393224 | tf_op jit(solution)/shard_map/ppermute | solution.py:275
  39.7 6.9 %copy-start.1 = (bf16[1,1024,1024]{2,1,0:T(8,128)(2,1)S(1)}, bf16[1,1024,1024]{2,1,0:T(8,128)(2,1)}, u32[]{:S(2)}) copy-start(bf16[1,1024,1024]{2,1,0:T(8,128)(2,1)} %param.13) | copy-start | bytes 6291460
  46.7 24.9 %copy-start.5 = (bf16[1,8,1024]{2,1,0:T(8,128)(2,1)S(1)}, bf16[1,8,1024]{2,1,0:T(8,128)(2,1)}, u32[]{:S(2)}) copy-start(bf16[1,8,1024]{2,1,0:T(8,128)(2,1)} %refs_1_.1) | copy-start | bytes 49156
  48.0 0.8 copy-start.4
  48.8 22.8 %all-to-all-start.1 = ((bf16[32,8,1024]{2,1,0:T(8,128)(2,1)}), bf16[32,8,1024]{2,1,0:T(8,128)(2,1)}, u32[]{:S(2)}, u32[]{:S(2)}) async-start(bf16[32,8,1024]{2,1,0:T(8,128)(2,1)} %bitcast.50), calls=%async_computation.1 | async-start | bytes 1048576 | tf_op jit(solution)/shard_map/all_to_all | solution.py:252
  53.4 31.7 %collective-permute-start.10 = (bf16[8,8,2048]{2,1,0:T(8,128)(2,1)S(1)}, bf16[8,8,2048]{2,1,0:T(8,128)(2,1)}, u32[]{:S(2)}, u32[]{:S(2)}) collective-permute-start(bf16[8,8,2048]{2,1,0:T(8,128)(2,1)S(1)} %get-tuple-element.60.refs_0_), channel_id=1, source_target_pairs={{0,3},{1,0},{2,1},{3,2},{4,7},{5,4},{6,5},{7,6},{8,11},{9,8},{10,9... | collective-permute-start | bytes 786440 | tf_op jit(solution)/shard_map/ppermute | solution.py:275
  56.3 29.6 %collective-permute-start.9 = (bf16[8,8,2048]{2,1,0:T(8,128)(2,1)S(1)}, bf16[8,8,2048]{2,1,0:T(8,128)(2,1)}, u32[]{:S(2)}, u32[]{:S(2)}) collective-permute-start(bf16[8,8,2048]{2,1,0:T(8,128)(2,1)S(1)} %get-tuple-element.60.refs_0_), channel_id=1, source_target_pairs={{0,2},{1,3},{2,0},{3,1},{4,6},{5,7},{6,4},{7,5},{8,10},{9,11},{10,... | collective-permute-start | bytes 786440 | tf_op jit(solution)/shard_map/ppermute | solution.py:275
  57.1 30.1 %collective-permute-start.8 = (bf16[8,8,2048]{2,1,0:T(8,128)(2,1)S(1)}, bf16[8,8,2048]{2,1,0:T(8,128)(2,1)}, u32[]{:S(2)}, u32[]{:S(2)}) collective-permute-start(bf16[8,8,2048]{2,1,0:T(8,128)(2,1)S(1)} %get-tuple-element.60.refs_0_), channel_id=1, source_target_pairs={{0,1},{1,2},{2,3},{3,0},{4,5},{5,6},{6,7},{7,4},{8,9},{9,10},{10,1... | collective-permute-start | bytes 786440 | tf_op jit(solution)/shard_map/ppermute | solution.py:275
  84.9 8.0 %collective-permute-start.7 = (bf16[8,8,1024]{2,1,0:T(8,128)(2,1)S(1)}, bf16[8,8,1024]{2,1,0:T(8,128)(2,1)S(1)}, u32[]{:S(2)}, u32[]{:S(2)}) collective-permute-start(bf16[8,8,1024]{2,1,0:T(8,128)(2,1)S(1)} %all_to_all.31), channel_id=1, source_target_pairs={{0,224},{1,225},{2,226},{3,227},{4,228},{5,229},{6,230},{7,231},{8... | collective-permute-start | bytes 393224 | tf_op jit(solution)/shard_map/ppermute | solution.py:275
  84.9 8.0 %collective-permute-start.13 = (bf16[8,8,1024]{2,1,0:T(8,128)(2,1)S(1)}, bf16[8,8,1024]{2,1,0:T(8,128)(2,1)S(1)}, u32[]{:S(2)}, u32[]{:S(2)}) collective-permute-start(bf16[8,8,1024]{2,1,0:T(8,128)(2,1)S(1)} %all_to_all.31), channel_id=1, source_target_pairs={{0,227},{1,224},{2,225},{3,226},{4,231},{5,228},{6,229},{7,230},{8... | collective-permute-start | bytes 393224 | tf_op jit(solution)/shard_map/ppermute | solution.py:275
  85.1 7.9 %collective-permute-start.12 = (bf16[8,8,1024]{2,1,0:T(8,128)(2,1)S(1)}, bf16[8,8,1024]{2,1,0:T(8,128)(2,1)S(1)}, u32[]{:S(2)}, u32[]{:S(2)}) collective-permute-start(bf16[8,8,1024]{2,1,0:T(8,128)(2,1)S(1)} %all_to_all.31), channel_id=1, source_target_pairs={{0,226},{1,227},{2,224},{3,225},{4,230},{5,231},{6,228},{7,229},{8... | collective-permute-start | bytes 393224 | tf_op jit(solution)/shard_map/ppermute | solution.py:275
  85.9 9.2 %collective-permute-start.11 = (bf16[8,8,1024]{2,1,0:T(8,128)(2,1)S(1)}, bf16[8,8,1024]{2,1,0:T(8,128)(2,1)S(1)}, u32[]{:S(2)}, u32[]{:S(2)}) collective-permute-start(bf16[8,8,1024]{2,1,0:T(8,128)(2,1)S(1)} %all_to_all.31), channel_id=1, source_target_pairs={{0,225},{1,226},{2,227},{3,224},{4,229},{5,230},{6,231},{7,228},{8... | collective-permute-start | bytes 393224 | tf_op jit(solution)/shard_map/ppermute | solution.py:275
  88.4 1.6 copy-start.2
  91.3 0.8 copy-start.6
  92.0 3.1 %copy-start.3 = (bf16[1,1024,1024]{2,1,0:T(8,128)(2,1)S(1)}, bf16[1,1024,1024]{2,1,0:T(8,128)(2,1)}, u32[]{:S(2)}) copy-start(bf16[1,1024,1024]{2,1,0:T(8,128)(2,1)} %param.13) | copy-start | bytes 6291460
  130.8 6.8 %collective-permute-start.14 = (bf16[8,8,1024]{2,1,0:T(8,128)(2,1)S(1)}, bf16[8,8,1024]{2,1,0:T(8,128)(2,1)S(1)}, u32[]{:S(2)}, u32[]{:S(2)}) collective-permute-start(bf16[8,8,1024]{2,1,0:T(8,128)(2,1)S(1)} %all_to_all.33), channel_id=1, source_target_pairs={{0,224},{1,225},{2,226},{3,227},{4,228},{5,229},{6,230},{7,231},{8... | collective-permute-start | bytes 393224 | tf_op jit(solution)/shard_map/ppermute | solution.py:275
  130.8 6.8 %collective-permute-start.17 = (bf16[8,8,1024]{2,1,0:T(8,128)(2,1)S(1)}, bf16[8,8,1024]{2,1,0:T(8,128)(2,1)S(1)}, u32[]{:S(2)}, u32[]{:S(2)}) collective-permute-start(bf16[8,8,1024]{2,1,0:T(8,128)(2,1)S(1)} %all_to_all.33), channel_id=1, source_target_pairs={{0,227},{1,224},{2,225},{3,226},{4,231},{5,228},{6,229},{7,230},{8... | collective-permute-start | bytes 393224 | tf_op jit(solution)/shard_map/ppermute | solution.py:275
  132.3 7.2 %collective-permute-start.16 = (bf16[8,8,1024]{2,1,0:T(8,128)(2,1)S(1)}, bf16[8,8,1024]{2,1,0:T(8,128)(2,1)S(1)}, u32[]{:S(2)}, u32[]{:S(2)}) collective-permute-start(bf16[8,8,1024]{2,1,0:T(8,128)(2,1)S(1)} %all_to_all.33), channel_id=1, source_target_pairs={{0,226},{1,227},{2,224},{3,225},{4,230},{5,231},{6,228},{7,229},{8... | collective-permute-start | bytes 393224 | tf_op jit(solution)/shard_map/ppermute | solution.py:275
  133.1 9.2 %collective-permute-start.15 = (bf16[8,8,1024]{2,1,0:T(8,128)(2,1)S(1)}, bf16[8,8,1024]{2,1,0:T(8,128)(2,1)S(1)}, u32[]{:S(2)}, u32[]{:S(2)}) collective-permute-start(bf16[8,8,1024]{2,1,0:T(8,128)(2,1)S(1)} %all_to_all.33), channel_id=1, source_target_pairs={{0,225},{1,226},{2,227},{3,224},{4,229},{5,230},{6,231},{7,228},{8... | collective-permute-start | bytes 393224 | tf_op jit(solution)/shard_map/ppermute | solution.py:275

commit v11 on v10

--- a/solution.py
+++ b/solution.py
@@ -312,10 +312,9 @@
     begun = exchange_along_z(blocks)
     pieces = [shape(along_z, rows, width * D) for width in (1, 1, slots - 1)]
     x, grads, later = call(split_kernel, pieces, (begun,), 0, "split")
-    x, grads, loss = lax.optimization_barrier((x, grads, loss_grads))
     x = [moved(x, 0, distance) if distance else x for distance in range(ALONG_X)]
     grads = [moved(grads, 0, distance) if distance else grads for distance in range(ALONG_X)]
-    grads[0], loss = lax.optimization_barrier((grads[0], moved(loss, -1, 0)))
+    loss = moved(loss_grads, -1, 0)
     [x], [grads] = assemble(x), assemble(grads)
 
     def forward(x):

time: 174 us -> 171 us (0.983)
  waiting for transfers between devices: 27.5 us -> 20.2 us
  starting transfers between devices: 26.4 us -> 28.7 us
  blocking collectives: 94.8 us -> 96.7 us
    ppermute x18, waiting for transfers between devices: 13.9 us -> 8.93 us  [moved(): return lax.ppermute(value, ('section', 'tensor'), pairs)]
    all_to_all x2, blocking collectives: 43 us -> 47 us  [exchange(): lax.all_to_all(blocks, 'tensor', split_axis=0, concat_axis=0, tiled=True)]
    ppermute x18, starting transfers between devices: 21.8 us -> 24.1 us  [moved(): return lax.ppermute(value, ('section', 'tensor'), pairs)]
    all_to_all x1, waiting for transfers between devices: 13.6 us -> 11.3 us  [exchange(): lax.all_to_all(blocks, 'tensor', split_axis=0, concat_axis=0, tiled=True)]
    all_to_all x3, blocking collectives: 51.7 us -> 49.7 us  [exchange_along_z(): lax.all_to_all(blocks, 'tensor', split_axis=0, concat_axis=0, axis_index_...]
where the time goes in v11:
time: 171 us; the launch traced here: 170 us
  blocking collectives  96.7 us (57%)
  starting transfers between devices  28.7 us (17%)
  waiting for transfers between devices  20.2 us (12%)
  Pallas kernels  20.1 us (12%)
  local copies, waits for them, and re-layouts  3 us (2%)
    all_to_all x3, blocking collectives, exchange_along_z(): lax.all_to_all(blocks, 'tensor', split_axis=0, concat_axis=0, axis_index_...  49.7 us
    all_to_all x2, blocking collectives, exchange(): lax.all_to_all(blocks, 'tensor', split_axis=0, concat_axis=0, tiled=True)  47 us
    ppermute x18, starting transfers between devices, moved(): return lax.ppermute(value, ('section', 'tensor'), pairs)  24.1 us
    pallas_call x18, Pallas kernels, call(): pl.pallas_call(kernel, out_shape=outs, in_specs=[VMEM] * len(operands), o...  12.7 us
    all_to_all x1, waiting for transfers between devices, exchange(): lax.all_to_all(blocks, 'tensor', split_axis=0, concat_axis=0, tiled=True)  11.3 us
    ppermute x18, waiting for transfers between devices, moved(): return lax.ppermute(value, ('section', 'tensor'), pairs)  8.93 us
    pallas_call x1, Pallas kernels, final_products(): pl.pallas_call(lambda *refs: final_kernel(slots, *refs), grid=(rows // bl...  5.52 us
    all_to_all x1, starting transfers between devices, exchange(): lax.all_to_all(blocks, 'tensor', split_axis=0, concat_axis=0, tiled=True)  4.62 us
  transfers between devices with their start and end apart: 19, of which 7 were waited for; matrix products, arithmetic and copies ran while one was open for 0% of the time, Pallas kernels for 5%

profile of v11, /device:TPU:8, one launch (start us, length us, event | category | flops | bytes accessed | tf_op | source)
XLA Modules:
  0.0 169.7 jit_solution(14607805598240698621)
XLA Ops:
  0.6 1.9 %start.1 = bf16[8,8,4096]{2,1,0:T(8,128)(2,1)} custom-call(s32[1,3]{1,0:T(1,128)} %index.1, bf16[4,8,1024]{2,1,0:T(8,128)(2,1)} %bitcast.61, bf16[8,1024]{1,0:T(8,128)(2,1)} %bitcast.56), custom_call_target="tpu_custom_call" | custom-call | tf_op jit(solution)/shard_map/start/pallas_call | solution.py:298
  2.6 26.0 %all_to_all.30.begun_ref = bf16[8,8,4096]{2,1,0:T(8,128)(2,1)S(1)} all-to-all(bf16[8,8,4096]{2,1,0:T(8,128)(2,1)} %start.1), channel_id=1, replica_groups={{0,4,8,12,16,20,24,28},{1,5,9,13,17,21,25,29},{2,6,10,14,18,22,26,30},{..., dimensions={0} | all-to-all | bytes 1048576 | tf_op jit(solution)/shard_map/all_to_all | solution.py:258
  28.6 2.8 %collective-permute-start.5 = (bf16[8,8,1024]{2,1,0:T(8,128)(2,1)S(1)}, bf16[8,8,1024]{2,1,0:T(8,128)(2,1)S(1)}, u32[]{:S(2)}, u32[]{:S(2)}) collective-permute-start(bf16[8,8,1024]{2,1,0:T(8,128)(2,1)S(1)} %get-tuple-element.48.refs_0_), channel_id=1, source_target_pairs={{0,3},{1,0},{2,1},{3,2},{4,7},{5,4},{6,5},{7,6},{8,11},{9,8},{10,9... | collective-permute-start | bytes 393224 | tf_op jit(solution)/shard_map/ppermute | solution.py:275
  31.4 0.8 collective-permute-start.4
  32.2 0.9 collective-permute-start.3
  33.1 2.4 %collective-permute-start.2 = (bf16[8,8,1024]{2,1,0:T(8,128)(2,1)S(1)}, bf16[8,8,1024]{2,1,0:T(8,128)(2,1)S(1)}, u32[]{:S(2)}, u32[]{:S(2)}) collective-permute-start(bf16[8,8,1024]{2,1,0:T(8,128)(2,1)S(1)} %get-tuple-element.47.refs_0_), channel_id=1, source_target_pairs={{0,3},{1,0},{2,1},{3,2},{4,7},{5,4},{6,5},{7,6},{8,11},{9,8},{10,9... | collective-permute-start | bytes 393224 | tf_op jit(solution)/shard_map/ppermute | solution.py:275
  35.5 1.5 collective-permute-start.1
  37.0 0.2 collective-permute-start
  37.2 2.2 %collective-permute-done.4.refs_2_ = bf16[8,8,1024]{2,1,0:T(8,128)(2,1)S(1)} collective-permute-done((bf16[8,8,1024]{2,1,0:T(8,128)(2,1)S(1)}, bf16[8,8,1024]{2,1,0:T(8,128)(2,1)S(1)}, u32[]{:S(2)}, u32[]{:S(2)}) %collective-permute-start.4) | collective-permute-done | bytes 131104 | tf_op jit(solution)/shard_map/ppermute | solution.py:275
  39.4 2.7 %collective-permute-done.3.refs_1_ = bf16[8,8,1024]{2,1,0:T(8,128)(2,1)S(1)} collective-permute-done((bf16[8,8,1024]{2,1,0:T(8,128)(2,1)S(1)}, bf16[8,8,1024]{2,1,0:T(8,128)(2,1)S(1)}, u32[]{:S(2)}, u32[]{:S(2)}) %collective-permute-start.3) | collective-permute-done | bytes 131104 | tf_op jit(solution)/shard_map/ppermute | solution.py:275
  42.1 0.7 slope.1.slope_ref
  42.9 0.8 collective-permute-done.1.refs_2_
  43.6 1.3 collective-permute-done.refs_1_
  45.0 1.3 first_back.1
  46.3 0.8 copy-done.4
  47.1 4.6 %all-to-all-start.1 = ((bf16[32,8,1024]{2,1,0:T(8,128)(2,1)}), bf16[32,8,1024]{2,1,0:T(8,128)(2,1)}, u32[]{:S(2)}, u32[]{:S(2)}) async-start(bf16[32,8,1024]{2,1,0:T(8,128)(2,1)} %bitcast.50), calls=%async_computation.1 | async-start | bytes 1048576 | tf_op jit(solution)/shard_map/all_to_all | solution.py:252
  51.8 0.0 collective-permute-start.6
  51.8 2.9 %collective-permute-start.10 = (bf16[8,8,2048]{2,1,0:T(8,128)(2,1)S(1)}, bf16[8,8,2048]{2,1,0:T(8,128)(2,1)}, u32[]{:S(2)}, u32[]{:S(2)}) collective-permute-start(bf16[8,8,2048]{2,1,0:T(8,128)(2,1)S(1)} %get-tuple-element.50.refs_0_), channel_id=1, source_target_pairs={{0,3},{1,0},{2,1},{3,2},{4,7},{5,4},{6,5},{7,6},{8,11},{9,8},{10,9... | collective-permute-start | bytes 786440 | tf_op jit(solution)/shard_map/ppermute | solution.py:275
  54.7 0.8 collective-permute-start.9
  55.5 0.9 collective-permute-start.8
  56.4 11.3 %all-to-all-done.1.refs_0_ = bf16[32,8,1024]{2,1,0:T(8,128)(2,1)} async-done(((bf16[32,8,1024]{2,1,0:T(8,128)(2,1)}), bf16[32,8,1024]{2,1,0:T(8,128)(2,1)}, u32[]{:S(2)}, u32[]{:S(2)}) %all-to-all-start.1) | async-done | bytes 524320 | tf_op jit(solution)/shard_map/all_to_all | solution.py:252
  67.7 1.1 add_up.2
  68.9 11.9 %all_to_all.31 = bf16[8,8,1024]{2,1,0:T(8,128)(2,1)S(1)} all-to-all(bf16[8,8,1024]{2,1,0:T(8,128)(2,1)S(1)} %get-tuple-element.49), channel_id=1, replica_groups={{0,4,8,12,16,20,24,28},{1,5,9,13,17,21,25,29},{2,6,10,14,18,22,26,30},{..., dimensions={0} | all-to-all | bytes 262144 | tf_op jit(solution)/shard_map/all_to_all | solution.py:258
  80.8 1.1 collective-permute-start.13
  81.9 0.7 collective-permute-start.12
  82.6 3.2 %collective-permute-start.11 = (bf16[8,8,1024]{2,1,0:T(8,128)(2,1)S(1)}, bf16[8,8,1024]{2,1,0:T(8,128)(2,1)S(1)}, u32[]{:S(2)}, u32[]{:S(2)}) collective-permute-start(bf16[8,8,1024]{2,1,0:T(8,128)(2,1)S(1)} %all_to_all.31), channel_id=1, source_target_pairs={{0,225},{1,226},{2,227},{3,224},{4,229},{5,230},{6,231},{7,228},{8... | collective-permute-start | bytes 393224 | tf_op jit(solution)/shard_map/ppermute | solution.py:275
  85.8 1.2 assemble.7
  87.0 1.6 copy-done.2
  88.6 1.3 again.1
  89.9 0.7 forward.2
  90.6 0.9 squares.2.refs_7_
  91.5 0.1 assemble.8
  91.6 0.6 copy-done.3
  92.2 1.3 back.1
  93.5 22.3 %all_to_all.32.refs_0_ = bf16[32,8,1024]{2,1,0:T(8,128)(2,1)S(1)} all-to-all(bf16[32,8,1024]{2,1,0:T(8,128)(2,1)S(1)} %bitcast.55), channel_id=1, replica_groups=mesh['section'=8,'tensor'=32] {'tensor'}, dimensions={0} | all-to-all | bytes 1048576 | tf_op jit(solution)/shard_map/all_to_all | solution.py:252
  115.8 0.1 add_up.3
  115.8 11.7 %all_to_all.33 = bf16[8,8,1024]{2,1,0:T(8,128)(2,1)S(1)} all-to-all(bf16[8,8,1024]{2,1,0:T(8,128)(2,1)S(1)} %get-tuple-element.64), channel_id=1, replica_groups={{0,4,8,12,16,20,24,28},{1,5,9,13,17,21,25,29},{2,6,10,14,18,22,26,30},{..., dimensions={0} | all-to-all | bytes 262144 | tf_op jit(solution)/shard_map/all_to_all | solution.py:258
  127.6 2.4 %collective-permute-start.17 = (bf16[8,8,1024]{2,1,0:T(8,128)(2,1)S(1)}, bf16[8,8,1024]{2,1,0:T(8,128)(2,1)S(1)}, u32[]{:S(2)}, u32[]{:S(2)}) collective-permute-start(bf16[8,8,1024]{2,1,0:T(8,128)(2,1)S(1)} %all_to_all.33), channel_id=1, source_target_pairs={{0,227},{1,224},{2,225},{3,226},{4,231},{5,228},{6,229},{7,230},{8... | collective-permute-start | bytes 393224 | tf_op jit(solution)/shard_map/ppermute | solution.py:275
  130.0 1.5 collective-permute-start.16
  131.5 2.0 %collective-permute-start.15 = (bf16[8,8,1024]{2,1,0:T(8,128)(2,1)S(1)}, bf16[8,8,1024]{2,1,0:T(8,128)(2,1)S(1)}, u32[]{:S(2)}, u32[]{:S(2)}) collective-permute-start(bf16[8,8,1024]{2,1,0:T(8,128)(2,1)S(1)} %all_to_all.33), channel_id=1, source_target_pairs={{0,225},{1,226},{2,227},{3,224},{4,229},{5,230},{6,231},{7,228},{8... | collective-permute-start | bytes 393224 | tf_op jit(solution)/shard_map/ppermute | solution.py:275
  133.5 0.7 forward.3
  134.3 0.5 grams.1
  134.7 0.9 squares.3.refs_8_
  135.6 0.2 collective-permute-done.16.refs_2_
  135.9 1.7 collective-permute-done.15.refs_1_
  137.6 1.8 %last_back.1 = (bf16[256,1024]{1,0:T(8,128)(2,1)S(1)}, bf16[256,1152]{1,0:T(8,128)(2,1)S(1)}) custom-call(s32[2,3]{1,0:T(2,128)S(1)} %bitcast.59, bf16[256,1024]{1,0:T(8,128)(2,1)S(1)} %bitcast.47, f32[256,1024]{1,0:T(8,128)S(1)} %get-tuple-element.78.refs_2_, bf16[1024,1024]{1,0:T(8,128)(2,1)S(1)} %bitcast.31, bf16[1024,1024]{1,0:T(8,128)(2,1)S(1)} %bitcast.27, ...), custom_call_target="tpu_custom_call" | custom-call | flops 1073741824 | bytes 1048576 | tf_op jit(solution)/shard_map/last_back/pallas_call | solution.py:27
  139.4 24.7 %all_to_all.34.refs_1_ = bf16[32,8,1152]{2,1,0:T(8,128)(2,1)S(1)} all-to-all(bf16[32,8,1152]{2,1,0:T(8,128)(2,1)S(1)} %bitcast.54), channel_id=1, replica_groups=mesh['section'=8,'tensor'=32] {'tensor'}, dimensions={0} | all-to-all | bytes 1179648 | tf_op jit(solution)/shard_map/all_to_all | solution.py:252
  164.2 5.5 %final.1 = (bf16[1024,1024]{1,0:T(8,128)(2,1)}, bf16[1024,1024]{1,0:T(8,128)(2,1)}, bf16[3,8,1024]{2,1,0:T(8,128)(2,1)}) custom-call(s32[2,3]{1,0:T(2,128)S(1)} %bitcast.60, bf16[32,8,1152]{2,1,0:T(8,128)(2,1)S(1)} %all_to_all.34.refs_1_, bf16[32,8,1024]{2,1,0:T(8,128)(2,1)S(1)} %bitcast.49, bf16[8,1024]{1,0:T(8,128)(2,1)S(1)} %get-tuple-element.84.refs_3_, ...), custom_call_target="tpu_custom_call" | custom-call | flops 3221225472 | bytes 4194304 | tf_op jit(solution)/shard_map/final/pallas_call | solution.py:236
  (31 shorter events, 0.3 us)
Async XLA Ops:
  0.6 41.5 %copy-start = (bf16[1,1024,1024]{2,1,0:T(8,128)(2,1)S(1)}, bf16[1,1024,1024]{2,1,0:T(8,128)(2,1)}, u32[]{:S(2)}) copy-start(bf16[1,1024,1024]{2,1,0:T(8,128)(2,1)} %param.12) | copy-start | bytes 6291460
  28.6 8.4 %collective-permute-start.5 = (bf16[8,8,1024]{2,1,0:T(8,128)(2,1)S(1)}, bf16[8,8,1024]{2,1,0:T(8,128)(2,1)S(1)}, u32[]{:S(2)}, u32[]{:S(2)}) collective-permute-start(bf16[8,8,1024]{2,1,0:T(8,128)(2,1)S(1)} %get-tuple-element.48.refs_0_), channel_id=1, source_target_pairs={{0,3},{1,0},{2,1},{3,2},{4,7},{5,4},{6,5},{7,6},{8,11},{9,8},{10,9... | collective-permute-start | bytes 393224 | tf_op jit(solution)/shard_map/ppermute | solution.py:275
  31.4 8.0 %collective-permute-start.4 = (bf16[8,8,1024]{2,1,0:T(8,128)(2,1)S(1)}, bf16[8,8,1024]{2,1,0:T(8,128)(2,1)S(1)}, u32[]{:S(2)}, u32[]{:S(2)}) collective-permute-start(bf16[8,8,1024]{2,1,0:T(8,128)(2,1)S(1)} %get-tuple-element.48.refs_0_), channel_id=1, source_target_pairs={{0,2},{1,3},{2,0},{3,1},{4,6},{5,7},{6,4},{7,5},{8,10},{9,11},{10,... | collective-permute-start | bytes 393224 | tf_op jit(solution)/shard_map/ppermute | solution.py:275
  32.2 9.8 %collective-permute-start.3 = (bf16[8,8,1024]{2,1,0:T(8,128)(2,1)S(1)}, bf16[8,8,1024]{2,1,0:T(8,128)(2,1)S(1)}, u32[]{:S(2)}, u32[]{:S(2)}) collective-permute-start(bf16[8,8,1024]{2,1,0:T(8,128)(2,1)S(1)} %get-tuple-element.48.refs_0_), channel_id=1, source_target_pairs={{0,1},{1,2},{2,3},{3,0},{4,5},{5,6},{6,7},{7,4},{8,9},{9,10},{10,1... | collective-permute-start | bytes 393224 | tf_op jit(solution)/shard_map/ppermute | solution.py:275
  33.1 9.8 %collective-permute-start.2 = (bf16[8,8,1024]{2,1,0:T(8,128)(2,1)S(1)}, bf16[8,8,1024]{2,1,0:T(8,128)(2,1)S(1)}, u32[]{:S(2)}, u32[]{:S(2)}) collective-permute-start(bf16[8,8,1024]{2,1,0:T(8,128)(2,1)S(1)} %get-tuple-element.47.refs_0_), channel_id=1, source_target_pairs={{0,3},{1,0},{2,1},{3,2},{4,7},{5,4},{6,5},{7,6},{8,11},{9,8},{10,9... | collective-permute-start | bytes 393224 | tf_op jit(solution)/shard_map/ppermute | solution.py:275
  35.5 8.2 %collective-permute-start.1 = (bf16[8,8,1024]{2,1,0:T(8,128)(2,1)S(1)}, bf16[8,8,1024]{2,1,0:T(8,128)(2,1)S(1)}, u32[]{:S(2)}, u32[]{:S(2)}) collective-permute-start(bf16[8,8,1024]{2,1,0:T(8,128)(2,1)S(1)} %get-tuple-element.47.refs_0_), channel_id=1, source_target_pairs={{0,2},{1,3},{2,0},{3,1},{4,6},{5,7},{6,4},{7,5},{8,10},{9,11},{10,... | collective-permute-start | bytes 393224 | tf_op jit(solution)/shard_map/ppermute | solution.py:275
  37.0 8.0 %collective-permute-start = (bf16[8,8,1024]{2,1,0:T(8,128)(2,1)S(1)}, bf16[8,8,1024]{2,1,0:T(8,128)(2,1)S(1)}, u32[]{:S(2)}, u32[]{:S(2)}) collective-permute-start(bf16[8,8,1024]{2,1,0:T(8,128)(2,1)S(1)} %get-tuple-element.47.refs_0_), channel_id=1, source_target_pairs={{0,1},{1,2},{2,3},{3,0},{4,5},{5,6},{6,7},{7,4},{8,9},{9,10},{10,1... | collective-permute-start | bytes 393224 | tf_op jit(solution)/shard_map/ppermute | solution.py:275
  42.1 2.9 %copy-start.1 = (bf16[1,1024,1024]{2,1,0:T(8,128)(2,1)S(1)}, bf16[1,1024,1024]{2,1,0:T(8,128)(2,1)}, u32[]{:S(2)}) copy-start(bf16[1,1024,1024]{2,1,0:T(8,128)(2,1)} %param.13) | copy-start | bytes 6291460
  45.0 6.7 %copy-start.7 = (bf16[2,8,1024]{2,1,0:T(8,128)(2,1)S(1)}, bf16[2,8,1024]{2,1,0:T(8,128)(2,1)}, u32[]{:S(2)}) copy-start(bf16[2,8,1024]{2,1,0:T(8,128)(2,1)} %param.11) | copy-start | bytes 98308
  45.0 22.7 %copy-start.5 = (bf16[1,8,1024]{2,1,0:T(8,128)(2,1)S(1)}, bf16[1,8,1024]{2,1,0:T(8,128)(2,1)}, u32[]{:S(2)}) copy-start(bf16[1,8,1024]{2,1,0:T(8,128)(2,1)} %refs_1_.1) | copy-start | bytes 49156
  46.3 0.8 copy-start.4
  47.1 20.6 %all-to-all-start.1 = ((bf16[32,8,1024]{2,1,0:T(8,128)(2,1)}), bf16[32,8,1024]{2,1,0:T(8,128)(2,1)}, u32[]{:S(2)}, u32[]{:S(2)}) async-start(bf16[32,8,1024]{2,1,0:T(8,128)(2,1)} %bitcast.50), calls=%async_computation.1 | async-start | bytes 1048576 | tf_op jit(solution)/shard_map/all_to_all | solution.py:252
  51.8 4.6 %collective-permute-start.6 = (bf16[2,8,1024]{2,1,0:T(8,128)(2,1)S(1)}, bf16[2,8,1024]{2,1,0:T(8,128)(2,1)S(1)}, u32[]{:S(2)}, u32[]{:S(2)}) collective-permute-start(bf16[2,8,1024]{2,1,0:T(8,128)(2,1)S(1)} %copy-done.7), channel_id=1, source_target_pairs={{0,32},{1,33},{2,34},{3,35},{4,36},{5,37},{6,38},{7,39},{8,40},{9,... | collective-permute-start | bytes 98312 | tf_op jit(solution)/shard_map/ppermute | solution.py:275
  51.8 30.1 %collective-permute-start.10 = (bf16[8,8,2048]{2,1,0:T(8,128)(2,1)S(1)}, bf16[8,8,2048]{2,1,0:T(8,128)(2,1)}, u32[]{:S(2)}, u32[]{:S(2)}) collective-permute-start(bf16[8,8,2048]{2,1,0:T(8,128)(2,1)S(1)} %get-tuple-element.50.refs_0_), channel_id=1, source_target_pairs={{0,3},{1,0},{2,1},{3,2},{4,7},{5,4},{6,5},{7,6},{8,11},{9,8},{10,9... | collective-permute-start | bytes 786440 | tf_op jit(solution)/shard_map/ppermute | solution.py:275
  54.7 27.9 %collective-permute-start.9 = (bf16[8,8,2048]{2,1,0:T(8,128)(2,1)S(1)}, bf16[8,8,2048]{2,1,0:T(8,128)(2,1)}, u32[]{:S(2)}, u32[]{:S(2)}) collective-permute-start(bf16[8,8,2048]{2,1,0:T(8,128)(2,1)S(1)} %get-tuple-element.50.refs_0_), channel_id=1, source_target_pairs={{0,2},{1,3},{2,0},{3,1},{4,6},{5,7},{6,4},{7,5},{8,10},{9,11},{10,... | collective-permute-start | bytes 786440 | tf_op jit(solution)/shard_map/ppermute | solution.py:275
  55.5 30.2 %collective-permute-start.8 = (bf16[8,8,2048]{2,1,0:T(8,128)(2,1)S(1)}, bf16[8,8,2048]{2,1,0:T(8,128)(2,1)}, u32[]{:S(2)}, u32[]{:S(2)}) collective-permute-start(bf16[8,8,2048]{2,1,0:T(8,128)(2,1)S(1)} %get-tuple-element.50.refs_0_), channel_id=1, source_target_pairs={{0,1},{1,2},{2,3},{3,0},{4,5},{5,6},{6,7},{7,4},{8,9},{9,10},{10,1... | collective-permute-start | bytes 786440 | tf_op jit(solution)/shard_map/ppermute | solution.py:275
  80.8 10.7 %collective-permute-start.7 = (bf16[8,8,1024]{2,1,0:T(8,128)(2,1)S(1)}, bf16[8,8,1024]{2,1,0:T(8,128)(2,1)S(1)}, u32[]{:S(2)}, u32[]{:S(2)}) collective-permute-start(bf16[8,8,1024]{2,1,0:T(8,128)(2,1)S(1)} %all_to_all.31), channel_id=1, source_target_pairs={{0,224},{1,225},{2,226},{3,227},{4,228},{5,229},{6,230},{7,231},{8... | collective-permute-start | bytes 393224 | tf_op jit(solution)/shard_map/ppermute | solution.py:275
  80.8 10.7 %collective-permute-start.13 = (bf16[8,8,1024]{2,1,0:T(8,128)(2,1)S(1)}, bf16[8,8,1024]{2,1,0:T(8,128)(2,1)S(1)}, u32[]{:S(2)}, u32[]{:S(2)}) collective-permute-start(bf16[8,8,1024]{2,1,0:T(8,128)(2,1)S(1)} %all_to_all.31), channel_id=1, source_target_pairs={{0,227},{1,224},{2,225},{3,226},{4,231},{5,228},{6,229},{7,230},{8... | collective-permute-start | bytes 393224 | tf_op jit(solution)/shard_map/ppermute | solution.py:275
  81.9 9.6 %collective-permute-start.12 = (bf16[8,8,1024]{2,1,0:T(8,128)(2,1)S(1)}, bf16[8,8,1024]{2,1,0:T(8,128)(2,1)S(1)}, u32[]{:S(2)}, u32[]{:S(2)}) collective-permute-start(bf16[8,8,1024]{2,1,0:T(8,128)(2,1)S(1)} %all_to_all.31), channel_id=1, source_target_pairs={{0,226},{1,227},{2,224},{3,225},{4,230},{5,231},{6,228},{7,229},{8... | collective-permute-start | bytes 393224 | tf_op jit(solution)/shard_map/ppermute | solution.py:275
  82.6 8.9 %collective-permute-start.11 = (bf16[8,8,1024]{2,1,0:T(8,128)(2,1)S(1)}, bf16[8,8,1024]{2,1,0:T(8,128)(2,1)S(1)}, u32[]{:S(2)}, u32[]{:S(2)}) collective-permute-start(bf16[8,8,1024]{2,1,0:T(8,128)(2,1)S(1)} %all_to_all.31), channel_id=1, source_target_pairs={{0,225},{1,226},{2,227},{3,224},{4,229},{5,230},{6,231},{7,228},{8... | collective-permute-start | bytes 393224 | tf_op jit(solution)/shard_map/ppermute | solution.py:275
  87.0 1.6 copy-start.2
  89.8 0.8 copy-start.6
  90.6 1.6 copy-start.3
  127.6 8.0 %collective-permute-start.14 = (bf16[8,8,1024]{2,1,0:T(8,128)(2,1)S(1)}, bf16[8,8,1024]{2,1,0:T(8,128)(2,1)S(1)}, u32[]{:S(2)}, u32[]{:S(2)}) collective-permute-start(bf16[8,8,1024]{2,1,0:T(8,128)(2,1)S(1)} %all_to_all.33), channel_id=1, source_target_pairs={{0,224},{1,225},{2,226},{3,227},{4,228},{5,229},{6,230},{7,231},{8... | collective-permute-start | bytes 393224 | tf_op jit(solution)/shard_map/ppermute | solution.py:275
  127.6 8.0 %collective-permute-start.17 = (bf16[8,8,1024]{2,1,0:T(8,128)(2,1)S(1)}, bf16[8,8,1024]{2,1,0:T(8,128)(2,1)S(1)}, u32[]{:S(2)}, u32[]{:S(2)}) collective-permute-start(bf16[8,8,1024]{2,1,0:T(8,128)(2,1)S(1)} %all_to_all.33), channel_id=1, source_target_pairs={{0,227},{1,224},{2,225},{3,226},{4,231},{5,228},{6,229},{7,230},{8... | collective-permute-start | bytes 393224 | tf_op jit(solution)/shard_map/ppermute | solution.py:275
  130.0 5.9 %collective-permute-start.16 = (bf16[8,8,1024]{2,1,0:T(8,128)(2,1)S(1)}, bf16[8,8,1024]{2,1,0:T(8,128)(2,1)S(1)}, u32[]{:S(2)}, u32[]{:S(2)}) collective-permute-start(bf16[8,8,1024]{2,1,0:T(8,128)(2,1)S(1)} %all_to_all.33), channel_id=1, source_target_pairs={{0,226},{1,227},{2,224},{3,225},{4,230},{5,231},{6,228},{7,229},{8... | collective-permute-start | bytes 393224 | tf_op jit(solution)/shard_map/ppermute | solution.py:275
  131.5 6.0 %collective-permute-start.15 = (bf16[8,8,1024]{2,1,0:T(8,128)(2,1)S(1)}, bf16[8,8,1024]{2,1,0:T(8,128)(2,1)S(1)}, u32[]{:S(2)}, u32[]{:S(2)}) collective-permute-start(bf16[8,8,1024]{2,1,0:T(8,128)(2,1)S(1)} %all_to_all.33), channel_id=1, source_target_pairs={{0,225},{1,226},{2,227},{3,224},{4,229},{5,230},{6,231},{7,228},{8... | collective-permute-start | bytes 393224 | tf_op jit(solution)/shard_map/ppermute | solution.py:275
